TPU v7x, 32 devices: a whole 2x2x4 slice. The times are simulated.
32 devices in a mesh: fsdp: 8 (over z, core), sp: 4 (over y, x).
Axes of the slice: x: 2, y: 2, z: 4, core: 2. Of those that a mesh axis runs over, the one named last changes fastest.
Arguments:
- tokens: bfloat16 [8, 1024, 2048], P('fsdp', 'sp'), may hold values from -6 to 6
- attn_gain: bfloat16 [2048], P('fsdp'), may hold values from 0.5 to 1.5
- attn_shift: bfloat16 [2048], P('fsdp'), may hold values from -1.25 to 1.25
- query_weight: bfloat16 [2048, 2048], P('fsdp'), may hold values from -0.125 to 0.125
- key_weight: bfloat16 [2048, 2048], P('fsdp'), may hold values from -0.125 to 0.125
- value_weight: bfloat16 [2048, 4096], P('fsdp'), may hold values from -0.125 to 0.125
- swish_weight: bfloat16 [2048, 4096], P('fsdp'), may hold values from -0.125 to 0.125
- group_gain: bfloat16 [4096], P('fsdp'), may hold values from 0.5 to 1.5
- group_shift: bfloat16 [4096], P('fsdp'), may hold values from -1.75 to 1.75
- out_weight: bfloat16 [4096, 2048], P('fsdp'), may hold values from -0.125 to 0.125
- ffn_gain: bfloat16 [2048], P('fsdp'), may hold values from 0.5 to 1.5
- ffn_shift: bfloat16 [2048], P('fsdp'), may hold values from -1.25 to 1.25
- gating_weight: bfloat16 [2048, 4096], P('fsdp'), may hold values from -0.125 to 0.125
- upward_weight: bfloat16 [2048, 4096], P('fsdp'), may hold values from -0.125 to 0.125
- gating_bias: bfloat16 [4096], P('fsdp'), may hold values from -1.75 to 1.75
- upward_bias: bfloat16 [4096], P('fsdp'), may hold values from -1.75 to 1.75
- downward_weight: bfloat16 [4096, 2048], P('fsdp'), may hold values from -0.125 to 0.125
- downward_bias: bfloat16 [2048], P('fsdp'), may hold values from -1.25 to 1.25
- cotangent: bfloat16 [8, 1024, 2048], P('fsdp', 'sp'), may hold values from -6 to 6
Outputs:
- layer_out: bfloat16 [8, 1024, 2048], P('fsdp', 'sp')
- input_grad: float32 [8, 1024, 2048], P('fsdp', 'sp')
- attn_gain_grad: float32 [2048], P('fsdp')
- attn_shift_grad: float32 [2048], P('fsdp')
- query_grad: float32 [2048, 2048], P('fsdp')
- key_grad: float32 [2048, 2048], P('fsdp')
- value_grad: float32 [2048, 4096], P('fsdp')
- swish_grad: float32 [2048, 4096], P('fsdp')
- group_gain_grad: float32 [4096], P('fsdp')
- group_shift_grad: float32 [4096], P('fsdp')
- out_weight_grad: float32 [4096, 2048], P('fsdp')
- ffn_gain_grad: float32 [2048], P('fsdp')
- ffn_shift_grad: float32 [2048], P('fsdp')
- gating_grad: float32 [2048, 4096], P('fsdp')
- upward_grad: float32 [2048, 4096], P('fsdp')
- gating_bias_grad: float32 [4096], P('fsdp')
- upward_bias_grad: float32 [4096], P('fsdp')
- downward_grad: float32 [4096, 2048], P('fsdp')
- downward_bias_grad: float32 [2048], P('fsdp')
All inputs are finite; a program needn't handle non-finite values.
Results may differ from a plain program's by a relative error of at most 0.02.
Values may be sent and summed in bfloat16 or wider, within the bound.
No kernel may reach another device: no remote copies, remote signals or barrier semaphores. Data moves between devices by JAX's collectives and lax.ppermute only.
A program may use at most 512 MiB of HBM per device.

v0:
```python
import jax
import jax.numpy as jnp
from jax import lax
from jax.sharding import PartitionSpec as P

HEADS = 8
V_HEAD = 512


EPSILON = 1e-05


def product(left, right):
    return jnp.dot(left, right, preferred_element_type=jnp.float32)


def over_rows(left, right):
    return lax.dot_general(
        left, right, (((0,), (0,)), ((), ())), preferred_element_type=jnp.float32
    )


def over_columns(left, right):
    return lax.dot_general(
        left, right, (((1,), (1,)), ((), ())), preferred_element_type=jnp.float32
    )


def normalize(values):
    middle = jnp.mean(values, -1, keepdims=True)
    centred = values - middle
    spread = jnp.mean(centred * centred, -1, keepdims=True)
    factor = lax.rsqrt(spread + EPSILON)
    return (centred * factor, factor)


def group_normalize(values):
    middle = jnp.mean(values, -1, keepdims=True)
    centred = values - middle
    spread = jnp.mean(centred * centred, -1, keepdims=True)
    factor = lax.rsqrt(jnp.maximum(spread, 1.0))
    active = jnp.where(spread > 1.0, 1.0, 0.0)
    return (centred * factor, factor, active)


def normalize_back(scaled, normed, factor, active=1.0):
    first_mean = jnp.mean(scaled, -1, keepdims=True)
    second_mean = jnp.mean(scaled * normed, -1, keepdims=True)
    return factor * (scaled - first_mean - active * normed * second_mean)


def silu_slope(values):
    sigma = jax.nn.sigmoid(values)
    return sigma * (1.0 + values * (1.0 - sigma))


def decay_mask(head_ids, length):
    rates = jnp.log(1.0 - jnp.exp2(-5.0 - head_ids.astype(jnp.float32)))
    places = jnp.arange(length)
    distance = places[:, None] - places[None, :]
    steps = jnp.maximum(distance, 0).astype(jnp.float32)
    return jnp.where(distance[None] >= 0, jnp.exp(steps[None] * rates[:, None, None]), 0.0)


def split_heads(array, heads_here):
    return array.reshape(array.shape[0], array.shape[1], heads_here, -1)


def join_heads(array):
    return array.reshape(array.shape[0], array.shape[1], -1)


def score_block(query_split, key_split):
    factor = query_split.shape[-1] ** (-0.5)
    raw = jnp.einsum("nihd,njhd->nhij", query_split, key_split, preferred_element_type=jnp.float32)
    return raw * factor


def retain(query_heads, key_heads, value_heads, mask, heads_here):
    query_split = split_heads(query_heads, heads_here)
    key_split = split_heads(key_heads, heads_here)
    value_split = split_heads(value_heads, heads_here)
    weights = (score_block(query_split, key_split) * mask).astype(jnp.bfloat16)
    output = jnp.einsum("nhij,njhe->nihe", weights, value_split, preferred_element_type=jnp.float32)
    return join_heads(output.astype(jnp.bfloat16))


def retain_back(query_heads, key_heads, value_heads, grad_heads, mask, heads_here):
    query_split = split_heads(query_heads, heads_here)
    key_split = split_heads(key_heads, heads_here)
    value_split = split_heads(value_heads, heads_here)
    grad_split = split_heads(grad_heads, heads_here)
    factor = query_split.shape[-1] ** (-0.5)
    weights = (score_block(query_split, key_split) * mask).astype(jnp.bfloat16)
    value_back = jnp.einsum(
        "nhij,nihe->njhe", weights, grad_split, preferred_element_type=jnp.float32
    )
    weight_back = jnp.einsum(
        "nihe,njhe->nhij", grad_split, value_split, preferred_element_type=jnp.float32
    )
    score_back = (weight_back * mask).astype(jnp.bfloat16)
    query_back = (
        jnp.einsum("nhij,njhd->nihd", score_back, key_split, preferred_element_type=jnp.float32)
        * factor
    )
    key_back = (
        jnp.einsum("nhij,nihd->njhd", score_back, query_split, preferred_element_type=jnp.float32)
        * factor
    )
    return (
        join_heads(query_back.astype(jnp.bfloat16)),
        join_heads(key_back.astype(jnp.bfloat16)),
        join_heads(value_back.astype(jnp.bfloat16)),
    )


def upper_reduce(terms):
    shares = (
        lax.psum_scatter(
            terms[0].astype(jnp.bfloat16), "fsdp", scatter_dimension=0, tiled=True
        ).astype(jnp.float32),
        lax.psum_scatter(
            terms[1].astype(jnp.bfloat16), "fsdp", scatter_dimension=0, tiled=True
        ).astype(jnp.float32),
        lax.psum_scatter(
            terms[2].astype(jnp.bfloat16), "fsdp", scatter_dimension=0, tiled=True
        ).astype(jnp.float32),
        lax.psum_scatter(
            terms[3].astype(jnp.bfloat16), "fsdp", scatter_dimension=0, tiled=True
        ).astype(jnp.float32),
        lax.psum_scatter(
            terms[4].astype(jnp.bfloat16), "fsdp", scatter_dimension=0, tiled=True
        ).astype(jnp.float32),
        lax.psum_scatter(
            terms[5].astype(jnp.bfloat16), "fsdp", scatter_dimension=0, tiled=True
        ).astype(jnp.float32),
        lax.psum_scatter(
            terms[6].astype(jnp.bfloat16), "fsdp", scatter_dimension=0, tiled=True
        ).astype(jnp.float32),
        lax.psum_scatter(
            terms[7].astype(jnp.bfloat16), "fsdp", scatter_dimension=0, tiled=True
        ).astype(jnp.float32),
        lax.psum_scatter(
            terms[8].astype(jnp.bfloat16), "fsdp", scatter_dimension=0, tiled=True
        ).astype(jnp.float32),
        lax.psum_scatter(
            terms[9].astype(jnp.bfloat16), "fsdp", scatter_dimension=0, tiled=True
        ).astype(jnp.float32),
        lax.psum_scatter(
            terms[10].astype(jnp.bfloat16), "fsdp", scatter_dimension=0, tiled=True
        ).astype(jnp.float32),
    )
    return (
        lax.psum(shares[0].astype(jnp.bfloat16), "sp").astype(jnp.float32),
        lax.psum(shares[1].astype(jnp.bfloat16), "sp").astype(jnp.float32),
        lax.psum(shares[2].astype(jnp.bfloat16), "sp").astype(jnp.float32),
        lax.psum(shares[3].astype(jnp.bfloat16), "sp").astype(jnp.float32),
        lax.psum(shares[4].astype(jnp.bfloat16), "sp").astype(jnp.float32),
        lax.psum(shares[5].astype(jnp.bfloat16), "sp").astype(jnp.float32),
        lax.psum(shares[6].astype(jnp.bfloat16), "sp").astype(jnp.float32),
        lax.psum(shares[7].astype(jnp.bfloat16), "sp").astype(jnp.float32),
        lax.psum(shares[8].astype(jnp.bfloat16), "sp").astype(jnp.float32),
        lax.psum(shares[9].astype(jnp.bfloat16), "sp").astype(jnp.float32),
        lax.psum(shares[10].astype(jnp.bfloat16), "sp").astype(jnp.float32),
    )


def lower_reduce(terms):
    shares = (
        lax.psum_scatter(
            terms[0].astype(jnp.bfloat16), "fsdp", scatter_dimension=0, tiled=True
        ).astype(jnp.float32),
        lax.psum_scatter(
            terms[1].astype(jnp.bfloat16), "fsdp", scatter_dimension=0, tiled=True
        ).astype(jnp.float32),
        lax.psum_scatter(
            terms[2].astype(jnp.bfloat16), "fsdp", scatter_dimension=0, tiled=True
        ).astype(jnp.float32),
        lax.psum_scatter(
            terms[3].astype(jnp.bfloat16), "fsdp", scatter_dimension=0, tiled=True
        ).astype(jnp.float32),
        lax.psum_scatter(
            terms[4].astype(jnp.bfloat16), "fsdp", scatter_dimension=0, tiled=True
        ).astype(jnp.float32),
        lax.psum_scatter(
            terms[5].astype(jnp.bfloat16), "fsdp", scatter_dimension=0, tiled=True
        ).astype(jnp.float32),
    )
    return (
        lax.psum(shares[0].astype(jnp.bfloat16), "sp").astype(jnp.float32),
        lax.psum(shares[1].astype(jnp.bfloat16), "sp").astype(jnp.float32),
        lax.psum(shares[2].astype(jnp.bfloat16), "sp").astype(jnp.float32),
        lax.psum(shares[3].astype(jnp.bfloat16), "sp").astype(jnp.float32),
        lax.psum(shares[4].astype(jnp.bfloat16), "sp").astype(jnp.float32),
        lax.psum(shares[5].astype(jnp.bfloat16), "sp").astype(jnp.float32),
    )


def local(
    tokens,
    attn_gain,
    attn_shift,
    query_weight,
    key_weight,
    value_weight,
    swish_weight,
    group_gain,
    group_shift,
    out_weight,
    ffn_gain,
    ffn_shift,
    gating_weight,
    upward_weight,
    gating_bias,
    upward_bias,
    downward_weight,
    downward_bias,
    cotangent,
):
    seq_count, local_len, width = tokens.shape
    parts = lax.axis_size("sp")
    heads_here = HEADS // parts
    full_len = local_len * parts
    (
        gain_one,
        shift_one,
        query_full,
        key_full,
        value_full,
        swish_full,
        ggain_full,
        gshift_full,
        out_full,
    ) = (
        lax.all_gather(attn_gain, "fsdp", axis=0, tiled=True),
        lax.all_gather(attn_shift, "fsdp", axis=0, tiled=True),
        lax.all_gather(query_weight, "fsdp", axis=0, tiled=True),
        lax.all_gather(key_weight, "fsdp", axis=0, tiled=True),
        lax.all_gather(value_weight, "fsdp", axis=0, tiled=True),
        lax.all_gather(swish_weight, "fsdp", axis=0, tiled=True),
        lax.all_gather(group_gain, "fsdp", axis=0, tiled=True),
        lax.all_gather(group_shift, "fsdp", axis=0, tiled=True),
        lax.all_gather(out_weight, "fsdp", axis=0, tiled=True),
    )
    (
        gain_two,
        shift_two,
        gating_full,
        upward_full,
        gbias_full,
        ubias_full,
        downward_full,
        dbias_full,
    ) = (
        lax.all_gather(ffn_gain, "fsdp", axis=0, tiled=True),
        lax.all_gather(ffn_shift, "fsdp", axis=0, tiled=True),
        lax.all_gather(gating_weight, "fsdp", axis=0, tiled=True),
        lax.all_gather(upward_weight, "fsdp", axis=0, tiled=True),
        lax.all_gather(gating_bias, "fsdp", axis=0, tiled=True),
        lax.all_gather(upward_bias, "fsdp", axis=0, tiled=True),
        lax.all_gather(downward_weight, "fsdp", axis=0, tiled=True),
        lax.all_gather(downward_bias, "fsdp", axis=0, tiled=True),
    )
    gain_one = gain_one.astype(jnp.float32)
    gain_two = gain_two.astype(jnp.float32)
    ggain_full = ggain_full.astype(jnp.float32)

    def by_seq(array):
        return array.reshape(seq_count, local_len, -1)

    flat = tokens.reshape(-1, width).astype(jnp.float32)
    first_norm, first_factor = normalize(flat)
    first = (first_norm * gain_one + shift_one.astype(jnp.float32)).astype(jnp.bfloat16)
    query_proj = product(first, query_full).astype(jnp.bfloat16)
    key_proj = product(first, key_full).astype(jnp.bfloat16)
    value_proj = product(first, value_full).astype(jnp.bfloat16)
    swish_pre = product(first, swish_full)
    query_heads, key_heads, value_heads = (
        lax.all_to_all(by_seq(query_proj), "sp", split_axis=2, concat_axis=1, tiled=True),
        lax.all_to_all(by_seq(key_proj), "sp", split_axis=2, concat_axis=1, tiled=True),
        lax.all_to_all(by_seq(value_proj), "sp", split_axis=2, concat_axis=1, tiled=True),
    )
    head_ids = lax.axis_index("sp") * heads_here + jnp.arange(heads_here)
    mask = decay_mask(head_ids, full_len)
    retained_heads = retain(query_heads, key_heads, value_heads, mask, heads_here)
    retained = lax.all_to_all(retained_heads, "sp", split_axis=1, concat_axis=2, tiled=True)
    value_width = retained.shape[-1]
    heads_flat = retained.reshape(-1, HEADS, V_HEAD).astype(jnp.float32)
    group_norm3, group_factor, group_active = group_normalize(heads_flat)
    group_norm = group_norm3.reshape(-1, value_width)
    grouped = group_norm * ggain_full + gshift_full.astype(jnp.float32)
    swish_gate = jax.nn.silu(swish_pre)
    mixed = (grouped * swish_gate).astype(jnp.bfloat16)
    resid = flat + product(mixed, out_full)
    second_norm, second_factor = normalize(resid)
    second = (second_norm * gain_two + shift_two.astype(jnp.float32)).astype(jnp.bfloat16)
    gating = product(second, gating_full) + gbias_full.astype(jnp.float32)
    upward = product(second, upward_full) + ubias_full.astype(jnp.float32)
    gate_act = jax.nn.silu(gating)
    hidden = (gate_act * upward).astype(jnp.bfloat16)
    result = resid + product(hidden, downward_full) + dbias_full.astype(jnp.float32)
    grad_low = cotangent.reshape(-1, width)
    grad_out = grad_low.astype(jnp.float32)
    dbias_term = jnp.sum(grad_out, 0)
    dhidden = over_columns(grad_low, downward_full)
    dgating = (dhidden * upward * silu_slope(gating)).astype(jnp.bfloat16)
    dupward = (dhidden * gate_act).astype(jnp.bfloat16)
    gbias_term = jnp.sum(dgating.astype(jnp.float32), 0)
    ubias_term = jnp.sum(dupward.astype(jnp.float32), 0)
    dsecond = over_columns(dgating, gating_full) + over_columns(dupward, upward_full)
    fgain_term = jnp.sum(dsecond * second_norm, 0)
    fshift_term = jnp.sum(dsecond, 0)
    dresid = grad_out + normalize_back(dsecond * gain_two, second_norm, second_factor)
    dres_low = dresid.astype(jnp.bfloat16)
    dmixed = over_columns(dres_low, out_full)
    dgrouped = dmixed * swish_gate
    dswish = (dmixed * grouped * silu_slope(swish_pre)).astype(jnp.bfloat16)
    ggain_term = jnp.sum(dgrouped * group_norm, 0)
    gshift_term = jnp.sum(dgrouped, 0)
    dnormed = (dgrouped * ggain_full).reshape(-1, HEADS, V_HEAD)
    dretained = normalize_back(dnormed, group_norm3, group_factor, group_active).astype(
        jnp.bfloat16
    )
    upper = upper_reduce(
        (
            over_rows(second, dgating),
            over_rows(second, dupward),
            over_rows(hidden, grad_low),
            over_rows(mixed, dres_low),
            gbias_term,
            ubias_term,
            dbias_term,
            fgain_term,
            fshift_term,
            ggain_term,
            gshift_term,
        )
    )
    grad_heads = lax.all_to_all(
        by_seq(dretained.reshape(-1, value_width)), "sp", split_axis=2, concat_axis=1, tiled=True
    )
    query_back, key_back, value_back = retain_back(
        query_heads, key_heads, value_heads, grad_heads, mask, heads_here
    )
    dquery, dkey, dvalue = (
        lax.all_to_all(query_back, "sp", split_axis=1, concat_axis=2, tiled=True),
        lax.all_to_all(key_back, "sp", split_axis=1, concat_axis=2, tiled=True),
        lax.all_to_all(value_back, "sp", split_axis=1, concat_axis=2, tiled=True),
    )
    dquery = dquery.reshape(-1, dquery.shape[-1])
    dkey = dkey.reshape(-1, dkey.shape[-1])
    dvalue = dvalue.reshape(-1, dvalue.shape[-1])
    dfirst = (
        over_columns(dquery, query_full)
        + over_columns(dkey, key_full)
        + over_columns(dvalue, value_full)
        + over_columns(dswish, swish_full)
    )
    again_term = jnp.sum(dfirst * first_norm, 0)
    ashift_term = jnp.sum(dfirst, 0)
    input_grad = dresid + normalize_back(dfirst * gain_one, first_norm, first_factor)
    lower = lower_reduce(
        (
            over_rows(first, dquery),
            over_rows(first, dkey),
            over_rows(first, dvalue),
            over_rows(first, dswish),
            again_term,
            ashift_term,
        )
    )
    gating_grad, upward_grad, downward_grad, out_grad = (upper[0], upper[1], upper[2], upper[3])
    gbias_grad, ubias_grad, dbias_grad = (upper[4], upper[5], upper[6])
    fgain_grad, fshift_grad, ggain_grad, gshift_grad = (upper[7], upper[8], upper[9], upper[10])
    query_grad, key_grad, value_grad, swish_grad = (lower[0], lower[1], lower[2], lower[3])
    again_grad, ashift_grad = (lower[4], lower[5])
    layer_out = result.astype(jnp.bfloat16).reshape(seq_count, local_len, width)
    return (
        layer_out,
        input_grad.reshape(seq_count, local_len, width),
        again_grad,
        ashift_grad,
        query_grad,
        key_grad,
        value_grad,
        swish_grad,
        ggain_grad,
        gshift_grad,
        out_grad,
        fgain_grad,
        fshift_grad,
        gating_grad,
        upward_grad,
        gbias_grad,
        ubias_grad,
        downward_grad,
        dbias_grad,
    )


def solution(mesh):
    return jax.shard_map(
        local,
        mesh=mesh,
        in_specs=(
            P("fsdp", "sp", None),
            P("fsdp"),
            P("fsdp"),
            P("fsdp", None),
            P("fsdp", None),
            P("fsdp", None),
            P("fsdp", None),
            P("fsdp"),
            P("fsdp"),
            P("fsdp", None),
            P("fsdp"),
            P("fsdp"),
            P("fsdp", None),
            P("fsdp", None),
            P("fsdp"),
            P("fsdp"),
            P("fsdp", None),
            P("fsdp"),
            P("fsdp", "sp", None),
        ),
        out_specs=(
            P("fsdp", "sp", None),
            P("fsdp", "sp", None),
            P("fsdp"),
            P("fsdp"),
            P("fsdp", None),
            P("fsdp", None),
            P("fsdp", None),
            P("fsdp", None),
            P("fsdp"),
            P("fsdp"),
            P("fsdp", None),
            P("fsdp"),
            P("fsdp"),
            P("fsdp", None),
            P("fsdp", None),
            P("fsdp"),
            P("fsdp"),
            P("fsdp", None),
            P("fsdp"),
        ),
        check_vma=False,
    )
```

profile of v0, /device:TPU:0, one launch (start us, length us, event | category | flops | bytes accessed | tf_op | source)
XLA Modules:
  0.0 2823.5 jit_solution(12277141040220913436)
XLA Ops:
  12.7 13.5 all-gather
  35.9 58.6 %all-gather.20.cloned.1.call-done = bf16[2048,2048]{1,0:T(8,128)(2,1)} async-done(((bf16[256,2048]{1,0:T(8,128)(2,1)}), bf16[2048,2048]{1,0:T(8,128)(2,1)}) %all-gather.20.cloned.1.call-update) | async-done | bytes 8388624 | tf_op jit(solution)/shard_map/all_gather | solution.py:237
  125.8 50.9 %all-gather.22.cloned.1.call-done = bf16[2048,2048]{1,0:T(8,128)(2,1)} async-done(((bf16[256,2048]{1,0:T(8,128)(2,1)}), bf16[2048,2048]{1,0:T(8,128)(2,1)}) %all-gather.22.cloned.1.call-update) | async-done | bytes 8388624 | tf_op jit(solution)/shard_map/all_gather | solution.py:238
  207.6 120.4 %all-gather.18.cloned.1.call-done = bf16[2048,4096]{1,0:T(8,128)(2,1)} async-done(((bf16[256,4096]{1,0:T(8,128)(2,1)}), bf16[2048,4096]{1,0:T(8,128)(2,1)}) %all-gather.18.cloned.1.call-update) | async-done | bytes 16777232 | tf_op jit(solution)/shard_map/all_gather | solution.py:239
  343.7 21.6 reduce.5
  449.1 19.3 all-gather.2
  502.6 13.6 all-gather.6
  516.8 20.9 all-gather.7
  583.2 18.2 multiply_convert_fusion.7
  601.3 28.9 %all-gather.26.cloned.1.call-done = bf16[4096,2048]{1,0:T(8,128)(2,1)} async-done(((bf16[512,2048]{1,0:T(8,128)(2,1)}), bf16[4096,2048]{1,0:T(8,128)(2,1)}) %all-gather.26.cloned.1.call-update) | async-done | bytes 16777232 | tf_op jit(solution)/shard_map/all_gather | solution.py:243
  642.2 138.7 %all-gather.28.cloned.1.call-done = bf16[2048,4096]{1,0:T(8,128)(2,1)} async-done(((bf16[256,4096]{1,0:T(8,128)(2,1)}), bf16[2048,4096]{1,0:T(8,128)(2,1)}) %all-gather.28.cloned.1.call-update) | async-done | bytes 16777232 | tf_op jit(solution)/shard_map/all_gather | solution.py:257
  793.9 138.0 %all-gather.30.cloned.1.call-done = bf16[2048,4096]{1,0:T(8,128)(2,1)} async-done(((bf16[256,4096]{1,0:T(8,128)(2,1)}), bf16[2048,4096]{1,0:T(8,128)(2,1)}) %all-gather.30.cloned.1.call-update) | async-done | bytes 16777232 | tf_op jit(solution)/shard_map/all_gather | solution.py:258
  931.9 15.2 multiply_convert_fusion.6
  947.2 135.7 %all-gather.32.cloned.1.call-done = bf16[4096,2048]{1,0:T(8,128)(2,1)} async-done(((bf16[512,2048]{1,0:T(8,128)(2,1)}), bf16[4096,2048]{1,0:T(8,128)(2,1)}) %all-gather.32.cloned.1.call-update) | async-done | bytes 16777232 | tf_op jit(solution)/shard_map/all_gather | solution.py:261
  1082.9 13.8 fusion.50
  1108.9 14.0 multiply_reduce_fusion.3
  1127.1 14.0 fusion.48
  1190.6 22.9 reduce.9
  1217.5 30.5 %all_to_all.114 = bf16[4,2,131072]{2,1,0:T(2,128)(2,1)} all-to-all(bf16[4,2,131072]{2,1,0:T(2,128)(2,1)} %reshape.455), channel_id=1, replica_groups=mesh['fsdp'=8,'sp'=4] {'sp'}, dimensions={0} | all-to-all | bytes 4194304 | tf_op jit(solution)/shard_map/all_to_all | solution.py:339
  1291.3 17.9 all_to_all.115
  1349.2 16.5 all_to_all.116
  1457.2 14.1 reduce.12
  1475.8 26.4 all_to_all.117
  1526.4 144.6 %reduce-scatter.17.cloned.1.call-done = bf16[512,2048]{1,0:T(8,128)(2,1)} async-done(((bf16[4096,2048]{1,0:T(8,128)(2,1)}), bf16[512,2048]{1,0:T(8,128)(2,1)}) %reduce-scatter.17.cloned.1.call-update) | async-done | bytes 2097168 | tf_op jit(solution)/shard_map/reduce_scatter | solution.py:128
  1670.9 168.8 %reduce-scatter.19.cloned.1.call-done = bf16[256,4096]{1,0:T(8,128)(2,1)} async-done(((bf16[2048,4096]{1,0:T(8,128)(2,1)}), bf16[256,4096]{1,0:T(8,128)(2,1)}) %reduce-scatter.19.cloned.1.call-update) | async-done | bytes 2097168 | tf_op jit(solution)/shard_map/reduce_scatter | solution.py:119
  1839.8 169.0 %reduce-scatter.21.cloned.1.call-done = bf16[256,4096]{1,0:T(8,128)(2,1)} async-done(((bf16[2048,4096]{1,0:T(8,128)(2,1)}), bf16[256,4096]{1,0:T(8,128)(2,1)}) %reduce-scatter.21.cloned.1.call-update) | async-done | bytes 2097168 | tf_op jit(solution)/shard_map/reduce_scatter | solution.py:122
  2008.8 168.8 %reduce-scatter.15.cloned.1.call-done = bf16[256,4096]{1,0:T(8,128)(2,1)} async-done(((bf16[2048,4096]{1,0:T(8,128)(2,1)}), bf16[256,4096]{1,0:T(8,128)(2,1)}) %reduce-scatter.15.cloned.1.call-update) | async-done | bytes 2097168 | tf_op jit(solution)/shard_map/reduce_scatter | solution.py:179
  2177.6 168.8 %reduce-scatter.23.cloned.1.call-done = bf16[512,2048]{1,0:T(8,128)(2,1)} async-done(((bf16[4096,2048]{1,0:T(8,128)(2,1)}), bf16[512,2048]{1,0:T(8,128)(2,1)}) %reduce-scatter.23.cloned.1.call-update) | async-done | bytes 2097168 | tf_op jit(solution)/shard_map/reduce_scatter | solution.py:125
  2346.4 168.8 %reduce-scatter.13.cloned.1.call-done = bf16[256,4096]{1,0:T(8,128)(2,1)} async-done(((bf16[2048,4096]{1,0:T(8,128)(2,1)}), bf16[256,4096]{1,0:T(8,128)(2,1)}) %reduce-scatter.13.cloned.1.call-update) | async-done | bytes 2097168 | tf_op jit(solution)/shard_map/reduce_scatter | solution.py:176
  2568.3 13.9 fusion.24
  2582.3 27.8 all-reduce.9
  2630.0 166.8 %all-reduce.14.cloned.1.call-done = (bf16[256,2048]{1,0:T(8,128)(2,1)}, bf16[256,2048]{1,0:T(8,128)(2,1)}, bf16[256,4096]{1,0:T(8,128)(2,1)}, bf16[256,4096]{1,0...) async-done(((bf16[256,2048]{1,0:T(8,128)(2,1)}, bf16[256,2048]{1,0:T(8,128)(2,1)}, ...) | async-done | bytes 14680080 | tf_op jit(solution)/shard_map/psum | solution.py:190
  (307 shorter events, 646.2 us)
Async XLA Ops:
  7.2 87.3 %all-gather.20.cloned.1.call-start = ((), (), s32[]{:S(2)}) async-start(), calls=%async_computation.17 | async-start | bytes 9437184 | tf_op jit(solution)/shard_map/all_gather | solution.py:237
  7.9 168.8 %all-gather.22.cloned.1.call-start = ((), (), s32[]{:S(2)}) async-start(), calls=%async_computation.18 | async-start | bytes 9437184 | tf_op jit(solution)/shard_map/all_gather | solution.py:238
  8.7 319.3 %all-gather.18.cloned.1.call-start = ((), (), s32[]{:S(2)}) async-start(), calls=%async_computation.16 | async-start | bytes 18874368 | tf_op jit(solution)/shard_map/all_gather | solution.py:239
  9.4 573.7 %all-gather.24.cloned.1.call-start = ((), (), s32[]{:S(2)}) async-start(), calls=%async_computation.19 | async-start | bytes 18874368 | tf_op jit(solution)/shard_map/all_gather | solution.py:240
  10.0 620.2 %all-gather.26.cloned.1.call-start = ((), (), s32[]{:S(2)}) async-start(), calls=%async_computation.20 | async-start | bytes 18874368 | tf_op jit(solution)/shard_map/all_gather | solution.py:243
  10.6 770.4 %all-gather.28.cloned.1.call-start = ((), (), s32[]{:S(2)}) async-start(), calls=%async_computation.21 | async-start | bytes 18874368 | tf_op jit(solution)/shard_map/all_gather | solution.py:257
  11.2 15.1 copy-start.41
  11.2 24.0 copy-start
  11.2 920.8 %all-gather.30.cloned.1.call-start = ((), (), s32[]{:S(2)}) async-start(), calls=%async_computation.22 | async-start | bytes 18874368 | tf_op jit(solution)/shard_map/all_gather | solution.py:258
  11.9 1071.0 %all-gather.32.cloned.1.call-start = ((), (), s32[]{:S(2)}) async-start(), calls=%async_computation.23 | async-start | bytes 18874368 | tf_op jit(solution)/shard_map/all_gather | solution.py:261
  35.4 292.6 %copy-start.18 = (f32[256]{0:T(256)}, f32[256]{0:T(256)S(1)}, u32[]{:S(2)}) copy-start(f32[256]{0:T(256)S(1)} %broadcast_multiply_fusion.9) | copy-start | bytes 3076
  35.9 292.2 %copy-start.21 = (f32[256]{0:T(256)}, f32[256]{0:T(256)S(1)}, u32[]{:S(2)}) copy-start(f32[256]{0:T(256)S(1)} %add_rsqrt_fusion.1) | copy-start | bytes 3076
  121.5 81.7 %all-to-all-start.1 = ((bf16[4,2,65536]{2,1,0:T(2,128)(2,1)}), bf16[4,2,65536]{2,1,0:T(2,128)(2,1)}, u32[]{:S(2)}, u32[]{:S(2)}) async-start(bf16[4,2,65536]{2,1,0:T(2,128)(2,1)} %reshape.449), calls=%async_computation.1 | async-start | bytes 2097152 | tf_op jit(solution)/shard_map/all_to_all | solution.py:279
  203.2 164.1 %all-to-all-start.2 = ((bf16[4,2,65536]{2,1,0:T(2,128)(2,1)}), bf16[4,2,65536]{2,1,0:T(2,128)(2,1)}, u32[]{:S(2)}, u32[]{:S(2)}) async-start(bf16[4,2,65536]{2,1,0:T(2,128)(2,1)} %reshape.451), calls=%async_computation.2 | async-start | bytes 2097152 | tf_op jit(solution)/shard_map/all_to_all | solution.py:280
  367.3 35.5 %all-to-all-start = ((bf16[4,2,131072]{2,1,0:T(2,128)(2,1)}), bf16[4,2,131072]{2,1,0:T(2,128)(2,1)S(1)}, u32[]{:S(2)}, u32[]{:S(2)}) async-start(bf16[4,2,131072]{2,1,0:T(2,128)(2,1)} %reshape.447), calls=%async_computation | async-start | bytes 4194304 | tf_op jit(solution)/shard_map/all_to_all | solution.py:281
  371.0 24.1 copy-start.46
  444.8 24.3 copy-start.37
  444.8 37.6 %copy-start.42 = (bf16[256]{0:T(256)(128)(2,1)S(1)}, bf16[256]{0:T(256)(128)(2,1)}, u32[]{:S(2)}) copy-start(bf16[256]{0:T(256)(128)(2,1)} %param.29) | copy-start | bytes 1540
  444.8 46.9 %copy-start.43 = (bf16[256]{0:T(256)(128)(2,1)S(1)}, bf16[256]{0:T(256)(128)(2,1)}, u32[]{:S(2)}) copy-start(bf16[256]{0:T(256)(128)(2,1)} %param.30) | copy-start | bytes 1540
  444.8 57.8 %copy-start.38 = (bf16[512]{0:T(512)(128)(2,1)S(1)}, bf16[512]{0:T(512)(128)(2,1)}, u32[]{:S(2)}) copy-start(bf16[512]{0:T(512)(128)(2,1)} %param.33) | copy-start | bytes 3076
  444.8 72.0 %copy-start.39 = (bf16[512]{0:T(512)(128)(2,1)S(1)}, bf16[512]{0:T(512)(128)(2,1)}, u32[]{:S(2)}) copy-start(bf16[512]{0:T(512)(128)(2,1)} %param.34) | copy-start | bytes 3076
  444.8 93.5 %all-to-all-start.3 = ((bf16[4,2,131072]{2,1,0:T(2,128)(2,1)}), bf16[4,2,131072]{2,1,0:T(2,128)(2,1)S(1)}, u32[]{:S(2)}, u32[]{:S(2)}) async-start(bf16[4,2,131072]{2,1,0:T(2,128)(2,1)} %reshape.453), calls=%async_computation.3 | async-start | bytes 4194304 | tf_op jit(solution)/shard_map/all_to_all | solution.py:286
  449.1 1077.2 %reduce-scatter.11.cloned.1.call-start = ((), (), s32[]{:S(2)}) async-start(), calls=%async_computation.25 | async-start | bytes 9437184 | tf_op jit(solution)/shard_map/reduce_scatter | solution.py:173
  639.6 469.4 %copy-start.3 = (f32[256,2048]{1,0:T(8,128)}, f32[256,2048]{1,0:T(8,128)S(1)}, u32[]{:S(2)}) copy-start(f32[256,2048]{1,0:T(8,128)S(1)} %get-tuple-element.71) | copy-start | bytes 6291460
  1325.3 201.1 %reduce-scatter.9.cloned.1.call-start = ((), (), s32[]{:S(2)}) async-start(), calls=%async_computation.24 | async-start | bytes 9437184 | tf_op jit(solution)/shard_map/reduce_scatter | solution.py:170
  1381.8 289.2 %reduce-scatter.17.cloned.1.call-start = ((), (), s32[]{:S(2)}) async-start(), calls=%async_computation.28 | async-start | bytes 18874368 | tf_op jit(solution)/shard_map/reduce_scatter | solution.py:128
  1391.9 447.9 %reduce-scatter.19.cloned.1.call-start = ((), (), s32[]{:S(2)}) async-start(), calls=%async_computation.29 | async-start | bytes 18874368 | tf_op jit(solution)/shard_map/reduce_scatter | solution.py:119
  1404.3 604.4 %reduce-scatter.21.cloned.1.call-start = ((), (), s32[]{:S(2)}) async-start(), calls=%async_computation.30 | async-start | bytes 18874368 | tf_op jit(solution)/shard_map/reduce_scatter | solution.py:122
  1416.7 760.9 %reduce-scatter.15.cloned.1.call-start = ((), (), s32[]{:S(2)}) async-start(), calls=%async_computation.27 | async-start | bytes 18874368 | tf_op jit(solution)/shard_map/reduce_scatter | solution.py:179
  1427.6 918.9 %reduce-scatter.23.cloned.1.call-start = ((), (), s32[]{:S(2)}) async-start(), calls=%async_computation.31 | async-start | bytes 18874368 | tf_op jit(solution)/shard_map/reduce_scatter | solution.py:125
  1439.9 1075.4 %reduce-scatter.13.cloned.1.call-start = ((), (), s32[]{:S(2)}) async-start(), calls=%async_computation.26 | async-start | bytes 18874368 | tf_op jit(solution)/shard_map/reduce_scatter | solution.py:176
  1526.3 1270.5 %all-reduce.14.cloned.1.call-start = ((), (), s32[]{:S(2)}) async-start(), calls=%async_computation.32 | async-start | bytes 29360128 | tf_op jit(solution)/shard_map/psum | solution.py:190
  (38 other events, 214.2 us)
Sparse Core Ops, SparseCore 0:
  9.6 84.8 all-gather.19
  96.1 80.5 all-gather.21
  178.3 149.6 all-gather.17
  329.5 149.5 all-gather.23
  480.5 149.6 all-gather.25
  631.7 149.2 all-gather.27
  782.6 149.3 all-gather.29
  933.5 149.3 all-gather.31
  1325.4 86.3 reduce-scatter.10
  1413.9 87.9 reduce-scatter.8
  1504.3 166.5 reduce-scatter.16
  1673.2 166.5 reduce-scatter.18
  1842.1 166.5 reduce-scatter.20
  2011.0 166.5 reduce-scatter.14
  2179.8 166.5 reduce-scatter.22
  2348.6 166.5 reduce-scatter.12
  2519.7 276.9 all-reduce.13
where the time goes:
time: 2840 us; the launch traced here: 2820 us
  waiting for transfers between devices  1830 us (64%)
  matrix products  302 us (11%)
  blocking collectives  247 us (9%)
  local copies, waits for them, and re-layouts  230 us (8%)
  other arithmetic  179 us (6%)
    reduce_scatter x1, waiting for transfers between devices, upper_reduce(): lax.psum_scatter(terms[1].astype(jnp.bfloat16), 'fsdp', scatter_dimension...  169 us
    reduce_scatter x1, waiting for transfers between devices, lower_reduce(): lax.psum_scatter(terms[2].astype(jnp.bfloat16), 'fsdp', scatter_dimension...  169 us
    reduce_scatter x1, waiting for transfers between devices, upper_reduce(): lax.psum_scatter(terms[0].astype(jnp.bfloat16), 'fsdp', scatter_dimension...  169 us
    reduce_scatter x1, waiting for transfers between devices, lower_reduce(): lax.psum_scatter(terms[3].astype(jnp.bfloat16), 'fsdp', scatter_dimension...  169 us
    reduce_scatter x1, waiting for transfers between devices, upper_reduce(): lax.psum_scatter(terms[2].astype(jnp.bfloat16), 'fsdp', scatter_dimension...  169 us
    psum x1, waiting for transfers between devices, lower_reduce(): lax.psum(shares[0].astype(jnp.bfloat16), 'sp').astype(jnp.float32)  167 us
    reduce_scatter x1, waiting for transfers between devices, upper_reduce(): lax.psum_scatter(terms[3].astype(jnp.bfloat16), 'fsdp', scatter_dimension...  145 us
    all_gather x1, waiting for transfers between devices, local(): lax.all_gather(gating_weight, 'fsdp', axis=0, tiled=True)  139 us
  transfers between devices with their start and end apart: 21, of which 14 were waited for; matrix products, arithmetic and copies ran while one was open for 18% of the time, Pallas kernels for 0%

commit v1 on v0

v1 whole, which is shorter than its diff:
```python
import jax
import jax.numpy as jnp
from jax import lax
from jax.sharding import PartitionSpec as P

HEADS = 8
EPSILON = 1e-05
BF16 = jnp.bfloat16
F32 = jnp.float32


def product(left, right):
    return jnp.dot(left, right, preferred_element_type=F32)


def over_rows(left, right):
    return lax.dot_general(left, right, (((0,), (0,)), ((), ())), preferred_element_type=F32)


def over_columns(left, right):
    return lax.dot_general(left, right, (((1,), (1,)), ((), ())), preferred_element_type=F32)


def normalize(values):
    middle = jnp.mean(values, -1, keepdims=True)
    centred = values - middle
    spread = jnp.mean(centred * centred, -1, keepdims=True)
    factor = lax.rsqrt(spread + EPSILON)
    return (centred * factor, factor)


def group_normalize(values):
    middle = jnp.mean(values, -1, keepdims=True)
    centred = values - middle
    spread = jnp.mean(centred * centred, -1, keepdims=True)
    factor = lax.rsqrt(jnp.maximum(spread, 1.0))
    active = jnp.where(spread > 1.0, 1.0, 0.0)
    return (centred * factor, factor, active)


def normalize_back(scaled, normed, factor, active=1.0):
    first_mean = jnp.mean(scaled, -1, keepdims=True)
    second_mean = jnp.mean(scaled * normed, -1, keepdims=True)
    return factor * (scaled - first_mean - active * normed * second_mean)


def silu_slope(values):
    sigma = jax.nn.sigmoid(values)
    return sigma * (1.0 + values * (1.0 - sigma))


def decay_mask(head_ids, length):
    rates = jnp.log(1.0 - jnp.exp2(-5.0 - head_ids.astype(F32)))
    places = jnp.arange(length)
    distance = places[:, None] - places[None, :]
    steps = jnp.maximum(distance, 0).astype(F32)
    return jnp.where(distance[None] >= 0, jnp.exp(steps[None] * rates[:, None, None]), 0.0)


def split_heads(array, heads_here):
    return array.reshape(array.shape[0], heads_here, -1)


def score_block(query_split, key_split):
    factor = query_split.shape[-1] ** (-0.5)
    raw = jnp.einsum("ihd,jhd->hij", query_split, key_split, preferred_element_type=F32)
    return raw * factor


def retain(query, key, value, mask, heads_here):
    query_split = split_heads(query, heads_here)
    key_split = split_heads(key, heads_here)
    value_split = split_heads(value, heads_here)
    weights = (score_block(query_split, key_split) * mask).astype(BF16)
    output = jnp.einsum("hij,jhe->ihe", weights, value_split, preferred_element_type=F32)
    return output.astype(BF16)


def retain_back(query, key, value, grad_split, mask, heads_here):
    query_split = split_heads(query, heads_here)
    key_split = split_heads(key, heads_here)
    value_split = split_heads(value, heads_here)
    factor = query_split.shape[-1] ** (-0.5)
    weights = (score_block(query_split, key_split) * mask).astype(BF16)
    value_back = jnp.einsum("hij,ihe->jhe", weights, grad_split, preferred_element_type=F32)
    weight_back = jnp.einsum("ihe,jhe->hij", grad_split, value_split, preferred_element_type=F32)
    score_back = (weight_back * mask).astype(BF16)
    query_back = jnp.einsum("hij,jhd->ihd", score_back, key_split, preferred_element_type=F32) * factor
    key_back = jnp.einsum("hij,ihd->jhd", score_back, query_split, preferred_element_type=F32) * factor
    length = query.shape[0]
    return (
        query_back.astype(BF16).reshape(length, -1),
        key_back.astype(BF16).reshape(length, -1),
        value_back.astype(BF16).reshape(length, -1),
    )


class Ring:
    def __init__(self, size):
        half = size // 2
        self.size = size
        self.half = half
        self.order = list(range(half)) + list(range(size - 1, half - 1, -1))
        place = [0] * size
        for position, rank in enumerate(self.order):
            place[rank] = position
        self.right = [(self.order[i], self.order[(i + 1) % size]) for i in range(size)]
        self.left = [(self.order[i], self.order[(i - 1) % size]) for i in range(size)]
        self.me = lax.axis_index("sp")
        self.position = jnp.array(place, jnp.int32)[self.me]

    def rank(self, step):
        return jnp.array(self.order, jnp.int32)[lax.rem(self.position + step + self.size, self.size)]

    def to_right(self, block):
        return lax.ppermute(block, "sp", self.right)

    def to_left(self, block):
        return lax.ppermute(block, "sp", self.left)

    def gather(self, block):
        middle = block.shape[0] // 2
        found = [(0, block)]
        from_left, from_right = block, block
        for step in range(1, self.half):
            from_left, from_right = self.to_right(from_left), self.to_left(from_right)
            found += [(-step, from_left), (step, from_right)]
        low = self.to_right(from_left[:middle])
        high = self.to_left(from_right[middle:])
        found.append((self.half, jnp.concatenate([low, high], 0)))
        out = jnp.zeros((self.size,) + block.shape, block.dtype)
        for step, part in found:
            out = lax.dynamic_update_slice(out, part[None], (self.rank(step), 0, 0))
        return out

    def scatter_sum(self, make):
        far = make(self.rank(self.half)).astype(BF16)
        middle = far.shape[0] // 2
        from_left, from_right = self.to_right(far[:middle]), self.to_left(far[middle:])
        for step in range(self.half - 1, 0, -1):
            ahead, behind = make(self.rank(step)), make(self.rank(-step))
            if step == self.half - 1:
                ahead = jnp.concatenate([ahead[:middle] + from_left.astype(F32), ahead[middle:]], 0)
                behind = jnp.concatenate([behind[:middle], behind[middle:] + from_right.astype(F32)], 0)
            else:
                ahead = ahead + from_left.astype(F32)
                behind = behind + from_right.astype(F32)
            from_left, from_right = self.to_right(ahead.astype(BF16)), self.to_left(behind.astype(BF16))
        return make(self.me) + from_left.astype(F32) + from_right.astype(F32)


def butterfly(vector):
    for axis in ("fsdp", "sp"):
        size = lax.axis_size(axis)
        step = 1
        while step < size:
            vector = vector + lax.ppermute(vector, axis, [(i, i ^ step) for i in range(size)])
            step *= 2
    return vector


def spread_pairs(shards, parts):
    per_block = shards // parts
    pairs = []
    for shard in range(shards):
        for piece in range(parts):
            block, inner = divmod(shard, per_block)
            pairs.append((shard * parts + piece, (inner * parts + piece) * parts + block))
    return pairs


def local(
    tokens,
    attn_gain,
    attn_shift,
    query_weight,
    key_weight,
    value_weight,
    swish_weight,
    group_gain,
    group_shift,
    out_weight,
    ffn_gain,
    ffn_shift,
    gating_weight,
    upward_weight,
    gating_bias,
    upward_bias,
    downward_weight,
    downward_bias,
    cotangent,
):
    seq_count, local_len, width = tokens.shape
    assert seq_count == 1
    parts = lax.axis_size("sp")
    shards = lax.axis_size("fsdp")
    me = lax.axis_index("sp")
    ring = Ring(parts)
    heads_here = HEADS // parts
    full_len = local_len * parts
    value_all = value_weight.shape[1]
    hidden_all = gating_weight.shape[1]
    value_width = value_all // parts
    hidden_width = hidden_all // parts
    query_width = query_weight.shape[1] // parts
    chunk = hidden_width // shards

    def columns(weight):
        size = weight.shape[1] // parts
        return lax.dynamic_slice_in_dim(weight, me * size, size, 1)

    def units(weight):
        pieces = [
            lax.dynamic_slice_in_dim(weight, (i * parts + me) * chunk, chunk, weight.ndim - 1)
            for i in range(shards)
        ]
        return jnp.concatenate(pieces, -1)

    def gathered(array):
        return lax.all_gather(array, "fsdp", axis=0, tiled=True)

    qkv_slice = jnp.concatenate([columns(query_weight), columns(key_weight), columns(value_weight)], 1)
    qkv_full = gathered(qkv_slice)
    swish_full = gathered(columns(swish_weight))
    spread = spread_pairs(shards, parts)
    rows = out_weight.shape[0] // parts
    out_piece = lax.ppermute(
        lax.dynamic_slice_in_dim(out_weight, me * rows, rows, 0), ("fsdp", "sp"), spread
    )
    out_full = gathered(out_piece)
    both_full = gathered(jnp.concatenate([units(gating_weight), units(upward_weight)], 1))
    down_full = gathered(lax.dynamic_slice_in_dim(downward_weight, me * rows, rows, 0))

    small = [
        attn_gain, attn_shift, group_gain, group_shift, ffn_gain, ffn_shift,
        gating_bias, upward_bias, downward_bias,
    ]
    sizes = [item.shape[0] for item in small]
    stacked = gathered(jnp.concatenate(small, 0)[None])
    offsets = [sum(sizes[:i]) for i in range(len(sizes))]
    (
        gain_one, shift_one, ggain_all, gshift_all, gain_two, shift_two, gbias_all, ubias_all, dbias,
    ) = (
        stacked[:, start : start + size].reshape(-1).astype(F32)
        for start, size in zip(offsets, sizes)
    )
    ggain = lax.dynamic_slice_in_dim(ggain_all, me * value_width, value_width, 0)
    gshift = lax.dynamic_slice_in_dim(gshift_all, me * value_width, value_width, 0)
    gbias = units(gbias_all)
    ubias = units(ubias_all)

    flat = tokens.reshape(-1, width).astype(F32)
    first_norm, first_factor = normalize(flat)
    first = ring.gather((first_norm * gain_one + shift_one).astype(BF16)).reshape(full_len, width)
    grad_own = cotangent.reshape(-1, width)
    grad_low = ring.gather(grad_own).reshape(full_len, width)
    qkv = product(first, qkv_full).astype(BF16)
    query, key, value = (
        qkv[:, :query_width], qkv[:, query_width : 2 * query_width], qkv[:, 2 * query_width :],
    )
    head_ids = me * heads_here + jnp.arange(heads_here)
    mask = decay_mask(head_ids, full_len)
    retained = retain(query, key, value, mask, heads_here).astype(F32)
    group_norm3, group_factor, group_active = group_normalize(retained)
    group_norm = group_norm3.reshape(full_len, value_width)
    grouped = group_norm * ggain + gshift
    swish_pre = product(first, swish_full)
    swish_gate = jax.nn.silu(swish_pre)
    mixed = (grouped * swish_gate).astype(BF16)

    def rows_of(array, rank):
        return lax.dynamic_slice_in_dim(array, rank * local_len, local_len, 0)

    resid = flat + ring.scatter_sum(lambda rank: product(rows_of(mixed, rank), out_full))
    second_norm, second_factor = normalize(resid)
    second = ring.gather((second_norm * gain_two + shift_two).astype(BF16)).reshape(full_len, width)
    both = product(second, both_full)
    gating = both[:, :hidden_width] + gbias
    upward = both[:, hidden_width:] + ubias
    gate_act = jax.nn.silu(gating)
    hidden = (gate_act * upward).astype(BF16)

    dhidden = over_columns(grad_low, down_full)
    dgating = (dhidden * upward * silu_slope(gating)).astype(BF16)
    dupward = (dhidden * gate_act).astype(BF16)
    dboth = jnp.concatenate([dgating, dupward], 1)
    gbias_term = jnp.sum(dgating.astype(F32), 0)
    ubias_term = jnp.sum(dupward.astype(F32), 0)

    def summed(term):
        return lax.psum_scatter(term.astype(BF16), "fsdp", scatter_dimension=0, tiled=True)

    both_share = summed(over_rows(second, dboth))
    down_share = summed(over_rows(hidden, grad_low))
    dsecond = ring.scatter_sum(lambda rank: over_columns(rows_of(dboth, rank), both_full))
    fgain_term = jnp.sum(dsecond * second_norm, 0)
    fshift_term = jnp.sum(dsecond, 0)
    grad_out = grad_own.astype(F32)
    dbias_term = jnp.sum(grad_out, 0)
    dresid = grad_out + normalize_back(dsecond * gain_two, second_norm, second_factor)
    dres_low = ring.gather(dresid.astype(BF16)).reshape(full_len, width)
    out_share = summed(over_rows(mixed, dres_low))
    dmixed = over_columns(dres_low, out_full)
    dgrouped = dmixed * swish_gate
    dswish = (dmixed * grouped * silu_slope(swish_pre)).astype(BF16)
    swish_share = summed(over_rows(first, dswish))
    ggain_term = jnp.sum(dgrouped * group_norm, 0)
    gshift_term = jnp.sum(dgrouped, 0)
    dnormed = (dgrouped * ggain).reshape(full_len, heads_here, -1)
    dretained = normalize_back(dnormed, group_norm3, group_factor, group_active).astype(BF16)
    dqkv = jnp.concatenate(retain_back(query, key, value, dretained, mask, heads_here), 1)
    qkv_share = summed(over_rows(first, dqkv))
    dfirst = ring.scatter_sum(
        lambda rank: over_columns(rows_of(dqkv, rank), qkv_full)
        + over_columns(rows_of(dswish, rank), swish_full)
    )
    again_term = jnp.sum(dfirst * first_norm, 0)
    ashift_term = jnp.sum(dfirst, 0)
    input_grad = dresid + normalize_back(dfirst * gain_one, first_norm, first_factor)

    result = ring.scatter_sum(lambda rank: product(rows_of(hidden, rank), down_full))
    layer_out = (resid + result + dbias).astype(BF16)

    def by_columns(share):
        return jnp.moveaxis(ring.gather(share), 0, 1)

    qkv_all = by_columns(qkv_share).astype(F32)
    owned = qkv_share.shape[0]
    query_grad = qkv_all[:, :, :query_width].reshape(owned, -1)
    key_grad = qkv_all[:, :, query_width : 2 * query_width].reshape(owned, -1)
    value_grad = qkv_all[:, :, 2 * query_width :].reshape(owned, -1)
    swish_grad = by_columns(swish_share).astype(F32).reshape(owned, -1)
    both_all = ring.gather(both_share).astype(F32)
    both_all = both_all.reshape(parts, owned, 2, shards, chunk).transpose(2, 1, 3, 0, 4)
    both_all = both_all.reshape(2, owned, hidden_all)
    back = [(target, source) for source, target in spread]
    out_share = lax.ppermute(out_share, ("fsdp", "sp"), back)
    out_grad = ring.gather(out_share).astype(F32).reshape(-1, width)
    downward_grad = ring.gather(down_share).astype(F32).reshape(-1, width)

    def placed(term, whole):
        return lax.dynamic_update_slice(jnp.zeros((whole,), F32), term, (me * term.shape[0],))

    def placed_units(term):
        blank = jnp.zeros((shards, parts, chunk), F32)
        return lax.dynamic_update_slice(blank, term.reshape(shards, 1, chunk), (0, me, 0)).reshape(-1)

    terms = [
        again_term, ashift_term, placed(ggain_term, value_all), placed(gshift_term, value_all),
        fgain_term, fshift_term, placed_units(gbias_term), placed_units(ubias_term), dbias_term,
    ]
    totals = butterfly(jnp.concatenate([term.reshape(shards, -1) for term in terms], 1))
    mine = lax.dynamic_slice_in_dim(totals, lax.axis_index("fsdp"), 1, 0)[0]
    (
        again_grad, ashift_grad, ggain_grad, gshift_grad, fgain_grad, fshift_grad,
        gbias_grad, ubias_grad, dbias_grad,
    ) = (mine[start : start + size] for start, size in zip(offsets, sizes))
    return (
        layer_out.reshape(seq_count, local_len, width),
        input_grad.reshape(seq_count, local_len, width),
        again_grad,
        ashift_grad,
        query_grad,
        key_grad,
        value_grad,
        swish_grad,
        ggain_grad,
        gshift_grad,
        out_grad,
        fgain_grad,
        fshift_grad,
        both_all[0],
        both_all[1],
        gbias_grad,
        ubias_grad,
        downward_grad,
        dbias_grad,
    )


def solution(mesh):
    row, vector, cube = P("fsdp", None), P("fsdp"), P("fsdp", "sp", None)
    return jax.shard_map(
        local,
        mesh=mesh,
        in_specs=(
            cube, vector, vector, row, row, row, row, vector, vector, row,
            vector, vector, row, row, vector, vector, row, vector, cube,
        ),
        out_specs=(
            cube, cube, vector, vector, row, row, row, row, vector, vector,
            row, vector, vector, row, row, vector, vector, row, vector,
        ),
        check_vma=False,
    )
```

time: 2840 us -> 887 us (0.31)
  waiting for transfers between devices: 1830 us -> 289 us
  blocking collectives: 247 us -> 57.9 us
  other arithmetic: 179 us -> 60.4 us
  matrix products: 302 us -> 186 us
  starting transfers between devices: 17.3 us -> 103 us
  local copies, waits for them, and re-layouts: 230 us -> 153 us
    reduce_scatter x8 -> x5, waiting for transfers between devices: 989 us -> 32 us  [summed(): lax.psum_scatter(term.astype(BF16), 'fsdp', scatter_dimension=0, tiled=True)]
    all_gather x8 -> x5, waiting for transfers between devices: 671 us -> 18.9 us  [gathered(): return lax.all_gather(array, 'fsdp', axis=0, tiled=True)]
    ppermute x0 -> x59, waiting for transfers between devices: none -> 238 us  [the longest x26 176 us: to_left(): return lax.ppermute(block, 'sp', self.left)]
    psum x1 -> x0, waiting for transfers between devices: 167 us -> none  [lower_reduce(): lax.psum(shares[0].astype(jnp.bfloat16), 'sp').astype(jnp.float32)]
    unnamed x8 -> x7, other arithmetic: 113 us -> 0.02 us
    ppermute x0 -> x59, starting transfers between devices: none -> 102 us  [the longest x26 58.1 us: to_left(): return lax.ppermute(block, 'sp', self.left)]
    all_to_all x4 -> x0, blocking collectives: 91.3 us -> none  [the longest x1 30.5 us: local(): lax.all_to_all(by_seq(dretained.reshape(-1, value_width)), 'sp', split_ax...]
    unnamed x148 -> x215, local copies, waits for them, and re-layouts: 121 us -> 44.3 us
  transfers between devices with their start and end apart: 21 -> 69, of which waited for: 14 -> 35; matrix products, arithmetic and copies ran while one was open for 18% -> 41% of each run, Pallas kernels for 0% -> 0%
where the time goes in v1:
time: 887 us; the launch traced here: 878 us
  waiting for transfers between devices  289 us (33%)
  matrix products  186 us (21%)
  local copies, waits for them, and re-layouts  153 us (17%)
  starting transfers between devices  103 us (12%)
  other arithmetic  60.4 us (7%)
  blocking collectives  57.9 us (7%)
  between operations  28.7 us (3%)
    ppermute x26, waiting for transfers between devices, to_left(): return lax.ppermute(block, 'sp', self.left)  176 us
    dot_general x14, matrix products, over_columns(): lax.dot_general(left, right, (((1,), (1,)), ((), ())), preferred_element_...  59.2 us
    ppermute x26, starting transfers between devices, to_left(): return lax.ppermute(block, 'sp', self.left)  58.1 us
    all_gather x1, blocking collectives, gathered(): return lax.all_gather(array, 'fsdp', axis=0, tiled=True)  57.9 us
    dot_general x11, matrix products, product(): return jnp.dot(left, right, preferred_element_type=F32)  55.4 us
    dot_general x5, matrix products, over_rows(): lax.dot_general(left, right, (((0,), (0,)), ((), ())), preferred_element_...  53.7 us
    unnamed x215, local copies, waits for them, and re-layouts  44.3 us
    ppermute x26, waiting for transfers between devices, to_right(): return lax.ppermute(block, 'sp', self.right)  37.3 us
  transfers between devices with their start and end apart: 69, of which 35 were waited for; matrix products, arithmetic and copies ran while one was open for 41% of the time, Pallas kernels for 0%

profile of v1, /device:TPU:0, one launch (start us, length us, event | category | flops | bytes accessed | tf_op | source)
XLA Modules:
  0.0 877.9 jit_solution(12633751739679664242)
XLA Ops:
  32.3 57.9 %all-gather.1 = bf16[8,1,3328]{2,1,0:T(2,128)(2,1)S(1)} all-gather(bf16[1,1,3328]{2,1,0:T(2,128)(2,1)S(1)} %reshape.427), channel_id=2, replica_groups=mesh['fsdp'=8,'sp'=4] {'fsdp'}, dimensions={0}, use_global_device_ids=true | all-gather | bytes 59904 | tf_op jit(solution)/shard_map/all_gather | solution.py:220
  127.6 28.3 %collective-permute-done.3 = bf16[128,2048]{1,0:T(8,128)(2,1)S(1)} collective-permute-done((bf16[128,2048]{1,0:T(8,128)(2,1)S(1)}, bf16[128,2048]{1,0:T(8,128)(2,1)S(1)}, u32[]{:S(2)}, u32[]{:S(2)}) %collective-permute-start.3) | collective-permute-done | bytes 524320 | tf_op jit(solution)/shard_map/ppermute | solution.py:119
  157.0 12.5 %convolution_convert_fusion.2 = bf16[1024,2048]{1,0:T(8,128)(2,1)S(1)} fusion(bf16[1024,2048]{1,0:T(8,128)(2,1)} %bitcast.12, bf16[2048,2048]{1,0:T(8,128)(2,1)} %all-gather.8.cloned.1.call-done), kind=kOutput, calls=%fused_computation.50 | convolution fusion | flops 8592031744 | bytes 16777216 | tf_op jit(solution)/shard_map/dot_general | solution.py:13
  186.1 12.1 %multiply_convert_fusion.6 = (bf16[1024,1024]{0,1:T(8,128)(2,1)S(1)}, f32[1024,1024]{0,1:T(8,128)}) fusion(f32[1024,2,512]{0,2,1:T(8,128)} %fusion.6, f32[1024]{0:T(1024)S(1)} %dynamic_slice.339, f32[1024]{0:T(1024)S(1)} %dynamic_slice.338, bf16[1024,2048]{1,0:T(8,128)(2,1)} %bitcast.12, bf16[2048,1024]{1,0:T(8,128)(2,1)} %all-gather.10.cloned.1.call-done), kind=kOutput, calls=%fused_computation.44 | convolution fusion | flops 4303355904 | bytes 18882560 | tf_op jit(solution)/shard_map/dot_general | solution.py:13
  214.2 9.3 %collective-permute-done.7 = bf16[128,2048]{1,0:T(8,128)(2,1)S(1)} collective-permute-done((bf16[128,2048]{1,0:T(8,128)(2,1)S(1)}, bf16[128,2048]{1,0:T(8,128)(2,1)S(1)}, u32[]{:S(2)}, u32[]{:S(2)}) %collective-permute-start.7) | collective-permute-done | bytes 524320 | tf_op jit(solution)/shard_map/ppermute | solution.py:119
  234.7 13.6 %collective-permute-done.8 = bf16[256,2048]{1,0:T(8,128)(2,1)S(1)} collective-permute-done((bf16[256,2048]{1,0:T(8,128)(2,1)S(1)}, bf16[256,2048]{1,0:T(8,128)(2,1)S(1)}, u32[]{:S(2)}, u32[]{:S(2)}) %collective-permute-start.8) | collective-permute-done | bytes 1048608 | tf_op jit(solution)/shard_map/ppermute | solution.py:119
  272.0 15.5 %collective-permute-done.10 = bf16[256,2048]{1,0:T(8,128)(2,1)S(1)} collective-permute-done((bf16[256,2048]{1,0:T(8,128)(2,1)S(1)}, bf16[256,2048]{1,0:T(8,128)(2,1)S(1)}, u32[]{:S(2)}, u32[]{:S(2)}) %collective-permute-start.10) | collective-permute-done | bytes 1048608 | tf_op jit(solution)/shard_map/ppermute | solution.py:119
  298.8 8.2 collective-permute-done.12
  308.5 14.7 %fusion.138 = f32[1024,2048]{0,1:T(8,128)} fusion(bf16[1024,2048]{1,0:T(8,128)(2,1)} %bitcast.22, bf16[2048,2048]{1,0:T(8,128)(2,1)} %all-gather.14.cloned.1.call-done), kind=kOutput, calls=%fused_computation.337 | convolution fusion | flops 8589934592 | bytes 20971520 | tf_op jit(solution)/shard_map/dot_general | solution.py:13
  323.2 12.0 %all-gather.16.cloned.1.call-done = bf16[1024,2048]{1,0:T(8,128)(2,1)} async-done(((bf16[128,2048]{1,0:T(8,128)(2,1)}), bf16[1024,2048]{1,0:T(8,128)(2,1)}) %all-gather.16.cloned.1.call-update) | async-done | bytes 4194320 | tf_op jit(solution)/shard_map/all_gather | solution.py:220
  335.2 11.7 %convert_reduce_fusion = (f32[1024]{0:T(1024)S(1)}, bf16[1024,1024]{0,1:T(8,128)(2,1)S(1)}, f32[1024]{0:T(1024)S(1)}, bf16[1024,1024]{0,1:T(8,128)(2,1)S(1)}, bf16[1024,1024]{0,1:T(8,128)(2,1)S(1)}) fusion(f32[1024]{0:T(1024)S(1)} %constant_dynamic-update-slice_fusion.14, f32[1024,2048]{0,1:T(8,128)} %fusion.138, ...), kind=kOutput, calls=%fused_computation.36 | convolution fusion | flops 4316985344 | bytes 23085056 | tf_op jit(solution)/shard_map/dot_general | solution.py:21
  370.4 8.2 convolution_convert_fusion.3
  393.1 14.7 %collective-permute-done.24 = bf16[256,2048]{1,0:T(8,128)(2,1)S(1)} collective-permute-done((bf16[256,2048]{1,0:T(8,128)(2,1)S(1)}, bf16[256,2048]{1,0:T(8,128)(2,1)S(1)}, u32[]{:S(2)}, u32[]{:S(2)}) %collective-permute-start.24) | collective-permute-done | bytes 1048608 | tf_op jit(solution)/shard_map/ppermute | solution.py:119
  414.4 13.9 %collective-permute-done.16 = bf16[256,2048]{1,0:T(8,128)(2,1)S(1)} collective-permute-done((bf16[256,2048]{1,0:T(8,128)(2,1)S(1)}, bf16[256,2048]{1,0:T(8,128)(2,1)S(1)}, u32[]{:S(2)}, u32[]{:S(2)}) %collective-permute-start.16) | collective-permute-done | bytes 1048608 | tf_op jit(solution)/shard_map/ppermute | solution.py:119
  439.4 21.2 %collective-permute-done.26 = bf16[256,2048]{1,0:T(8,128)(2,1)S(1)} collective-permute-done((bf16[256,2048]{1,0:T(8,128)(2,1)S(1)}, bf16[256,2048]{1,0:T(8,128)(2,1)S(1)}, u32[]{:S(2)}, u32[]{:S(2)}) %collective-permute-start.26) | collective-permute-done | bytes 1048608 | tf_op jit(solution)/shard_map/ppermute | solution.py:119
  463.2 8.4 collective-permute-done.28
  472.7 8.4 fusion.126
  482.4 8.4 convolution_convert_fusion.5
  492.4 8.2 convolution_convert_fusion.4
  502.2 13.3 %convolution_convert_fusion = bf16[2048,2048]{1,0:T(8,128)(2,1)} fusion(bf16[1024,2048]{1,0:T(8,128)(2,1)} %bitcast.22, bf16[1024,1024]{0,1:T(8,128)(2,1)S(1)} %copy-done.68, bf16[1024,1024]{0,1:T(8,128)(2,1)} %copy-done.69), kind=kOutput, calls=%fused_computation.5 | convolution fusion | flops 8602517504 | bytes 16777216 | tf_op jit(solution)/shard_map/dot_general | solution.py:17
  537.2 15.6 %convolution_convert_fusion.1 = bf16[2048,2048]{1,0:T(8,128)(2,1)} fusion(bf16[1024,2048]{1,0:T(8,128)(2,1)} %bitcast.12, bf16[1024,1024]{0,1:T(8,128)(2,1)S(1)} %bitcast.335, bf16[1024,512]{0,1:T(8,128)(2,1)S(1)} %bitcast.341, bf16[1024,512]{0,1:T(8,128)(2,1)S(1)} %bitcast.343), kind=kOutput, calls=%fused_computation.6 | convolution fusion | flops 8606711808 | bytes 16777216 | tf_op jit(solution)/shard_map/dot_general | solution.py:17
  597.7 8.9 %collective-permute-done.30 = bf16[256,2048]{1,0:T(8,128)(2,1)S(1)} collective-permute-done((bf16[256,2048]{1,0:T(8,128)(2,1)S(1)}, bf16[256,2048]{1,0:T(8,128)(2,1)S(1)}, u32[]{:S(2)}, u32[]{:S(2)}) %collective-permute-start.30) | collective-permute-done | bytes 1048608 | tf_op jit(solution)/shard_map/ppermute | solution.py:116
  610.8 7.8 collective-permute-done.34
  619.8 11.6 %collective-permute-done.35 = f32[8,3328]{1,0:T(8,128)S(1)} collective-permute-done((f32[8,3328]{1,0:T(8,128)S(1)}, f32[8,3328]{1,0:T(8,128)S(1)}, u32[]{:S(2)}, u32[]{:S(2)}) %collective-permute-start.35) | collective-permute-done | bytes 106528 | tf_op jit(solution)/shard_map/ppermute | solution.py:157
  645.6 9.0 %collective-permute-done.56 = bf16[128,2048]{1,0:T(8,128)(2,1)S(1)} collective-permute-done((bf16[128,2048]{1,0:T(8,128)(2,1)}, bf16[128,2048]{1,0:T(8,128)(2,1)S(1)}, u32[]{:S(2)}, u32[]{:S(2)}) %collective-permute-start.56) | collective-permute-done | bytes 524320 | tf_op jit(solution)/shard_map/ppermute | solution.py:119
  681.7 9.9 %collective-permute-start.47 = (bf16[128,2048]{1,0:T(8,128)(2,1)}, bf16[128,2048]{1,0:T(8,128)(2,1)}, u32[]{:S(2)}, u32[]{:S(2)}) collective-permute-start(bf16[128,2048]{1,0:T(8,128)(2,1)} %collective-permute-done.46), channel_id=1, source_target_pairs={{0,1},{1,3},{3,2},{2,0},{4,5},{5,7},{7,6},{6,4},{8,9},{9,11},{11,1... | collective-permute-start | bytes 1572872 | tf_op jit(solution)/shard_map/ppermute | solution.py:116
  691.6 25.2 %collective-permute-start.48 = (bf16[128,2048]{1,0:T(8,128)(2,1)}, bf16[128,2048]{1,0:T(8,128)(2,1)}, u32[]{:S(2)}, u32[]{:S(2)}) collective-permute-start(bf16[128,2048]{1,0:T(8,128)(2,1)} %collective-permute-done.46), channel_id=1, source_target_pairs={{0,2},{1,0},{3,1},{2,3},{4,6},{5,4},{7,5},{6,7},{8,10},{9,8},{11,9... | collective-permute-start | bytes 1572872 | tf_op jit(solution)/shard_map/ppermute | solution.py:119
  758.9 10.9 %collective-permute-done.52 = bf16[256,2048]{1,0:T(8,128)(2,1)S(1)} collective-permute-done((bf16[256,2048]{1,0:T(8,128)(2,1)}, bf16[256,2048]{1,0:T(8,128)(2,1)S(1)}, u32[]{:S(2)}, u32[]{:S(2)}) %collective-permute-start.52) | collective-permute-done | bytes 1048608 | tf_op jit(solution)/shard_map/ppermute | solution.py:119
  775.6 32.0 %reduce-scatter.6.cloned.1.call-done = bf16[256,2048]{1,0:T(8,128)(2,1)} async-done(((bf16[2048,2048]{1,0:T(8,128)(2,1)}), bf16[256,2048]{1,0:T(8,128)(2,1)}) %reduce-scatter.6.cloned.1.call-update) | async-done | bytes 1048592 | tf_op jit(solution)/shard_map/reduce_scatter | solution.py:291
  817.6 12.1 %copy.171 = f32[4,256,2,8,128]{4,0,3,1,2:T(4,128)} copy(f32[4,256,2,8,128]{4,3,2,1,0:T(8,128)} %bitcast.324) | data formatting | bytes 16777216 | tf_op jit(solution)/shard_map/transpose | solution.py:334
  829.7 8.9 %fusion.128 = (f32[1,256,8,4,128]{4,3,2,1,0:T(4,128)}, f32[1,256,8,4,128]{4,3,2,1,0:T(4,128)}) fusion(f32[2,256,8,4,128]{4,3,2,1,0:T(4,128)} %bitcast.323), kind=kLoop, calls=%fused_computation.327 | loop fusion | bytes 16777216 | tf_op jit(solution)/shard_map/slice | solution.py:373
  853.5 8.4 collective-permute-done.41
  (549 shorter events, 388.3 us)
Async XLA Ops:
  7.2 149.8 %all-gather.8.cloned.1.call-start = ((), (), s32[]{:S(2)}) async-start(), calls=%async_computation.5 | async-start | bytes 9437184 | tf_op jit(solution)/shard_map/all_gather | solution.py:220
  10.6 175.5 %all-gather.10.cloned.1.call-start = ((), (), s32[]{:S(2)}) async-start(), calls=%async_computation.6 | async-start | bytes 4718592 | tf_op jit(solution)/shard_map/all_gather | solution.py:220
  12.7 192.5 %all-gather.12.cloned.1.call-start = ((), (), s32[]{:S(2)}) async-start(), calls=%async_computation.7 | async-start | bytes 4718592 | tf_op jit(solution)/shard_map/all_gather | solution.py:220
  15.3 293.1 %all-gather.14.cloned.1.call-start = ((), (), s32[]{:S(2)}) async-start(), calls=%async_computation.8 | async-start | bytes 9437184 | tf_op jit(solution)/shard_map/all_gather | solution.py:220
  30.4 304.8 %all-gather.16.cloned.1.call-start = ((), (), s32[]{:S(2)}) async-start(), calls=%async_computation.9 | async-start | bytes 4718592 | tf_op jit(solution)/shard_map/all_gather | solution.py:220
  92.4 30.8 %collective-permute-start = (bf16[256,2048]{1,0:T(8,128)(2,1)}, bf16[256,2048]{1,0:T(8,128)(2,1)S(1)}, u32[]{:S(2)}, u32[]{:S(2)}) collective-permute-start(bf16[256,2048]{1,0:T(8,128)(2,1)} %fusion.23), channel_id=1, source_target_pairs={{0,1},{1,3},{3,2},{2,0},{4,5},{5,7},{7,6},{6,4},{8,9},{9,11},{11,1... | collective-permute-start | bytes 3145736 | tf_op jit(solution)/shard_map/ppermute | solution.py:116
  96.9 26.2 %collective-permute-start.1 = (bf16[256,2048]{1,0:T(8,128)(2,1)}, bf16[256,2048]{1,0:T(8,128)(2,1)S(1)}, u32[]{:S(2)}, u32[]{:S(2)}) collective-permute-start(bf16[256,2048]{1,0:T(8,128)(2,1)} %fusion.23), channel_id=1, source_target_pairs={{0,2},{1,0},{3,1},{2,3},{4,6},{5,4},{7,5},{6,7},{8,10},{9,8},{11,9... | collective-permute-start | bytes 3145736 | tf_op jit(solution)/shard_map/ppermute | solution.py:119
  96.9 168.8 %collective-permute-start.17 = (bf16[256,2048]{1,0:T(8,128)(2,1)}, bf16[256,2048]{1,0:T(8,128)(2,1)}, u32[]{:S(2)}, u32[]{:S(2)}) collective-permute-start(bf16[256,2048]{1,0:T(8,128)(2,1)} %bitcast.24), channel_id=1, source_target_pairs={{0,1},{1,3},{3,2},{2,0},{4,5},{5,7},{7,6},{6,4},{8,9},{9,11},{11,1... | collective-permute-start | bytes 3145736 | tf_op jit(solution)/shard_map/ppermute | solution.py:116
  98.9 164.2 %collective-permute-start.18 = (bf16[256,2048]{1,0:T(8,128)(2,1)}, bf16[256,2048]{1,0:T(8,128)(2,1)}, u32[]{:S(2)}, u32[]{:S(2)}) collective-permute-start(bf16[256,2048]{1,0:T(8,128)(2,1)} %bitcast.24), channel_id=1, source_target_pairs={{0,2},{1,0},{3,1},{2,3},{4,6},{5,4},{7,5},{6,7},{8,10},{9,8},{11,9... | collective-permute-start | bytes 3145736 | tf_op jit(solution)/shard_map/ppermute | solution.py:119
  100.8 540.8 %reduce-scatter.14.cloned.1.call-start = ((), (), s32[]{:S(2)}) async-start(), calls=%async_computation.14 | async-start | bytes 4718592 | tf_op jit(solution)/shard_map/reduce_scatter | solution.py:291
  123.2 32.8 %collective-permute-start.3 = (bf16[128,2048]{1,0:T(8,128)(2,1)S(1)}, bf16[128,2048]{1,0:T(8,128)(2,1)S(1)}, u32[]{:S(2)}, u32[]{:S(2)}) collective-permute-start(bf16[128,2048]{1,0:T(8,128)(2,1)S(1)} %slice.329), channel_id=1, source_target_pairs={{0,2},{1,0},{3,1},{2,3},{4,6},{5,4},{7,5},{6,7},{8,10},{9,8},{11,9... | collective-permute-start | bytes 1572872 | tf_op jit(solution)/shard_map/ppermute | solution.py:119
  123.3 32.6 %collective-permute-start.2 = (bf16[128,2048]{1,0:T(8,128)(2,1)S(1)}, bf16[128,2048]{1,0:T(8,128)(2,1)S(1)}, u32[]{:S(2)}, u32[]{:S(2)}) collective-permute-start(bf16[128,2048]{1,0:T(8,128)(2,1)S(1)} %slice.328), channel_id=1, source_target_pairs={{0,1},{1,3},{3,2},{2,0},{4,5},{5,7},{7,6},{6,4},{8,9},{9,11},{11,1... | collective-permute-start | bytes 1572872 | tf_op jit(solution)/shard_map/ppermute | solution.py:116
  261.0 28.2 %collective-permute-start.9 = (bf16[256,2048]{1,0:T(8,128)(2,1)S(1)}, bf16[256,2048]{1,0:T(8,128)(2,1)S(1)}, u32[]{:S(2)}, u32[]{:S(2)}) collective-permute-start(bf16[256,2048]{1,0:T(8,128)(2,1)S(1)} %get-tuple-element.41), channel_id=1, source_target_pairs={{0,1},{1,3},{3,2},{2,0},{4,5},{5,7},{7,6},{6,4},{8,9},{9,11},{11,1... | collective-permute-start | bytes 3145736 | tf_op jit(solution)/shard_map/ppermute | solution.py:116
  264.2 34.6 %collective-permute-start.20 = (bf16[128,2048]{1,0:T(8,128)(2,1)S(1)}, bf16[128,2048]{1,0:T(8,128)(2,1)S(1)}, u32[]{:S(2)}, u32[]{:S(2)}) collective-permute-start(bf16[128,2048]{1,0:T(8,128)(2,1)S(1)} %slice.357), channel_id=1, source_target_pairs={{0,2},{1,0},{3,1},{2,3},{4,6},{5,4},{7,5},{6,7},{8,10},{9,8},{11,9... | collective-permute-start | bytes 1572872 | tf_op jit(solution)/shard_map/ppermute | solution.py:119
  266.8 32.0 %collective-permute-start.19 = (bf16[128,2048]{1,0:T(8,128)(2,1)S(1)}, bf16[128,2048]{1,0:T(8,128)(2,1)S(1)}, u32[]{:S(2)}, u32[]{:S(2)}) collective-permute-start(bf16[128,2048]{1,0:T(8,128)(2,1)S(1)} %slice.356), channel_id=1, source_target_pairs={{0,1},{1,3},{3,2},{2,0},{4,5},{5,7},{7,6},{6,4},{8,9},{9,11},{11,1... | collective-permute-start | bytes 1572872 | tf_op jit(solution)/shard_map/ppermute | solution.py:116
  350.4 28.3 %collective-permute-start.23 = (bf16[128,2048]{1,0:T(8,128)(2,1)}, bf16[128,2048]{1,0:T(8,128)(2,1)}, u32[]{:S(2)}, u32[]{:S(2)}) collective-permute-start(bf16[128,2048]{1,0:T(8,128)(2,1)} %get-tuple-element.56), channel_id=1, source_target_pairs={{0,2},{1,0},{3,1},{2,3},{4,6},{5,4},{7,5},{6,7},{8,10},{9,8},{11,9... | collective-permute-start | bytes 1572872 | tf_op jit(solution)/shard_map/ppermute | solution.py:119
  378.6 284.5 %reduce-scatter.8.cloned.1.call-start = ((), (), s32[]{:S(2)}) async-start(), calls=%async_computation.11 | async-start | bytes 4718592 | tf_op jit(solution)/shard_map/reduce_scatter | solution.py:291
  381.6 26.2 %collective-permute-start.24 = (bf16[256,2048]{1,0:T(8,128)(2,1)S(1)}, bf16[256,2048]{1,0:T(8,128)(2,1)S(1)}, u32[]{:S(2)}, u32[]{:S(2)}) collective-permute-start(bf16[256,2048]{1,0:T(8,128)(2,1)S(1)} %pad_maximum_fusion.9), channel_id=1, source_target_pairs={{0,2},{1,0},{3,1},{2,3},{4,6},{5,4},{7,5},{6,7},{8,10},{9,8},{11,9... | collective-permute-start | bytes 3145736 | tf_op jit(solution)/shard_map/ppermute | solution.py:119
  384.5 26.2 %collective-permute-start.22 = (bf16[256,2048]{1,0:T(8,128)(2,1)S(1)}, bf16[256,2048]{1,0:T(8,128)(2,1)S(1)}, u32[]{:S(2)}, u32[]{:S(2)}) collective-permute-start(bf16[256,2048]{1,0:T(8,128)(2,1)S(1)} %pad_maximum_fusion.8), channel_id=1, source_target_pairs={{0,1},{1,3},{3,2},{2,0},{4,5},{5,7},{7,6},{6,4},{8,9},{9,11},{11,1... | collective-permute-start | bytes 3145736 | tf_op jit(solution)/shard_map/ppermute | solution.py:116
  386.6 41.6 %collective-permute-start.16 = (bf16[256,2048]{1,0:T(8,128)(2,1)S(1)}, bf16[256,2048]{1,0:T(8,128)(2,1)S(1)}, u32[]{:S(2)}, u32[]{:S(2)}) collective-permute-start(bf16[256,2048]{1,0:T(8,128)(2,1)S(1)} %pad_maximum_fusion.7), channel_id=1, source_target_pairs={{0,2},{1,0},{3,1},{2,3},{4,6},{5,4},{7,5},{6,7},{8,10},{9,8},{11,9... | collective-permute-start | bytes 3145736 | tf_op jit(solution)/shard_map/ppermute | solution.py:119
  389.5 41.3 %collective-permute-start.14 = (bf16[256,2048]{1,0:T(8,128)(2,1)S(1)}, bf16[256,2048]{1,0:T(8,128)(2,1)S(1)}, u32[]{:S(2)}, u32[]{:S(2)}) collective-permute-start(bf16[256,2048]{1,0:T(8,128)(2,1)S(1)} %pad_maximum_fusion.6), channel_id=1, source_target_pairs={{0,1},{1,3},{3,2},{2,0},{4,5},{5,7},{7,6},{6,4},{8,9},{9,11},{11,1... | collective-permute-start | bytes 3145736 | tf_op jit(solution)/shard_map/ppermute | solution.py:116
  490.8 177.1 %reduce-scatter.10.cloned.1.call-start = ((), (), s32[]{:S(2)}) async-start(), calls=%async_computation.12 | async-start | bytes 4718592 | tf_op jit(solution)/shard_map/reduce_scatter | solution.py:291
  500.6 248.5 %reduce-scatter.12.cloned.1.call-start = ((), (), s32[]{:S(2)}) async-start(), calls=%async_computation.13 | async-start | bytes 9437184 | tf_op jit(solution)/shard_map/reduce_scatter | solution.py:291
  515.6 292.0 %reduce-scatter.6.cloned.1.call-start = ((), (), s32[]{:S(2)}) async-start(), calls=%async_computation.10 | async-start | bytes 9437184 | tf_op jit(solution)/shard_map/reduce_scatter | solution.py:291
  678.8 41.5 %collective-permute-start.45 = (bf16[128,1024]{1,0:T(8,128)(2,1)S(1)}, bf16[128,1024]{1,0:T(8,128)(2,1)S(1)}, u32[]{:S(2)}, u32[]{:S(2)}) collective-permute-start(bf16[128,1024]{1,0:T(8,128)(2,1)S(1)} %slice.380), channel_id=1, source_target_pairs={{0,2},{1,0},{3,1},{2,3},{4,6},{5,4},{7,5},{6,7},{8,10},{9,8},{11,9... | collective-permute-start | bytes 786440 | tf_op jit(solution)/shard_map/ppermute | solution.py:119
  678.9 41.4 %collective-permute-start.44 = (bf16[128,1024]{1,0:T(8,128)(2,1)S(1)}, bf16[128,1024]{1,0:T(8,128)(2,1)S(1)}, u32[]{:S(2)}, u32[]{:S(2)}) collective-permute-start(bf16[128,1024]{1,0:T(8,128)(2,1)S(1)} %slice.379), channel_id=1, source_target_pairs={{0,1},{1,3},{3,2},{2,0},{4,5},{5,7},{7,6},{6,4},{8,9},{9,11},{11,1... | collective-permute-start | bytes 786440 | tf_op jit(solution)/shard_map/ppermute | solution.py:116
  681.7 56.4 %collective-permute-start.47 = (bf16[128,2048]{1,0:T(8,128)(2,1)}, bf16[128,2048]{1,0:T(8,128)(2,1)}, u32[]{:S(2)}, u32[]{:S(2)}) collective-permute-start(bf16[128,2048]{1,0:T(8,128)(2,1)} %collective-permute-done.46), channel_id=1, source_target_pairs={{0,1},{1,3},{3,2},{2,0},{4,5},{5,7},{7,6},{6,4},{8,9},{9,11},{11,1... | collective-permute-start | bytes 1572872 | tf_op jit(solution)/shard_map/ppermute | solution.py:116
  691.6 43.4 %collective-permute-start.48 = (bf16[128,2048]{1,0:T(8,128)(2,1)}, bf16[128,2048]{1,0:T(8,128)(2,1)}, u32[]{:S(2)}, u32[]{:S(2)}) collective-permute-start(bf16[128,2048]{1,0:T(8,128)(2,1)} %collective-permute-done.46), channel_id=1, source_target_pairs={{0,2},{1,0},{3,1},{2,3},{4,6},{5,4},{7,5},{6,7},{8,10},{9,8},{11,9... | collective-permute-start | bytes 1572872 | tf_op jit(solution)/shard_map/ppermute | solution.py:119
  770.6 39.1 %collective-permute-start.54 = (bf16[128,2048]{1,0:T(8,128)(2,1)}, bf16[128,2048]{1,0:T(8,128)(2,1)S(1)}, u32[]{:S(2)}, u32[]{:S(2)}) collective-permute-start(bf16[128,2048]{1,0:T(8,128)(2,1)} %slice.388), channel_id=1, source_target_pairs={{0,2},{1,0},{3,1},{2,3},{4,6},{5,4},{7,5},{6,7},{8,10},{9,8},{11,9... | collective-permute-start | bytes 1572872 | tf_op jit(solution)/shard_map/ppermute | solution.py:119
  773.5 36.3 %collective-permute-start.53 = (bf16[128,2048]{1,0:T(8,128)(2,1)}, bf16[128,2048]{1,0:T(8,128)(2,1)S(1)}, u32[]{:S(2)}, u32[]{:S(2)}) collective-permute-start(bf16[128,2048]{1,0:T(8,128)(2,1)} %slice.387), channel_id=1, source_target_pairs={{0,1},{1,3},{3,2},{2,0},{4,5},{5,7},{7,6},{6,4},{8,9},{9,11},{11,1... | collective-permute-start | bytes 1572872 | tf_op jit(solution)/shard_map/ppermute | solution.py:116
  807.6 44.9 %collective-permute-start.38 = (bf16[256,2048]{1,0:T(8,128)(2,1)}, bf16[256,2048]{1,0:T(8,128)(2,1)S(1)}, u32[]{:S(2)}, u32[]{:S(2)}) collective-permute-start(bf16[256,2048]{1,0:T(8,128)(2,1)} %reduce-scatter.6.cloned.1.call-done), channel_id=1, source_target_pairs={{0,1},{1,3},{3,2},{2,0},{4,5},{5,7},{7,6},{6,4},{8,9},{9,11},{11,1... | collective-permute-start | bytes 3145736 | tf_op jit(solution)/shard_map/ppermute | solution.py:116
  809.0 41.9 %collective-permute-start.39 = (bf16[256,2048]{1,0:T(8,128)(2,1)}, bf16[256,2048]{1,0:T(8,128)(2,1)S(1)}, u32[]{:S(2)}, u32[]{:S(2)}) collective-permute-start(bf16[256,2048]{1,0:T(8,128)(2,1)} %reduce-scatter.6.cloned.1.call-done), channel_id=1, source_target_pairs={{0,2},{1,0},{3,1},{2,3},{4,6},{5,4},{7,5},{6,7},{8,10},{9,8},{11,9... | collective-permute-start | bytes 3145736 | tf_op jit(solution)/shard_map/ppermute | solution.py:119
  (115 other events, 1546.1 us)
Sparse Core Ops, SparseCore 0:
  10.7 97.7 all-gather.7
  110.7 46.2 all-gather.9
  159.3 45.8 all-gather.11
  207.2 80.7 all-gather.13
  289.5 45.6 all-gather.15
  378.8 48.6 reduce-scatter.13
  490.9 47.6 reduce-scatter.7
  540.9 48.1 reduce-scatter.9
  591.4 102.5 reduce-scatter.11
  696.1 111.4 reduce-scatter.5

commit v2 on v1

v2 whole, which is shorter than its diff:
```python
import functools

import jax
import jax.numpy as jnp
from jax import lax
from jax.experimental import pallas as pl
from jax.experimental.pallas import tpu as pltpu
from jax.sharding import PartitionSpec as P

HEADS = 8
EPSILON = 1e-05
BF16 = jnp.bfloat16
F32 = jnp.float32
COST = pl.CostEstimate(flops=1024, bytes_accessed=1024, transcendentals=0)
UNREAD = pl.BlockSpec(memory_space=pl.ANY)
NT = (((1,), (1,)), ((), ()))
NN = (((1,), (0,)), ((), ()))
TN = (((0,), (0,)), ((), ()))


def dot(left, right, dims):
    return lax.dot_general(left, right, dims, preferred_element_type=F32)


def product(left, right):
    return dot(left, right, NN)


def over_rows(left, right):
    return dot(left, right, TN)


def after(value, *others):
    return lax.optimization_barrier((value,) + others)[0]


def normalize(values):
    middle = jnp.mean(values, -1, keepdims=True)
    centred = values - middle
    spread = jnp.mean(centred * centred, -1, keepdims=True)
    factor = lax.rsqrt(spread + EPSILON)
    return (centred * factor, factor)


def group_normalize(values):
    middle = jnp.mean(values, -1, keepdims=True)
    centred = values - middle
    spread = jnp.mean(centred * centred, -1, keepdims=True)
    factor = lax.rsqrt(jnp.maximum(spread, 1.0))
    active = jnp.where(spread > 1.0, 1.0, 0.0)
    return (centred * factor, factor, active)


def normalize_back(scaled, normed, factor, active=1.0):
    first_mean = jnp.mean(scaled, -1, keepdims=True)
    second_mean = jnp.mean(scaled * normed, -1, keepdims=True)
    return factor * (scaled - first_mean - active * normed * second_mean)


def silu_slope(values, sigma):
    return sigma * (1.0 + values * (1.0 - sigma))


def decay_rates(head_ids):
    return jnp.log(1.0 - jnp.exp2(-5.0 - head_ids.astype(F32)))


def decay_block(rate, size, blocks_apart):
    distance = (
        lax.broadcasted_iota(jnp.int32, (size, size), 0)
        - lax.broadcasted_iota(jnp.int32, (size, size), 1)
        + blocks_apart * size
    )
    decay = jnp.exp(jnp.maximum(distance, 0).astype(F32) * rate)
    return jnp.where(distance >= 0, decay, 0.0) if blocks_apart == 0 else decay


def project(first, first_full, third):
    length, width = first.shape
    total = first_full.shape[1]
    step = 512
    steps, low_steps = total // step, third // step

    def kernel(x_ref, w_ref, low_ref, high_ref):
        terms = dot(x_ref[...], w_ref[...], NN)

        @pl.when(pl.program_id(0) < low_steps)
        def _():
            low_ref[...] = terms.astype(BF16)

        @pl.when(pl.program_id(0) >= low_steps)
        def _():
            high_ref[...] = terms

    return pl.pallas_call(
        kernel,
        grid=(steps,),
        in_specs=[
            pl.BlockSpec((length, width), lambda n: (0, 0)),
            pl.BlockSpec((width, step), lambda n: (0, n)),
        ],
        out_specs=[
            pl.BlockSpec((length, step), lambda n: (0, jnp.minimum(n, low_steps - 1))),
            pl.BlockSpec((length, step), lambda n: (0, jnp.maximum(n - low_steps, 0))),
        ],
        out_shape=[
            jax.ShapeDtypeStruct((length, third), BF16),
            jax.ShapeDtypeStruct((length, total - third), F32),
        ],
        cost_estimate=COST,
        name="project",
    )(first, first_full)


def retain_mix(qkv, swish_pre, rates, ggain, gshift, query_width, value_width, places):
    length = qkv.shape[0]
    heads_here = rates.shape[0]
    narrow, wide = query_width // heads_here, value_width // heads_here
    block = 256
    count = length // block
    factor = narrow ** (-0.5)

    size = value_width // places.shape[0]
    chunks = wide // size

    def kernel(rate_ref, place_ref, q_ref, k_ref, v_ref, s_ref, gain_ref, shift_ref, r_ref, m_ref):
        rate = rate_ref[pl.program_id(0)]
        decays = [decay_block(rate, block, apart) for apart in range(count)]
        for i in range(count):
            rows = slice(i * block, (i + 1) * block)
            query = q_ref[rows, :]
            total = jnp.zeros((block, wide), F32)
            for j in range(i + 1):
                cols = slice(j * block, (j + 1) * block)
                weights = (dot(query, k_ref[cols, :], NT) * factor * decays[i - j]).astype(BF16)
                total += dot(weights, v_ref[cols, :], NN)
            retained = total.astype(BF16)
            r_ref[rows, :] = retained
            normed = group_normalize(retained.astype(F32))[0]
            swish = s_ref[rows, :]
            grouped = normed * gain_ref[...] + shift_ref[...]
            mixed = (grouped * (swish * jax.nn.sigmoid(swish))).astype(BF16)
            if size % 128:
                m_ref[rows, :] = mixed
            else:
                for k in range(chunks):
                    at = pl.multiple_of(place_ref[pl.program_id(0) * chunks + k] * size, size)
                    m_ref[rows, pl.ds(at, size)] = mixed[:, k * size : (k + 1) * size]

    def head(width, start):
        return pl.BlockSpec((length, width), lambda h: (0, start // width + h))

    flat = pl.BlockSpec((1, wide), lambda h: (0, h))
    moved = head(wide, 0) if size % 128 else pl.BlockSpec((length, value_width), lambda h: (0, 0))
    return pl.pallas_call(
        kernel,
        grid=(heads_here,),
        in_specs=[
            pl.BlockSpec(memory_space=pltpu.SMEM),
            pl.BlockSpec(memory_space=pltpu.SMEM),
            head(narrow, 0),
            head(narrow, query_width),
            head(wide, 2 * query_width),
            head(wide, 0),
            flat,
            flat,
        ],
        out_specs=[head(wide, 0), moved],
        out_shape=[jax.ShapeDtypeStruct((length, value_width), BF16)] * 2,
        cost_estimate=COST,
        name="retain_mix",
    )(rates, places, qkv, qkv, qkv, swish_pre, ggain[None], gshift[None])


def retain_back(qkv, dretained, rates, query_width, value_width, deps):
    length = qkv.shape[0]
    heads_here = rates.shape[0]
    narrow, wide = query_width // heads_here, value_width // heads_here
    block = 256
    count = length // block
    factor = narrow ** (-0.5)

    def kernel(rate_ref, q_ref, k_ref, v_ref, g_ref, *rest):
        dq_ref, dk_ref, dv_ref, acc_ref = rest[len(deps) :]
        rate = rate_ref[pl.program_id(0)]
        decays = [decay_block(rate, block, apart) for apart in range(count)]
        acc_ref[...] = jnp.zeros_like(acc_ref)
        for j in range(count):
            cols = slice(j * block, (j + 1) * block)
            key, value = k_ref[cols, :], v_ref[cols, :]
            dkey = jnp.zeros((block, narrow), F32)
            dvalue = jnp.zeros((block, wide), F32)
            for i in range(j, count):
                rows = slice(i * block, (i + 1) * block)
                query, grad = q_ref[rows, :], g_ref[rows, :]
                decay = decays[i - j]
                weights = (dot(query, key, NT) * factor * decay).astype(BF16)
                dvalue += dot(weights, grad, TN)
                dscores = (dot(grad, value, NT) * decay).astype(BF16)
                acc_ref[rows, :] += dot(dscores, key, NN)
                dkey += dot(dscores, query, TN)
            dk_ref[cols, :] = (dkey * factor).astype(BF16)
            dv_ref[cols, :] = dvalue.astype(BF16)
        dq_ref[...] = (acc_ref[...] * factor).astype(BF16)

    def head(width, start):
        return pl.BlockSpec((length, width), lambda h: (0, start // width + h))

    return pl.pallas_call(
        kernel,
        grid=(heads_here,),
        in_specs=[
            pl.BlockSpec(memory_space=pltpu.SMEM),
            head(narrow, 0),
            head(narrow, query_width),
            head(wide, 2 * query_width),
            head(wide, 0),
        ]
        + [UNREAD] * len(deps),
        out_specs=[head(narrow, 0), head(narrow, 0), head(wide, 0)],
        out_shape=[
            jax.ShapeDtypeStruct((length, query_width), BF16),
            jax.ShapeDtypeStruct((length, query_width), BF16),
            jax.ShapeDtypeStruct((length, value_width), BF16),
        ],
        scratch_shapes=[pltpu.VMEM((length, narrow), F32)],
        cost_estimate=COST,
        name="retain_back",
    )(rates, qkv, qkv, qkv, dretained, *deps)


def gate_back(grad, down_full, both, gbias, ubias, deps):
    length, width = grad.shape
    hidden = down_full.shape[0]
    block, rows = 256, 128
    steps = hidden // block

    def kernel(g_ref, w_ref, gate_ref, up_ref, gb_ref, ub_ref, *rest):
        dg_ref, du_ref, gsum_ref, usum_ref, acc_ref = rest[len(deps) :]
        acc_ref[...] = dot(g_ref[...], w_ref[...], NT)
        gsum_ref[...] = jnp.zeros_like(gsum_ref)
        usum_ref[...] = jnp.zeros_like(usum_ref)

        @pl.loop(0, length // rows)
        def _(i):
            at = pl.ds(pl.multiple_of(i * rows, rows), rows)
            dhidden = acc_ref[at, :]
            gating, upward = gate_ref[at, :] + gb_ref[...], up_ref[at, :] + ub_ref[...]
            sigma = jax.nn.sigmoid(gating)
            dgating = (dhidden * upward * silu_slope(gating, sigma)).astype(BF16)
            dupward = (dhidden * (gating * sigma)).astype(BF16)
            dg_ref[at, :] = dgating
            du_ref[at, :] = dupward
            gsum_ref[...] += jnp.sum(dgating.astype(F32), 0, keepdims=True)
            usum_ref[...] += jnp.sum(dupward.astype(F32), 0, keepdims=True)

    tall = pl.BlockSpec((length, block), lambda j: (0, j))
    flat = pl.BlockSpec((1, block), lambda j: (0, j))
    return pl.pallas_call(
        kernel,
        grid=(steps,),
        in_specs=[
            pl.BlockSpec((length, width), lambda j: (0, 0)),
            pl.BlockSpec((block, width), lambda j: (j, 0)),
            tall,
            pl.BlockSpec((length, block), lambda j: (0, steps + j)),
            flat,
            flat,
        ]
        + [UNREAD] * len(deps),
        out_specs=[tall, tall, flat, flat],
        out_shape=[jax.ShapeDtypeStruct((length, hidden), BF16)] * 2
        + [jax.ShapeDtypeStruct((1, hidden), F32)] * 2,
        scratch_shapes=[pltpu.VMEM((length, block), F32)],
        cost_estimate=COST,
        name="gate_back",
    )(grad, down_full, both, both, gbias[None], ubias[None], *deps)


def mixed_back(dres_low, out_full, retained, swish_pre, ggain, gshift, heads_here, places, deps):
    length, width = dres_low.shape
    value_width = out_full.shape[0]
    block, rows = value_width // heads_here, 128

    size = value_width // places.shape[0]
    chunks = block // size
    aligned = size % 128 == 0

    def kernel(place_ref, d_ref, w_ref, r_ref, s_ref, gain_ref, shift_ref, *rest):
        ds_ref, dr_ref, gsum_ref, ssum_ref, acc_ref, head_ref = rest[len(deps) :]
        if aligned:
            for k in range(chunks):
                at = pl.multiple_of(place_ref[pl.program_id(0) * chunks + k] * size, size)
                head_ref[k * size : (k + 1) * size, :] = w_ref[pl.ds(at, size), :]
            acc_ref[...] = dot(d_ref[...], head_ref[...], NT)
        else:
            acc_ref[...] = dot(d_ref[...], w_ref[...], NT)
        gsum_ref[...] = jnp.zeros_like(gsum_ref)
        ssum_ref[...] = jnp.zeros_like(ssum_ref)

        @pl.loop(0, length // rows)
        def _(i):
            at = pl.ds(pl.multiple_of(i * rows, rows), rows)
            dmixed = acc_ref[at, :]
            normed, factor, active = group_normalize(r_ref[at, :].astype(F32))
            swish = s_ref[at, :]
            sigma = jax.nn.sigmoid(swish)
            dgrouped = dmixed * (swish * sigma)
            grouped = normed * gain_ref[...] + shift_ref[...]
            ds_ref[at, :] = (dmixed * grouped * silu_slope(swish, sigma)).astype(BF16)
            gsum_ref[...] += jnp.sum(dgrouped * normed, 0, keepdims=True)
            ssum_ref[...] += jnp.sum(dgrouped, 0, keepdims=True)
            dr_ref[at, :] = normalize_back(dgrouped * gain_ref[...], normed, factor, active).astype(BF16)

    tall = pl.BlockSpec((length, block), lambda h: (0, h))
    flat = pl.BlockSpec((1, block), lambda h: (0, h))
    return pl.pallas_call(
        kernel,
        grid=(heads_here,),
        in_specs=[
            pl.BlockSpec(memory_space=pltpu.SMEM),
            pl.BlockSpec((length, width), lambda h: (0, 0)),
            pl.BlockSpec((value_width, width), lambda h: (0, 0))
            if aligned
            else pl.BlockSpec((block, width), lambda h: (h, 0)),
            tall,
            tall,
            flat,
            flat,
        ]
        + [UNREAD] * len(deps),
        out_specs=[tall, tall, flat, flat],
        out_shape=[jax.ShapeDtypeStruct((length, value_width), BF16)] * 2
        + [jax.ShapeDtypeStruct((1, value_width), F32)] * 2,
        scratch_shapes=[pltpu.VMEM((length, block), F32), pltpu.VMEM((block, width), BF16)],
        cost_estimate=COST,
        name="mixed_back",
    )(places, dres_low, out_full, retained, swish_pre, ggain[None], gshift[None], *deps)


def full_product(lefts, rights, dims, wide, deps):
    length = lefts[0].shape[0]
    step = min(wide, 512)
    specs = [pl.BlockSpec((length, left.shape[1]), lambda n: (0, 0)) for left in lefts]
    for left, (_, column) in zip(lefts, rights):
        depth = left.shape[1]
        if dims is NT:
            specs.append(pl.BlockSpec((step, depth), lambda n, c=column: (n, c)))
        else:
            specs.append(pl.BlockSpec((depth, step), lambda n: (0, n)))

    def kernel(*refs):
        total = dot(refs[0][...], refs[len(lefts)][...], dims)
        for k in range(1, len(lefts)):
            total += dot(refs[k][...], refs[len(lefts) + k][...], dims)
        refs[-1][...] = total.astype(BF16)

    return pl.pallas_call(
        kernel,
        grid=(wide // step,),
        in_specs=specs + [UNREAD] * len(deps),
        out_specs=pl.BlockSpec((length, step), lambda n: (0, n)),
        out_shape=jax.ShapeDtypeStruct((length, wide), BF16),
        cost_estimate=COST,
        name="full_product",
    )(*lefts, *[right for right, _ in rights], *deps)


class Ring:
    def __init__(self, size):
        half = size // 2
        self.size = size
        self.half = half
        self.order = list(range(half)) + list(range(size - 1, half - 1, -1))
        place = [0] * size
        for position, rank in enumerate(self.order):
            place[rank] = position
        self.right = [(self.order[i], self.order[(i + 1) % size]) for i in range(size)]
        self.left = [(self.order[i], self.order[(i - 1) % size]) for i in range(size)]
        self.me = lax.axis_index("sp")
        self.position = jnp.array(place, jnp.int32)[self.me]

    def rank(self, step):
        return jnp.array(self.order, jnp.int32)[lax.rem(self.position + step + self.size, self.size)]

    def ranks(self, *steps):
        return jnp.stack([self.rank(step) for step in steps])

    def to_right(self, block):
        return lax.ppermute(block, "sp", self.right)

    def to_left(self, block):
        return lax.ppermute(block, "sp", self.left)

    def pieces(self, block):
        middle = block.shape[0] // 2
        found = [(0, block)]
        from_left, from_right = block, block
        for step in range(1, self.half):
            from_left, from_right = self.to_right(from_left), self.to_left(from_right)
            found += [(-step, from_left), (step, from_right)]
        low = self.to_right(from_left[:middle])
        high = self.to_left(from_right[middle:])
        return found, low, high

    def gather(self, block, base=None):
        found, low, high = self.pieces(block)
        if base is None:
            out = jnp.zeros((self.size,) + block.shape, block.dtype)
        else:
            out = after(base, *[part for _, part in found]).reshape((self.size,) + block.shape)
        found.append((self.half, jnp.concatenate([low, high], 0)))
        for step, part in found:
            out = lax.dynamic_update_slice(out, part[None], (self.rank(step), 0, 0))
        return out.reshape(self.size * block.shape[0], block.shape[1])

    def gather_columns(self, pieces, outs, deps):
        found, low, high = pieces
        block = found[0][1]
        rows = block.shape[0]
        widths = [width for width, _ in outs]
        if any(chunk % 128 for _, chunk in outs):
            found.append((self.half, jnp.concatenate([low, high], 0)))
            whole = jnp.zeros((self.size,) + block.shape, block.dtype)
            for step, part in found:
                whole = lax.dynamic_update_slice(whole, part[None], (self.rank(step), 0, 0))
            results, start = [], 0
            for width, chunk in outs:
                share = whole[:, :, start : start + width].reshape(self.size, rows, -1, chunk)
                share = share.transpose(1, 2, 0, 3).reshape(rows, -1)
                results.append(share.astype(F32))
                start += width
            return results
        step_rows = min(64, rows // 2)
        steps = rows // step_rows
        middle = steps // 2
        size = self.size
        ranks = self.ranks(*[step for step, _ in found], self.half)

        def kernel(rank_ref, *refs):
            sources, out_refs = refs[: len(found) + 2], refs[len(found) + 2 + len(deps) :]

            def put(source, rank):
                start = 0
                for (width, chunk), out_ref in zip(outs, out_refs):
                    for k in range(width // chunk):
                        at = pl.multiple_of(k * size * chunk + rank * chunk, 128)
                        piece = source[:, start + k * chunk : start + (k + 1) * chunk]
                        out_ref[:, pl.ds(at, chunk)] = piece.astype(F32)
                    start += width

            for k in range(len(found)):
                put(sources[k], rank_ref[k])

            @pl.when(pl.program_id(0) < middle)
            def _():
                put(sources[-2], rank_ref[len(found)])

            @pl.when(pl.program_id(0) >= middle)
            def _():
                put(sources[-1], rank_ref[len(found)])

        total = block.shape[1]
        in_specs = [pl.BlockSpec((step_rows, total), lambda i, r: (i, 0)) for _ in found]
        in_specs.append(pl.BlockSpec((step_rows, total), lambda i, r: (jnp.minimum(i, middle - 1), 0)))
        in_specs.append(pl.BlockSpec((step_rows, total), lambda i, r: (jnp.maximum(i - middle, 0), 0)))
        return pl.pallas_call(
            kernel,
            grid_spec=pltpu.PrefetchScalarGridSpec(
                num_scalar_prefetch=1,
                grid=(steps,),
                in_specs=in_specs + [UNREAD] * len(deps),
                out_specs=[pl.BlockSpec((step_rows, size * width), lambda i, r: (i, 0)) for width in widths],
            ),
            out_shape=[jax.ShapeDtypeStruct((rows, size * width), F32) for width in widths],
            cost_estimate=COST,
            name="gather_columns",
        )(ranks, *[part for _, part in found], low, high, *deps)

    def gather_rows(self, pieces, deps):
        found, low, high = pieces
        rows, wide = found[0][1].shape
        step = min(wide, 512)
        parts = [part for _, part in found] + [low, high]
        ranks = self.ranks(*[place for place, _ in found], self.half)

        def kernel(rank_ref, *refs):
            out_ref = refs[-1]
            for k in range(len(found) + 2):
                size = parts[k].shape[0]
                at = rank_ref[min(k, len(found))] * rows
                if k == len(found) + 1:
                    at = at + rows - size
                out_ref[pl.ds(pl.multiple_of(at, size), size), :] = refs[k][...].astype(F32)

        return pl.pallas_call(
            kernel,
            grid_spec=pltpu.PrefetchScalarGridSpec(
                num_scalar_prefetch=1,
                grid=(wide // step,),
                in_specs=[pl.BlockSpec((part.shape[0], step), lambda n, r: (0, n)) for part in parts]
                + [UNREAD] * len(deps),
                out_specs=pl.BlockSpec((self.size * rows, step), lambda n, r: (0, n)),
            ),
            out_shape=jax.ShapeDtypeStruct((self.size * rows, wide), F32),
            cost_estimate=COST,
            name="gather_rows",
        )(ranks, *parts, *deps)

    def rows_of(self, terms, step):
        rows = terms.shape[0] // self.size
        return lax.dynamic_slice_in_dim(terms, self.rank(step) * rows, rows, 0)

    def sum_far(self, terms, *others):
        far = self.rows_of(terms, self.half)
        middle = far.shape[0] // 2
        low, high = far[:middle], far[middle:]
        if others:
            low, high = after(low, *others), after(high, *others)
        return (low, high), (self.to_right(low), self.to_left(high))

    def sum_near(self, terms, arrived, *others):
        from_left, from_right = arrived
        for step in range(self.half - 1, 0, -1):
            ahead = self.rows_of(terms, step).astype(F32)
            behind = self.rows_of(terms, -step).astype(F32)
            rows, part = ahead.shape[0], from_left.shape[0]
            ahead = ahead + jnp.pad(from_left.astype(F32), ((0, rows - part), (0, 0)))
            behind = behind + jnp.pad(from_right.astype(F32), ((rows - part, 0), (0, 0)))
            ahead, behind = ahead.astype(BF16), behind.astype(BF16)
            from_left, from_right = self.to_right(ahead), self.to_left(behind)
        return (ahead, behind), (from_left, from_right)

    def sum_own(self, terms, arrived):
        return self.rows_of(terms, 0).astype(F32) + arrived[0].astype(F32) + arrived[1].astype(F32)

    def scatter_sum(self, terms):
        return self.sum_own(terms, self.sum_near(terms, self.sum_far(terms)[1])[1])


class Line:
    def __init__(self, shards):
        self.shards = shards
        self.chips = shards // 2
        index = lax.axis_index("fsdp")
        self.core = lax.rem(index, 2)
        self.groups = [[2 * i + core for i in range(self.chips)] for core in range(2)]
        self.swap = [(i, i ^ 1) for i in range(shards)]

    def to_core(self, block):
        return lax.ppermute(block, "fsdp", self.swap)

    def half(self, left, rights, core, other, deps):
        length = left.shape[0]
        rows = left.shape[1] // self.shards
        wide = sum(right.shape[1] for right in rights)
        if rows % 128:
            columns = [
                lax.dynamic_slice_in_dim(left, (2 * i + core) * rows, rows, 1) for i in range(self.chips)
            ]
            left = after(jnp.concatenate(columns, 1), *deps)
            total = over_rows(left, jnp.concatenate(rights, 1))
            if other is not None:
                total = total + other.astype(F32)
            return total.astype(BF16)
        extra = [] if other is None else [other]

        def kernel(core_ref, x_ref, *refs):
            out_ref = refs[-1]
            start = 0
            for ref, right in zip(refs, rights):
                size = right.shape[1]
                total = dot(x_ref[...], ref[...], TN)
                if extra:
                    total += refs[len(rights)][:, start : start + size].astype(F32)
                out_ref[:, start : start + size] = total.astype(BF16)
                start += size

        return pl.pallas_call(
            kernel,
            grid_spec=pltpu.PrefetchScalarGridSpec(
                num_scalar_prefetch=1,
                grid=(self.chips,),
                in_specs=[pl.BlockSpec((length, rows), lambda i, c: (0, 2 * i + c[0]))]
                + [pl.BlockSpec((length, right.shape[1]), lambda i, c: (0, 0)) for right in rights]
                + [pl.BlockSpec((rows, wide), lambda i, c: (i, 0)) for _ in extra]
                + [UNREAD] * len(deps),
                out_specs=pl.BlockSpec((rows, wide), lambda i, c: (i, 0)),
            ),
            out_shape=jax.ShapeDtypeStruct((self.chips * rows, wide), BF16),
            cost_estimate=COST,
            name="rows_sum",
        )(core.reshape(1), left, *rights, *extra, *deps)

    def theirs(self, left, rights, deps):
        return self.half(left, rights, 1 - self.core, None, deps)

    def mine(self, left, rights, sent, deps):
        return self.half(left, rights, self.core, self.to_core(sent), deps)

    def scatter(self, block):
        return lax.psum_scatter(
            block, "fsdp", scatter_dimension=0, tiled=True, axis_index_groups=self.groups
        )


def butterfly(vector, axes=("fsdp", "sp")):
    for axis in axes:
        size = lax.axis_size(axis)
        step = 1
        while step < size:
            vector = vector + lax.ppermute(vector, axis, [(i, i ^ step) for i in range(size)])
            step *= 2
    return vector


class Spread:
    def __init__(self, shards, parts):
        chips = shards // 2
        assert chips == parts
        if parts == 4:
            moves = [[0, 2, 1, 3], [1, 3, 0, 2], [2, 0, 3, 1], [3, 1, 2, 0]]
        else:
            moves = [[(chip + rank) % chips for chip in range(chips)] for rank in range(parts)]
        self.along, self.across = [], []
        self.places = [[0] * shards for _ in range(parts)]
        self.pieces = [[0] * shards for _ in range(parts)]
        for rank, move in enumerate(moves):
            for chip, target in enumerate(move):
                for core in range(2):
                    middle = (2 * target + core) * parts + rank
                    self.along.append(((2 * chip + core) * parts + rank, middle))
                    self.across.append((middle, (2 * target + core) * parts + chip))
                    piece = core * parts + rank
                    self.places[chip][piece] = 2 * target + core
                    self.pieces[chip][2 * target + core] = piece

    def forth(self, block):
        block = lax.ppermute(block, ("fsdp", "sp"), self.along)
        return lax.ppermute(block, ("fsdp", "sp"), self.across)

    def back(self, block):
        block = lax.ppermute(block, ("fsdp", "sp"), [(there, here) for here, there in self.across])
        return lax.ppermute(block, ("fsdp", "sp"), [(there, here) for here, there in self.along])


def reorder(array, order, size, axis):
    chunks = [
        lax.dynamic_slice_in_dim(array, order[i] * size, size, axis)
        for i in range(array.shape[axis] // size)
    ]
    return jnp.concatenate(chunks, axis)


def local(
    tokens,
    attn_gain,
    attn_shift,
    query_weight,
    key_weight,
    value_weight,
    swish_weight,
    group_gain,
    group_shift,
    out_weight,
    ffn_gain,
    ffn_shift,
    gating_weight,
    upward_weight,
    gating_bias,
    upward_bias,
    downward_weight,
    downward_bias,
    cotangent,
):
    seq_count, local_len, width = tokens.shape
    assert seq_count == 1
    parts = lax.axis_size("sp")
    shards = lax.axis_size("fsdp")
    me = lax.axis_index("sp")
    ring = Ring(parts)
    line = Line(shards)
    heads_here = HEADS // parts
    full_len = local_len * parts
    value_all = value_weight.shape[1]
    hidden_all = gating_weight.shape[1]
    value_width = value_all // parts
    hidden_width = hidden_all // parts
    query_width = query_weight.shape[1] // parts
    third = 2 * query_width + value_width
    chunk = hidden_width // shards

    def columns(weight):
        size = weight.shape[1] // parts
        return lax.dynamic_slice_in_dim(weight, me * size, size, 1)

    def units(weight):
        pieces = [
            lax.dynamic_slice_in_dim(weight, (i * parts + me) * chunk, chunk, weight.ndim - 1)
            for i in range(shards)
        ]
        return jnp.concatenate(pieces, -1)

    def gathered(array):
        return lax.all_gather(array, "fsdp", axis=0, tiled=True)

    small = [
        attn_gain, attn_shift, group_gain, group_shift, ffn_gain, ffn_shift,
        gating_bias, upward_bias, downward_bias,
    ]
    sizes = [item.shape[0] for item in small]
    stacked = jnp.zeros((shards, sum(sizes)), BF16)
    stacked = lax.dynamic_update_slice(
        stacked, jnp.concatenate(small, 0)[None], (lax.axis_index("fsdp"), 0)
    )
    stacked = butterfly(stacked, ("fsdp",))
    offsets = [sum(sizes[:i]) for i in range(len(sizes))]
    (
        gain_one, shift_one, ggain_all, gshift_all, gain_two, shift_two, gbias_all, ubias_all, dbias,
    ) = (
        stacked[:, start : start + size].reshape(-1).astype(F32)
        for start, size in zip(offsets, sizes)
    )
    ggain = lax.dynamic_slice_in_dim(ggain_all, me * value_width, value_width, 0)
    gshift = lax.dynamic_slice_in_dim(gshift_all, me * value_width, value_width, 0)
    gbias = units(gbias_all)
    ubias = units(ubias_all)

    tokens_all = ring.gather(tokens.reshape(-1, width))
    flat = tokens.reshape(-1, width).astype(F32)
    first_norm, first_factor = normalize(flat)
    first = normalize(tokens_all.astype(F32))[0]
    first = (first * gain_one + shift_one).astype(BF16)
    grad_own = cotangent.reshape(-1, width)
    grad_low = ring.gather(after(grad_own, first))

    first_full = gathered(
        jnp.concatenate(
            [columns(query_weight), columns(key_weight), columns(value_weight), columns(swish_weight)], 1
        )
    )
    spread = Spread(shards, parts)
    places = jnp.array(spread.places, jnp.int32)[me]
    rows = out_weight.shape[0] // parts
    out_piece = spread.forth(lax.dynamic_slice_in_dim(out_weight, me * rows, rows, 0))
    out_full = gathered(after(out_piece, first))
    both_full = gathered(jnp.concatenate([units(gating_weight), units(upward_weight)], 1))
    down_full = gathered(lax.dynamic_slice_in_dim(downward_weight, me * rows, rows, 0))

    qkv, swish_pre = project(first, first_full, third)
    rates = decay_rates(me * heads_here + jnp.arange(heads_here))
    retained, mixed = retain_mix(qkv, swish_pre, rates, ggain, gshift, query_width, value_width, places)
    out_ordered = out_full
    if rows % 128:
        mixed = reorder(mixed, jnp.array(spread.pieces, jnp.int32)[me], rows, 1)
        out_ordered = reorder(out_full, places, rows, 0)
    mixed = after(mixed, grad_low)

    terms = full_product([mixed], [(out_full, 0)], NN, width, ())
    resid = flat + ring.scatter_sum(terms)
    spare = terms
    second_norm, second_factor = normalize(resid)
    second = ring.gather((second_norm * gain_two + shift_two).astype(BF16), tokens_all)
    both = product(second, both_full)
    hidden = (jax.nn.silu(both[:, :hidden_width] + gbias) * (both[:, hidden_width:] + ubias)).astype(BF16)

    sent = line.theirs(hidden, [grad_low], ())
    down_sum = line.mine(hidden, [grad_low], sent, ())
    down_share = line.scatter(down_sum)
    dgating, dupward, gbias_term, ubias_term = gate_back(
        grad_low, down_full, both, gbias, ubias, (down_sum,)
    )
    terms = full_product([dgating, dupward], [(both_full, 0), (both_full, 1)], NT, width, ())
    far, arrived = ring.sum_far(terms)
    sent = line.theirs(second, [dgating, dupward], far)
    arrived = lax.optimization_barrier(arrived + (down_share,))[:2]
    near, arrived = ring.sum_near(terms, arrived)
    both_sum = line.mine(second, [dgating, dupward], sent, near)
    both_share = line.scatter(both_sum)
    result = full_product([hidden], [(down_full, 0)], NN, width, (both_sum,))
    dsecond = ring.sum_own(after(terms, result), arrived)
    fgain_term = jnp.sum(dsecond * second_norm, 0)
    fshift_term = jnp.sum(dsecond, 0)
    grad_out = grad_own.astype(F32)
    dbias_term = jnp.sum(grad_out, 0)
    dresid = grad_out + normalize_back(dsecond * gain_two, second_norm, second_factor)

    dres_own = dresid.astype(BF16)
    dres_low = ring.gather(dres_own, spare)
    sent = line.theirs(mixed, [dres_low], ())
    far, result_far = ring.sum_far(result, dres_low)
    out_sum = line.mine(mixed, [dres_low], sent, far)
    out_share = line.scatter(out_sum)
    both_pieces = ring.pieces(after(both_share, out_sum))
    both_near = tuple(part for _, part in both_pieces[0])
    dswish, dretained, ggain_term, gshift_term = mixed_back(
        dres_low, out_ordered, retained, swish_pre, ggain, gshift, heads_here, places, (out_sum, both_share)
    )
    dquery, dkey, dvalue = retain_back(qkv, dretained, rates, query_width, value_width, ())
    result_far = lax.optimization_barrier(result_far + (dvalue,))[:2]
    near, result_near = ring.sum_near(result, result_far)
    sent = line.theirs(first, [dvalue, dswish], near + both_near)
    sent_qk = line.theirs(first, [dquery, dkey], (sent, out_share))
    out_share = spread.back(out_share)
    vs_sum = line.mine(first, [dvalue, dswish], sent, (sent_qk, out_share))
    vs_share = line.scatter(vs_sum)
    rights = [(first_full, 0), (first_full, 1), (first_full, 2 * query_width // value_width)]
    rights.append((first_full, third // value_width))
    terms = full_product([dquery, dkey, dvalue, dswish], rights, NT, width, (vs_sum,))
    far, arrived = ring.sum_far(terms)
    down_pieces = ring.pieces(after(down_share, sent))
    qk_sum = line.mine(first, [dquery, dkey], sent_qk, far)
    qk_share = line.scatter(qk_sum)
    result = ring.sum_own(after(result, qk_sum), result_near)
    layer_out = (resid + result + dbias).astype(BF16)
    arrived = lax.optimization_barrier(arrived + (layer_out,))[:2]
    near, arrived = ring.sum_near(terms, arrived)
    gating_grad, upward_grad = ring.gather_columns(
        both_pieces, [(hidden_width, chunk), (hidden_width, chunk)], near
    )
    dfirst = ring.sum_own(after(terms, gating_grad), arrived)
    again_term = jnp.sum(dfirst * first_norm, 0)
    ashift_term = jnp.sum(dfirst, 0)
    input_grad = dresid + normalize_back(dfirst * gain_one, first_norm, first_factor)

    downward_grad = ring.gather_rows(down_pieces, (dfirst,))
    out_grad = ring.gather_rows(ring.pieces(after(out_share, *near)), (downward_grad,))
    vs_pieces = ring.pieces(vs_share)
    value_grad, swish_grad = ring.gather_columns(
        vs_pieces, [(value_width, value_width), (value_width, value_width)], ()
    )
    query_grad, key_grad = ring.gather_columns(
        ring.pieces(qk_share), [(query_width, query_width), (query_width, query_width)], (value_grad,)
    )

    def placed(term, whole):
        return lax.dynamic_update_slice(jnp.zeros((whole,), F32), term, (me * term.shape[0],))

    def placed_units(term):
        blank = jnp.zeros((shards, parts, chunk), F32)
        return lax.dynamic_update_slice(blank, term.reshape(shards, 1, chunk), (0, me, 0)).reshape(-1)

    terms = [
        again_term, ashift_term, placed(ggain_term[0], value_all), placed(gshift_term[0], value_all),
        fgain_term, fshift_term, placed_units(gbias_term[0]), placed_units(ubias_term[0]), dbias_term,
    ]
    terms = jnp.concatenate([term.reshape(shards, -1) for term in terms], 1)
    totals = butterfly(after(butterfly(after(terms, *[part for _, part in vs_pieces[0]]), ("fsdp",)), qk_share), ("sp",))
    mine = lax.dynamic_slice_in_dim(totals, lax.axis_index("fsdp"), 1, 0)[0]
    (
        again_grad, ashift_grad, ggain_grad, gshift_grad, fgain_grad, fshift_grad,
        gbias_grad, ubias_grad, dbias_grad,
    ) = (mine[start : start + size] for start, size in zip(offsets, sizes))
    return (
        layer_out.reshape(seq_count, local_len, width),
        input_grad.reshape(seq_count, local_len, width),
        again_grad,
        ashift_grad,
        query_grad,
        key_grad,
        value_grad,
        swish_grad,
        ggain_grad,
        gshift_grad,
        out_grad,
        fgain_grad,
        fshift_grad,
        gating_grad,
        upward_grad,
        gbias_grad,
        ubias_grad,
        downward_grad,
        dbias_grad,
    )


def solution(mesh):
    row, vector, cube = P("fsdp", None), P("fsdp"), P("fsdp", "sp", None)
    return jax.shard_map(
        local,
        mesh=mesh,
        in_specs=(
            cube, vector, vector, row, row, row, row, vector, vector, row,
            vector, vector, row, row, vector, vector, row, vector, cube,
        ),
        out_specs=(
            cube, cube, vector, vector, row, row, row, row, vector, vector,
            row, vector, vector, row, row, vector, vector, row, vector,
        ),
        check_vma=False,
    )
```

time: 887 us -> 789 us (0.89)
  Pallas kernels: 0 us -> 226 us
  matrix products: 186 us -> 12.6 us
  local copies, waits for them, and re-layouts: 153 us -> 82.8 us
  blocking collectives: 57.9 us -> 0 us
  waiting for transfers between devices: 289 us -> 272 us
    pallas_call x0 -> x24, Pallas kernels: none -> 226 us  [the longest x10 76 us: half(): pl.pallas_call(kernel, grid_spec=pltpu.PrefetchScalarGridSpec(num_scalar_...]
    dot_general x36 -> x1, matrix products: 186 us -> 12.6 us  [dot(): return lax.dot_general(left, right, dims, preferred_element_type=F32)]
    ppermute x26, waiting for transfers between devices: 37.3 us -> 173 us  [to_right(): return lax.ppermute(block, 'sp', self.right)]
    ppermute x26, waiting for transfers between devices: 176 us -> 44.2 us  [to_left(): return lax.ppermute(block, 'sp', self.left)]
    all_gather x1 -> x0, blocking collectives: 57.9 us -> none  [gathered(): return lax.all_gather(array, 'fsdp', axis=0, tiled=True)]
    ppermute x26, starting transfers between devices: 58.1 us -> 20.8 us  [to_left(): return lax.ppermute(block, 'sp', self.left)]
    reduce_scatter x5, waiting for transfers between devices: 32 us -> 0.01 us  [scatter(): lax.psum_scatter(block, 'fsdp', scatter_dimension=0, tiled=True, axis_ind...]
    unnamed x215 -> x127, local copies, waits for them, and re-layouts: 44.3 us -> 21.3 us
  transfers between devices with their start and end apart: 69 -> 78, of which waited for: 35 -> 34; matrix products, arithmetic and copies ran while one was open for 41% -> 18% of each run, Pallas kernels for 0% -> 27%
where the time goes in v2:
time: 789 us; the launch traced here: 778 us
  waiting for transfers between devices  272 us (34%)
  Pallas kernels  226 us (29%)
  starting transfers between devices  97.3 us (12%)
  local copies, waits for them, and re-layouts  82.8 us (10%)
  other arithmetic  58.8 us (7%)
  between operations  28 us (4%)
  matrix products  12.6 us (2%)
    ppermute x26, waiting for transfers between devices, to_right(): return lax.ppermute(block, 'sp', self.right)  173 us
    pallas_call x10, Pallas kernels, half(): pl.pallas_call(kernel, grid_spec=pltpu.PrefetchScalarGridSpec(num_scalar_...  76 us
    ppermute x26, starting transfers between devices, to_right(): return lax.ppermute(block, 'sp', self.right)  51.2 us
    pallas_call x4, Pallas kernels, full_product(): pl.pallas_call(kernel, grid=(wide // step,), in_specs=specs + [UNREAD] *...  49.1 us
    ppermute x26, waiting for transfers between devices, to_left(): return lax.ppermute(block, 'sp', self.left)  44.2 us
    ppermute x8, waiting for transfers between devices, butterfly(): lax.ppermute(vector, axis, [(i, i ^ step) for i in range(size)])  34.6 us
    unnamed x127, local copies, waits for them, and re-layouts  21.3 us
    ppermute x26, starting transfers between devices, to_left(): return lax.ppermute(block, 'sp', self.left)  20.8 us
  transfers between devices with their start and end apart: 78, of which 34 were waited for; matrix products, arithmetic and copies ran while one was open for 18% of the time, Pallas kernels for 27%

profile of v2, /device:TPU:0, one launch (start us, length us, event | category | flops | bytes accessed | tf_op | source)
XLA Modules:
  0.0 777.7 jit_solution(7219987187348227981)
XLA Ops:
  40.4 29.7 %collective-permute-done.6 = bf16[8,3328]{1,0:T(8,128)(2,1)S(1)} collective-permute-done((bf16[8,3328]{1,0:T(8,128)(2,1)S(1)}, bf16[8,3328]{1,0:T(8,128)(2,1)S(1)}, u32[]{:S(2)}, u32[]{:S(2)}) %collective-permute-start.6) | collective-permute-done | bytes 53280 | tf_op jit(solution)/shard_map/ppermute | solution.py:612
  122.1 13.9 %collective-permute-done.8 = bf16[256,2048]{1,0:T(8,128)(2,1)S(1)} collective-permute-done((bf16[256,2048]{1,0:T(8,128)(2,1)S(1)}, bf16[256,2048]{1,0:T(8,128)(2,1)S(1)}, u32[]{:S(2)}, u32[]{:S(2)}) %collective-permute-start.8) | collective-permute-done | bytes 1048608 | tf_op jit(solution)/shard_map/ppermute | solution.py:393
  149.2 19.6 %project.1 = (bf16[1024,2048]{1,0:T(8,128)(2,1)}, f32[1024,1024]{1,0:T(8,128)}) custom-call(bf16[1024,2048]{1,0:T(8,128)(2,1)} %add_convert_fusion.x_ref, bf16[2048,3072]{1,0:T(8,128)(2,1)} %all-gather.5.cloned.1.call-done.w_ref.refs_4_.refs_5_.refs_6_.refs_7_), custom_call_target="tpu_custom_call" | custom-call | flops 1024 | bytes 1024 | tf_op jit(solution)/shard_map/project/pallas_call | solution.py:95
  168.9 9.0 %retain_mix.1 = (bf16[1024,1024]{1,0:T(8,128)(2,1)}, bf16[1024,1024]{1,0:T(8,128)(2,1)}) custom-call(f32[2]{0:T(128)} %subtract_log_fusion.rate_ref, s32[8]{0:T(128)} %fusion.22.place_ref, bf16[1024,2048]{1,0:T(8,128)(2,1)} %get-tuple-element.61.q_ref.k_ref.v_ref, bf16[1024,2048]{1,0:T(8,128)(2,1)} %get-tuple-element.61.q_ref.k_ref.v_ref, ...), custom_call_target="tpu_custom_call" | custom-call | flops 1024 | bytes 1024 | tf_op jit(solution)/shard_map/retain_mix/pallas_call | solution.py:155
  177.9 13.8 %all-gather.7.cloned.1.call-done.refs_1_.w_ref = bf16[1024,2048]{1,0:T(8,128)(2,1)} async-done(((bf16[128,2048]{1,0:T(8,128)(2,1)}), bf16[1024,2048]{1,0:T(8,128)(2,1)}) %all-gather.7.cloned.1.call-update) | async-done | bytes 4194320 | tf_op jit(solution)/shard_map/all_gather | solution.py:705
  191.7 8.3 %full_product.4 = bf16[1024,2048]{1,0:T(8,128)(2,1)} custom-call(bf16[1024,1024]{1,0:T(8,128)(2,1)} %get-tuple-element.65.refs_0_.x_ref, bf16[1024,2048]{1,0:T(8,128)(2,1)} %all-gather.7.cloned.1.call-done.refs_1_.w_ref), custom_call_target="tpu_custom_call" | custom-call | flops 1024 | bytes 1024 | tf_op jit(solution)/shard_map/full_product/pallas_call | solution.py:358
  204.8 10.8 %collective-permute-done.13 = bf16[128,2048]{1,0:T(8,128)(2,1)S(1)} collective-permute-done((bf16[128,2048]{1,0:T(8,128)(2,1)S(1)}, bf16[128,2048]{1,0:T(8,128)(2,1)S(1)}, u32[]{:S(2)}, u32[]{:S(2)}) %collective-permute-start.13) | collective-permute-done | bytes 524320 | tf_op jit(solution)/shard_map/ppermute | solution.py:390
  225.7 19.0 %collective-permute-done.14 = bf16[256,2048]{1,0:T(8,128)(2,1)S(1)} collective-permute-done((bf16[256,2048]{1,0:T(8,128)(2,1)}, bf16[256,2048]{1,0:T(8,128)(2,1)S(1)}, u32[]{:S(2)}, u32[]{:S(2)}) %collective-permute-start.14) | collective-permute-done | bytes 1048608 | tf_op jit(solution)/shard_map/ppermute | solution.py:390
  252.4 20.5 %collective-permute-done.17 = bf16[256,2048]{1,0:T(8,128)(2,1)S(1)} collective-permute-done((bf16[256,2048]{1,0:T(8,128)(2,1)S(1)}, bf16[256,2048]{1,0:T(8,128)(2,1)S(1)}, u32[]{:S(2)}, u32[]{:S(2)}) %collective-permute-start.17) | collective-permute-done | bytes 1048608 | tf_op jit(solution)/shard_map/ppermute | solution.py:390
  288.6 12.6 %fusion.29.gate_ref.up_ref = f32[1024,2048]{1,0:T(8,128)S(1)} fusion(bf16[1024,2048]{1,0:T(8,128)(2,1)} %bitcast.31.x_ref, bf16[2048,2048]{1,0:T(8,128)(2,1)} %all-gather.9.cloned.1.call-done.refs_2_.refs_3_), kind=kOutput, calls=%fused_computation.157 | convolution fusion | flops 8589934592 | bytes 20971520 | tf_op jit(solution)/shard_map/dot_general | solution.py:22
  316.3 6.9 rows_sum.11.rest_0_
  323.3 13.3 %gate_back.1 = (bf16[1024,1024]{1,0:T(8,128)(2,1)}, bf16[1024,1024]{1,0:T(8,128)(2,1)}, f32[1,1024]{1,0:T(1,128)}, f32[1,1024]{1,0:T(1,128)}) custom-call(bf16[1024,2048]{1,0:T(8,128)(2,1)} %bitcast.21.refs_0_.g_ref, bf16[1024,2048]{1,0:T(8,128)(2,1)} %all-gather.11.cloned.1.call-done.w_ref.refs_1_, f32[1024,2048]{1,0:T(8,128)} %copy-done.2, ...), custom_call_target="tpu_custom_call" | custom-call | flops 1024 | bytes 1024 | tf_op jit(solution)/shard_map/gate_back/pallas_call | solution.py:259
  336.6 13.4 %full_product.5 = bf16[1024,2048]{1,0:T(8,128)(2,1)} custom-call(bf16[1024,1024]{1,0:T(8,128)(2,1)} %get-tuple-element.68.refs_0_, bf16[1024,1024]{1,0:T(8,128)(2,1)} %get-tuple-element.69.refs_1_, bf16[2048,2048]{1,0:T(8,128)(2,1)} %all-gather.9.cloned.1.call-done.refs_2_.refs_3_, bf16[2048,2048]{1,0:T(8,128)(2,1)} %all-gather.9.cloned.1.call-done.refs_2_.refs_3_), custom_call_target="tpu_custom_call" | custom-call | flops 1024 | bytes 1024 | tf_op jit(solution)/shard_map/full_product/pallas_call | solution.py:358
  352.3 8.8 %rows_sum.12 = bf16[1024,2048]{1,0:T(8,128)(2,1)} custom-call(s32[1]{0:T(128)} %bitcast.35.core_ref, bf16[1024,2048]{1,0:T(8,128)(2,1)} %bitcast.31.x_ref, bf16[1024,1024]{1,0:T(8,128)(2,1)} %get-tuple-element.68.refs_0_, bf16[1024,1024]{1,0:T(8,128)(2,1)} %get-tuple-element.69.refs_1_, bf16[128,2048]{1,0:T(8,128)(2,1)} %get-tuple-element.128.refs_2_, ...), custom_call_target="tpu_custom_call" | custom-call | flops 1024 | bytes 1024 | tf_op jit(solution)/shard_map/rows_sum/pallas_call | solution.py:579
  363.4 12.4 %collective-permute-done.23 = bf16[128,2048]{1,0:T(8,128)(2,1)} collective-permute-done((bf16[128,2048]{1,0:T(8,128)(2,1)}, bf16[128,2048]{1,0:T(8,128)(2,1)}, u32[]{:S(2)}, u32[]{:S(2)}) %collective-permute-start.23) | collective-permute-done | bytes 524320 | tf_op jit(solution)/shard_map/ppermute | solution.py:390
  379.9 9.5 %rows_sum.13.refs_2_ = bf16[1024,2048]{1,0:T(8,128)(2,1)} custom-call(s32[1]{0:T(128)} %bitcast.32.core_ref, bf16[1024,2048]{1,0:T(8,128)(2,1)} %bitcast.31.x_ref, bf16[1024,1024]{1,0:T(8,128)(2,1)} %get-tuple-element.68.refs_0_, bf16[1024,1024]{1,0:T(8,128)(2,1)} %get-tuple-element.69.refs_1_, bf16[1024,2048]{1,0:T(8,128)(2,1)} %collective-permute-done.22.refs_2_, ...), custom_call_target="tpu_custom_call" | custom-call | flops 1024 | bytes 1024 | tf_op jit(solution)/shard_map/rows_sum/pallas_call | solution.py:579
  391.7 8.5 %full_product.6 = bf16[1024,2048]{1,0:T(8,128)(2,1)} custom-call(bf16[1024,1024]{1,0:T(8,128)(2,1)} %fusion.3.x_ref.refs_0_, bf16[1024,2048]{1,0:T(8,128)(2,1)} %all-gather.11.cloned.1.call-done.w_ref.refs_1_, bf16[1024,2048]{1,0:T(8,128)(2,1)} %rows_sum.13.refs_2_), custom_call_target="tpu_custom_call" | custom-call | flops 1024 | bytes 1024 | tf_op jit(solution)/shard_map/full_product/pallas_call | solution.py:358
  400.2 14.0 %collective-permute-done.25 = bf16[256,2048]{1,0:T(8,128)(2,1)} collective-permute-done((bf16[256,2048]{1,0:T(8,128)(2,1)}, bf16[256,2048]{1,0:T(8,128)(2,1)}, u32[]{:S(2)}, u32[]{:S(2)}) %collective-permute-start.25) | collective-permute-done | bytes 1048608 | tf_op jit(solution)/shard_map/ppermute | solution.py:390
  422.3 21.1 %collective-permute-done.27 = bf16[256,2048]{1,0:T(8,128)(2,1)S(1)} collective-permute-done((bf16[256,2048]{1,0:T(8,128)(2,1)S(1)}, bf16[256,2048]{1,0:T(8,128)(2,1)S(1)}, u32[]{:S(2)}, u32[]{:S(2)}) %collective-permute-start.27) | collective-permute-done | bytes 1048608 | tf_op jit(solution)/shard_map/ppermute | solution.py:390
  468.2 6.9 rows_sum.15.rest_0_
  479.2 17.5 %mixed_back.1 = (bf16[1024,1024]{1,0:T(8,128)(2,1)}, bf16[1024,1024]{1,0:T(8,128)(2,1)}, f32[1,1024]{1,0:T(1,128)}, f32[1,1024]{1,0:T(1,128)}) custom-call(s32[8]{0:T(128)} %fusion.22.place_ref, bf16[1024,2048]{1,0:T(8,128)(2,1)} %bitcast.41.refs_0_.d_ref, bf16[1024,2048]{1,0:T(8,128)(2,1)} %all-gather.7.cloned.1.call-done.refs_1_.w_ref, ...), custom_call_target="tpu_custom_call" | custom-call | flops 1024 | bytes 1024 | tf_op jit(solution)/shard_map/mixed_back/pallas_call | solution.py:317
  496.8 12.7 %retain_back.1 = (bf16[1024,512]{1,0:T(8,128)(2,1)}, bf16[1024,512]{1,0:T(8,128)(2,1)}, bf16[1024,1024]{1,0:T(8,128)(2,1)}) custom-call(f32[2]{0:T(128)} %subtract_log_fusion.rate_ref, bf16[1024,2048]{1,0:T(8,128)(2,1)} %get-tuple-element.61.q_ref.k_ref.v_ref, bf16[1024,2048]{1,0:T(8,128)(2,1)} %get-tuple-element.61.q_ref.k_ref.v_ref, ...), custom_call_target="tpu_custom_call" | custom-call | flops 1024 | bytes 1024 | tf_op jit(solution)/shard_map/retain_back/pallas_call | solution.py:209
  516.7 8.8 %rows_sum.16.refs_2_ = bf16[1024,2048]{1,0:T(8,128)(2,1)} custom-call(s32[1]{0:T(128)} %bitcast.35.core_ref, bf16[1024,2048]{1,0:T(8,128)(2,1)} %add_convert_fusion.x_ref, bf16[1024,1024]{1,0:T(8,128)(2,1)} %get-tuple-element.80.refs_0_.refs_2_, bf16[1024,1024]{1,0:T(8,128)(2,1)} %get-tuple-element.81.refs_1_.refs_3_, ...), custom_call_target="tpu_custom_call" | custom-call | flops 1024 | bytes 1024 | tf_op jit(solution)/shard_map/rows_sum/pallas_call | solution.py:579
  542.3 9.5 %rows_sum.18.refs_8_ = bf16[1024,2048]{1,0:T(8,128)(2,1)} custom-call(s32[1]{0:T(128)} %bitcast.32.core_ref, bf16[1024,2048]{1,0:T(8,128)(2,1)} %add_convert_fusion.x_ref, bf16[1024,1024]{1,0:T(8,128)(2,1)} %get-tuple-element.80.refs_0_.refs_2_, bf16[1024,1024]{1,0:T(8,128)(2,1)} %get-tuple-element.81.refs_1_.refs_3_, ...), custom_call_target="tpu_custom_call" | custom-call | flops 1024 | bytes 1024 | tf_op jit(solution)/shard_map/rows_sum/pallas_call | solution.py:579
  552.4 16.5 %collective-permute-start.40 = (bf16[256,2048]{1,0:T(8,128)(2,1)}, bf16[256,2048]{1,0:T(8,128)(2,1)}, u32[]{:S(2)}, u32[]{:S(2)}) collective-permute-start(bf16[256,2048]{1,0:T(8,128)(2,1)} %get-tuple-element.121.refs_2_), channel_id=1, source_target_pairs={{0,1},{1,3},{3,2},{2,0},{4,5},{5,7},{7,6},{6,4},{8,9},{9,11},{11,1... | collective-permute-start | bytes 3145736 | tf_op jit(solution)/shard_map/ppermute | solution.py:390
  570.0 18.8 %full_product.7 = bf16[1024,2048]{1,0:T(8,128)(2,1)} custom-call(bf16[1024,512]{1,0:T(8,128)(2,1)} %get-tuple-element.78.refs_0_, bf16[1024,512]{1,0:T(8,128)(2,1)} %get-tuple-element.79.refs_1_, bf16[1024,1024]{1,0:T(8,128)(2,1)} %get-tuple-element.80.refs_0_.refs_2_, bf16[1024,1024]{1,0:T(8,128)(2,1)} %get-tuple-element.81.refs_1_.refs_3_, ...), custom_call_target="tpu_custom_call" | custom-call | flops 1024 | bytes 1024 | tf_op jit(solution)/shard_map/full_product/pallas_call | solution.py:358
  605.2 8.5 %collective-permute-done.44 = bf16[128,2048]{1,0:T(8,128)(2,1)S(1)} collective-permute-done((bf16[128,2048]{1,0:T(8,128)(2,1)}, bf16[128,2048]{1,0:T(8,128)(2,1)S(1)}, u32[]{:S(2)}, u32[]{:S(2)}) %collective-permute-start.44) | collective-permute-done | bytes 524320 | tf_op jit(solution)/shard_map/ppermute | solution.py:390
  629.5 23.9 %collective-permute-done.42.refs_3_ = bf16[128,2048]{1,0:T(8,128)(2,1)} collective-permute-done((bf16[128,2048]{1,0:T(8,128)(2,1)}, bf16[128,2048]{1,0:T(8,128)(2,1)}, u32[]{:S(2)}, u32[]{:S(2)}) %collective-permute-start.42) | collective-permute-done | bytes 524320 | tf_op jit(solution)/shard_map/ppermute | solution.py:390
  653.7 7.2 gather_columns.3
  669.2 27.1 %collective-permute-done.48.refs_1_ = bf16[256,2048]{1,0:T(8,128)(2,1)S(1)} collective-permute-done((bf16[256,2048]{1,0:T(8,128)(2,1)}, bf16[256,2048]{1,0:T(8,128)(2,1)S(1)}, u32[]{:S(2)}, u32[]{:S(2)}) %collective-permute-start.48) | collective-permute-done | bytes 1048608 | tf_op jit(solution)/shard_map/ppermute | solution.py:390
  717.5 12.3 %collective-permute-done.68.refs_4_ = bf16[64,2048]{1,0:T(8,128)(2,1)} collective-permute-done((bf16[64,2048]{1,0:T(8,128)(2,1)S(1)}, bf16[64,2048]{1,0:T(8,128)(2,1)}, u32[]{:S(2)}, u32[]{:S(2)}) %collective-permute-start.68) | collective-permute-done | bytes 262176 | tf_op jit(solution)/shard_map/ppermute | solution.py:393
  757.8 6.8 gather_columns.4
  (403 shorter events, 307.9 us)
Async XLA Ops:
  7.2 142.0 %all-gather.5.cloned.1.call-start = ((), (), s32[]{:S(2)}) async-start(), calls=%async_computation.5 | async-start | bytes 14155776 | tf_op jit(solution)/shard_map/all_gather | solution.py:705
  11.2 180.5 %all-gather.7.cloned.1.call-start = ((), (), s32[]{:S(2)}) async-start(), calls=%async_computation.6 | async-start | bytes 4718592 | tf_op jit(solution)/shard_map/all_gather | solution.py:705
  13.8 58.6 %collective-permute-start = (bf16[256,2048]{1,0:T(8,128)(2,1)S(1)}, bf16[256,2048]{1,0:T(8,128)(2,1)}, u32[]{:S(2)}, u32[]{:S(2)}) collective-permute-start(bf16[256,2048]{1,0:T(8,128)(2,1)S(1)} %bitcast.132), channel_id=1, source_target_pairs={{0,1},{1,3},{3,2},{2,0},{4,5},{5,7},{7,6},{6,4},{8,9},{9,11},{11,1... | collective-permute-start | bytes 3145736 | tf_op jit(solution)/shard_map/ppermute | solution.py:390
  16.4 57.2 %collective-permute-start.1 = (bf16[256,2048]{1,0:T(8,128)(2,1)S(1)}, bf16[256,2048]{1,0:T(8,128)(2,1)}, u32[]{:S(2)}, u32[]{:S(2)}) collective-permute-start(bf16[256,2048]{1,0:T(8,128)(2,1)S(1)} %bitcast.133), channel_id=1, source_target_pairs={{0,2},{1,0},{3,1},{2,3},{4,6},{5,4},{7,5},{6,7},{8,10},{9,8},{11,9... | collective-permute-start | bytes 3145736 | tf_op jit(solution)/shard_map/ppermute | solution.py:393
  19.6 51.1 %collective-permute-start.11 = (bf16[128,2048]{1,0:T(8,128)(2,1)}, bf16[128,2048]{1,0:T(8,128)(2,1)}, u32[]{:S(2)}, u32[]{:S(2)}) collective-permute-start(bf16[128,2048]{1,0:T(8,128)(2,1)} %constant_dynamic-slice_fusion.10), channel_id=1, source_target_pairs={{0,0},{4,4},{8,16},{12,20},{16,8},{20,12},{24,24},{28,28},{1,9},{5... | collective-permute-start | bytes 1572872 | tf_op jit(solution)/shard_map/ppermute | solution.py:639
  30.8 39.2 %collective-permute-start.6 = (bf16[8,3328]{1,0:T(8,128)(2,1)S(1)}, bf16[8,3328]{1,0:T(8,128)(2,1)S(1)}, u32[]{:S(2)}, u32[]{:S(2)}) collective-permute-start(bf16[8,3328]{1,0:T(8,128)(2,1)S(1)} %add.294), channel_id=1, source_target_pairs={{0,16},{4,20},{8,24},{12,28},{16,0},{20,4},{24,8},{28,12},{1,17},{... | collective-permute-start | bytes 159752 | tf_op jit(solution)/shard_map/ppermute | solution.py:612
  97.8 190.8 %all-gather.9.cloned.1.call-start = ((), (), s32[]{:S(2)}) async-start(), calls=%async_computation.7 | async-start | bytes 9437184 | tf_op jit(solution)/shard_map/all_gather | solution.py:705
  112.8 210.5 %all-gather.11.cloned.1.call-start = ((), (), s32[]{:S(2)}) async-start(), calls=%async_computation.8 | async-start | bytes 4718592 | tf_op jit(solution)/shard_map/all_gather | solution.py:705
  224.3 151.9 %reduce-scatter.6.cloned.1.call-start = ((), (), s32[]{:S(2)}) async-start(), calls=%async_computation.9 | async-start | bytes 2621440 | tf_op jit(solution)/shard_map/reduce_scatter | solution.py:602
  323.2 151.8 %reduce-scatter.8.cloned.1.call-start = ((), (), s32[]{:S(2)}) async-start(), calls=%async_computation.10 | async-start | bytes 5242880 | tf_op jit(solution)/shard_map/reduce_scatter | solution.py:602
  389.4 136.0 %reduce-scatter.10.cloned.1.call-start = ((), (), s32[]{:S(2)}) async-start(), calls=%async_computation.11 | async-start | bytes 2621440 | tf_op jit(solution)/shard_map/reduce_scatter | solution.py:602
  475.1 41.6 %collective-permute-start.34 = (bf16[256,2048]{1,0:T(8,128)(2,1)}, bf16[256,2048]{1,0:T(8,128)(2,1)}, u32[]{:S(2)}, u32[]{:S(2)}) collective-permute-start(bf16[256,2048]{1,0:T(8,128)(2,1)} %reduce-scatter.8.cloned.1.call-done.rest_1_.refs_4_.refs_0_), channel_id=1, source_target_pairs={{0,1},{1,3},{3,2},{2,0},{4,5},{5,7},{7,6},{6,4},{8,9},{9,11},{11,1... | collective-permute-start | bytes 3145736 | tf_op jit(solution)/shard_map/ppermute | solution.py:390
  476.4 40.3 %collective-permute-start.35 = (bf16[256,2048]{1,0:T(8,128)(2,1)}, bf16[256,2048]{1,0:T(8,128)(2,1)}, u32[]{:S(2)}, u32[]{:S(2)}) collective-permute-start(bf16[256,2048]{1,0:T(8,128)(2,1)} %reduce-scatter.8.cloned.1.call-done.rest_1_.refs_4_.refs_0_), channel_id=1, source_target_pairs={{0,2},{1,0},{3,1},{2,3},{4,6},{5,4},{7,5},{6,7},{8,10},{9,8},{11,9... | collective-permute-start | bytes 3145736 | tf_op jit(solution)/shard_map/ppermute | solution.py:393
  477.1 185.5 %reduce-scatter.12.cloned.1.call-start = ((), (), s32[]{:S(2)}) async-start(), calls=%async_computation.12 | async-start | bytes 5242880 | tf_op jit(solution)/shard_map/reduce_scatter | solution.py:602
  477.2 35.7 %collective-permute-start.33 = (bf16[128,2048]{1,0:T(8,128)(2,1)}, bf16[128,2048]{1,0:T(8,128)(2,1)}, u32[]{:S(2)}, u32[]{:S(2)}) collective-permute-start(bf16[128,2048]{1,0:T(8,128)(2,1)} %get-tuple-element.76.refs_3_), channel_id=1, source_target_pairs={{0,2},{1,0},{3,1},{2,3},{4,6},{5,4},{7,5},{6,7},{8,10},{9,8},{11,9... | collective-permute-start | bytes 1572872 | tf_op jit(solution)/shard_map/ppermute | solution.py:393
  478.1 34.8 %collective-permute-start.32 = (bf16[128,2048]{1,0:T(8,128)(2,1)}, bf16[128,2048]{1,0:T(8,128)(2,1)}, u32[]{:S(2)}, u32[]{:S(2)}) collective-permute-start(bf16[128,2048]{1,0:T(8,128)(2,1)} %get-tuple-element.75.refs_2_), channel_id=1, source_target_pairs={{0,1},{1,3},{3,2},{2,0},{4,5},{5,7},{7,6},{6,4},{8,9},{9,11},{11,1... | collective-permute-start | bytes 1572872 | tf_op jit(solution)/shard_map/ppermute | solution.py:390
  551.8 155.8 %reduce-scatter.14.cloned.1.call-start = ((), (), s32[]{:S(2)}) async-start(), calls=%async_computation.13 | async-start | bytes 2621440 | tf_op jit(solution)/shard_map/reduce_scatter | solution.py:602
  551.8 39.3 %collective-permute-start.36 = (bf16[1024,1024]{1,0:T(8,128)(2,1)}, bf16[1024,1024]{1,0:T(8,128)(2,1)}, u32[]{:S(2)}, u32[]{:S(2)}) collective-permute-start(bf16[1024,1024]{1,0:T(8,128)(2,1)} %rows_sum.17.refs_3_), channel_id=1, source_target_pairs={{0,4},{4,0},{8,12},{12,8},{16,20},{20,16},{24,28},{28,24},{1,5},{5... | collective-permute-start | bytes 6291464 | tf_op jit(solution)/shard_map/ppermute | solution.py:551
  552.4 49.1 %collective-permute-start.40 = (bf16[256,2048]{1,0:T(8,128)(2,1)}, bf16[256,2048]{1,0:T(8,128)(2,1)}, u32[]{:S(2)}, u32[]{:S(2)}) collective-permute-start(bf16[256,2048]{1,0:T(8,128)(2,1)} %get-tuple-element.121.refs_2_), channel_id=1, source_target_pairs={{0,1},{1,3},{3,2},{2,0},{4,5},{5,7},{7,6},{6,4},{8,9},{9,11},{11,1... | collective-permute-start | bytes 3145736 | tf_op jit(solution)/shard_map/ppermute | solution.py:390
  568.9 32.6 %collective-permute-start.41 = (bf16[256,2048]{1,0:T(8,128)(2,1)}, bf16[256,2048]{1,0:T(8,128)(2,1)}, u32[]{:S(2)}, u32[]{:S(2)}) collective-permute-start(bf16[256,2048]{1,0:T(8,128)(2,1)} %get-tuple-element.122.refs_3_), channel_id=1, source_target_pairs={{0,2},{1,0},{3,1},{2,3},{4,6},{5,4},{7,5},{6,7},{8,10},{9,8},{11,9... | collective-permute-start | bytes 3145736 | tf_op jit(solution)/shard_map/ppermute | solution.py:393
  615.9 46.7 %collective-permute-start.46 = (bf16[256,2048]{1,0:T(8,128)(2,1)S(1)}, bf16[256,2048]{1,0:T(8,128)(2,1)}, u32[]{:S(2)}, u32[]{:S(2)}) collective-permute-start(bf16[256,2048]{1,0:T(8,128)(2,1)S(1)} %get-tuple-element.117.refs_5_), channel_id=1, source_target_pairs={{0,1},{1,3},{3,2},{2,0},{4,5},{5,7},{7,6},{6,4},{8,9},{9,11},{11,1... | collective-permute-start | bytes 3145736 | tf_op jit(solution)/shard_map/ppermute | solution.py:390
  617.7 46.6 %collective-permute-start.47 = (bf16[256,2048]{1,0:T(8,128)(2,1)S(1)}, bf16[256,2048]{1,0:T(8,128)(2,1)}, u32[]{:S(2)}, u32[]{:S(2)}) collective-permute-start(bf16[256,2048]{1,0:T(8,128)(2,1)S(1)} %get-tuple-element.118.refs_6_), channel_id=1, source_target_pairs={{0,2},{1,0},{3,1},{2,3},{4,6},{5,4},{7,5},{6,7},{8,10},{9,8},{11,9... | collective-permute-start | bytes 3145736 | tf_op jit(solution)/shard_map/ppermute | solution.py:393
  619.8 33.5 %collective-permute-start.42 = (bf16[128,2048]{1,0:T(8,128)(2,1)}, bf16[128,2048]{1,0:T(8,128)(2,1)}, u32[]{:S(2)}, u32[]{:S(2)}) collective-permute-start(bf16[128,2048]{1,0:T(8,128)(2,1)} %slice.239), channel_id=1, source_target_pairs={{0,1},{1,3},{3,2},{2,0},{4,5},{5,7},{7,6},{6,4},{8,9},{9,11},{11,1... | collective-permute-start | bytes 1572872 | tf_op jit(solution)/shard_map/ppermute | solution.py:390
  623.5 30.2 %collective-permute-start.43 = (bf16[128,2048]{1,0:T(8,128)(2,1)}, bf16[128,2048]{1,0:T(8,128)(2,1)}, u32[]{:S(2)}, u32[]{:S(2)}) collective-permute-start(bf16[128,2048]{1,0:T(8,128)(2,1)} %slice.240), channel_id=1, source_target_pairs={{0,2},{1,0},{3,1},{2,3},{4,6},{5,4},{7,5},{6,7},{8,10},{9,8},{11,9... | collective-permute-start | bytes 1572872 | tf_op jit(solution)/shard_map/ppermute | solution.py:393
  627.7 69.3 %collective-permute-start.65 = (bf16[128,2048]{1,0:T(8,128)(2,1)}, bf16[128,2048]{1,0:T(8,128)(2,1)}, u32[]{:S(2)}, u32[]{:S(2)}) collective-permute-start(bf16[128,2048]{1,0:T(8,128)(2,1)} %reduce-scatter.6.cloned.1.call-done.refs_0_), channel_id=1, source_target_pairs={{0,1},{1,3},{3,2},{2,0},{4,5},{5,7},{7,6},{6,4},{8,9},{9,11},{11,1... | collective-permute-start | bytes 1572872 | tf_op jit(solution)/shard_map/ppermute | solution.py:390
  653.4 54.2 %collective-permute-start.66 = (bf16[128,2048]{1,0:T(8,128)(2,1)}, bf16[128,2048]{1,0:T(8,128)(2,1)}, u32[]{:S(2)}, u32[]{:S(2)}) collective-permute-start(bf16[128,2048]{1,0:T(8,128)(2,1)} %reduce-scatter.6.cloned.1.call-done.refs_0_), channel_id=1, source_target_pairs={{0,2},{1,0},{3,1},{2,3},{4,6},{5,4},{7,5},{6,7},{8,10},{9,8},{11,9... | collective-permute-start | bytes 1572872 | tf_op jit(solution)/shard_map/ppermute | solution.py:393
  660.9 48.1 %collective-permute-start.61 = (bf16[128,2048]{1,0:T(8,128)(2,1)}, bf16[128,2048]{1,0:T(8,128)(2,1)}, u32[]{:S(2)}, u32[]{:S(2)}) collective-permute-start(bf16[128,2048]{1,0:T(8,128)(2,1)} %collective-permute-done.39.refs_4_.refs_0_), channel_id=1, source_target_pairs={{0,1},{1,3},{3,2},{2,0},{4,5},{5,7},{7,6},{6,4},{8,9},{9,11},{11,1... | collective-permute-start | bytes 1572872 | tf_op jit(solution)/shard_map/ppermute | solution.py:390
  662.6 33.7 %collective-permute-start.48 = (bf16[256,2048]{1,0:T(8,128)(2,1)}, bf16[256,2048]{1,0:T(8,128)(2,1)S(1)}, u32[]{:S(2)}, u32[]{:S(2)}) collective-permute-start(bf16[256,2048]{1,0:T(8,128)(2,1)} %reduce-scatter.12.cloned.1.call-done.refs_0_), channel_id=1, source_target_pairs={{0,1},{1,3},{3,2},{2,0},{4,5},{5,7},{7,6},{6,4},{8,9},{9,11},{11,1... | collective-permute-start | bytes 3145736 | tf_op jit(solution)/shard_map/ppermute | solution.py:390
  668.6 28.3 %collective-permute-start.49 = (bf16[256,2048]{1,0:T(8,128)(2,1)}, bf16[256,2048]{1,0:T(8,128)(2,1)S(1)}, u32[]{:S(2)}, u32[]{:S(2)}) collective-permute-start(bf16[256,2048]{1,0:T(8,128)(2,1)} %reduce-scatter.12.cloned.1.call-done.refs_0_), channel_id=1, source_target_pairs={{0,2},{1,0},{3,1},{2,3},{4,6},{5,4},{7,5},{6,7},{8,10},{9,8},{11,9... | collective-permute-start | bytes 3145736 | tf_op jit(solution)/shard_map/ppermute | solution.py:393
  709.0 29.5 %collective-permute-start.56 = (bf16[256,1024]{1,0:T(8,128)(2,1)}, bf16[256,1024]{1,0:T(8,128)(2,1)}, u32[]{:S(2)}, u32[]{:S(2)}) collective-permute-start(bf16[256,1024]{1,0:T(8,128)(2,1)} %reduce-scatter.14.cloned.1.call-done.refs_0_), channel_id=1, source_target_pairs={{0,2},{1,0},{3,1},{2,3},{4,6},{5,4},{7,5},{6,7},{8,10},{9,8},{11,9... | collective-permute-start | bytes 1572872 | tf_op jit(solution)/shard_map/ppermute | solution.py:393
  714.6 31.5 %collective-permute-start.63 = (bf16[64,2048]{1,0:T(8,128)(2,1)}, bf16[64,2048]{1,0:T(8,128)(2,1)}, u32[]{:S(2)}, u32[]{:S(2)}) collective-permute-start(bf16[64,2048]{1,0:T(8,128)(2,1)} %slice.249), channel_id=1, source_target_pairs={{0,1},{1,3},{3,2},{2,0},{4,5},{5,7},{7,6},{6,4},{8,9},{9,11},{11,1... | collective-permute-start | bytes 786440 | tf_op jit(solution)/shard_map/ppermute | solution.py:390
  716.0 30.7 %collective-permute-start.64 = (bf16[64,2048]{1,0:T(8,128)(2,1)}, bf16[64,2048]{1,0:T(8,128)(2,1)}, u32[]{:S(2)}, u32[]{:S(2)}) collective-permute-start(bf16[64,2048]{1,0:T(8,128)(2,1)} %slice.250), channel_id=1, source_target_pairs={{0,2},{1,0},{3,1},{2,3},{4,6},{5,4},{7,5},{6,7},{8,10},{9,8},{11,9... | collective-permute-start | bytes 786440 | tf_op jit(solution)/shard_map/ppermute | solution.py:393
  (82 other events, 1190.2 us)
Sparse Core Ops, SparseCore 0:
  11.3 129.9 all-gather.4
  143.4 48.1 all-gather.6
  193.8 80.7 all-gather.8
  276.1 45.6 all-gather.10
  323.9 43.6 reduce-scatter.5
  389.6 77.8 reduce-scatter.7
  477.2 45.1 reduce-scatter.9
  551.9 95.8 reduce-scatter.11
  650.7 44.3 reduce-scatter.13

commit v3 on v2

--- a/solution.py
+++ b/solution.py
@@ -797,35 +797,39 @@
         dres_low, out_ordered, retained, swish_pre, ggain, gshift, heads_here, places, (out_sum, both_share)
     )
     dquery, dkey, dvalue = retain_back(qkv, dretained, rates, query_width, value_width, ())
-    result_far = lax.optimization_barrier(result_far + (dvalue,))[:2]
+    sent = line.theirs(first, [dvalue, dswish], both_near + result_far)
+    result_far = lax.optimization_barrier(result_far + (sent,))[:2]
     near, result_near = ring.sum_near(result, result_far)
-    sent = line.theirs(first, [dvalue, dswish], near + both_near)
-    sent_qk = line.theirs(first, [dquery, dkey], (sent, out_share))
-    out_share = spread.back(out_share)
-    vs_sum = line.mine(first, [dvalue, dswish], sent, (sent_qk, out_share))
+    vs_sum = line.mine(first, [dvalue, dswish], sent, near + (out_share,) + both_pieces[1:])
     vs_share = line.scatter(vs_sum)
+    down_pieces = ring.pieces(after(down_share, vs_sum))
+    down_near = tuple(part for _, part in down_pieces[0])
     rights = [(first_full, 0), (first_full, 1), (first_full, 2 * query_width // value_width)]
     rights.append((first_full, third // value_width))
     terms = full_product([dquery, dkey, dvalue, dswish], rights, NT, width, (vs_sum,))
-    far, arrived = ring.sum_far(terms)
-    down_pieces = ring.pieces(after(down_share, sent))
-    qk_sum = line.mine(first, [dquery, dkey], sent_qk, far)
+    far, arrived = ring.sum_far(after(terms, *(result_near + down_near)))
+    sent_qk = line.theirs(first, [dquery, dkey], far)
+    arrived = lax.optimization_barrier(arrived + down_pieces[1:])[:2]
+    near, arrived = ring.sum_near(terms, arrived)
+    qk_sum = line.mine(first, [dquery, dkey], sent_qk, near)
     qk_share = line.scatter(qk_sum)
     result = ring.sum_own(after(result, qk_sum), result_near)
     layer_out = (resid + result + dbias).astype(BF16)
-    arrived = lax.optimization_barrier(arrived + (layer_out,))[:2]
-    near, arrived = ring.sum_near(terms, arrived)
     gating_grad, upward_grad = ring.gather_columns(
-        both_pieces, [(hidden_width, chunk), (hidden_width, chunk)], near
-    )
-    dfirst = ring.sum_own(after(terms, gating_grad), arrived)
+        both_pieces, [(hidden_width, chunk), (hidden_width, chunk)], (layer_out,)
+    )
+    downward_grad = ring.gather_rows(down_pieces, (gating_grad,))
+    arrived = lax.optimization_barrier(arrived + (downward_grad,))[:2]
+    dfirst = ring.sum_own(terms, arrived)
     again_term = jnp.sum(dfirst * first_norm, 0)
     ashift_term = jnp.sum(dfirst, 0)
     input_grad = dresid + normalize_back(dfirst * gain_one, first_norm, first_factor)
 
-    downward_grad = ring.gather_rows(down_pieces, (dfirst,))
-    out_grad = ring.gather_rows(ring.pieces(after(out_share, *near)), (downward_grad,))
-    vs_pieces = ring.pieces(vs_share)
+    vs_pieces = ring.pieces(after(vs_share, dfirst))
+    vs_near = tuple(part for _, part in vs_pieces[0])
+    out_share = spread.back(after(out_share, qk_sum))
+    out_pieces = ring.pieces(after(out_share, *vs_near))
+    out_grad = ring.gather_rows(out_pieces, ())
     value_grad, swish_grad = ring.gather_columns(
         vs_pieces, [(value_width, value_width), (value_width, value_width)], ()
     )
@@ -845,7 +849,7 @@
         fgain_term, fshift_term, placed_units(gbias_term[0]), placed_units(ubias_term[0]), dbias_term,
     ]
     terms = jnp.concatenate([term.reshape(shards, -1) for term in terms], 1)
-    totals = butterfly(after(butterfly(after(terms, *[part for _, part in vs_pieces[0]]), ("fsdp",)), qk_share), ("sp",))
+    totals = butterfly(after(butterfly(after(terms, *vs_near), ("fsdp",)), qk_share), ("sp",))
     mine = lax.dynamic_slice_in_dim(totals, lax.axis_index("fsdp"), 1, 0)[0]
     (
         again_grad, ashift_grad, ggain_grad, gshift_grad, fgain_grad, fshift_grad,

time: 789 us -> 773 us (0.980)
  starting transfers between devices: 97.3 us -> 82 us
    ppermute x26, starting transfers between devices: 51.2 us -> 27.4 us  [to_right(): return lax.ppermute(block, 'sp', self.right)]
    ppermute x8, waiting for transfers between devices: 34.6 us -> 43.3 us  [butterfly(): lax.ppermute(vector, axis, [(i, i ^ step) for i in range(size)])]
    unnamed x127 -> x133, local copies, waits for them, and re-layouts: 21.3 us -> 25 us
  transfers between devices with their start and end apart: 78 -> 78, of which waited for: 34 -> 43; matrix products, arithmetic and copies ran while one was open for 18% -> 18% of each run, Pallas kernels for 27% -> 27%
where the time goes in v3:
time: 773 us; the launch traced here: 762 us
  waiting for transfers between devices  275 us (36%)
  Pallas kernels  226 us (29%)
  starting transfers between devices  82 us (11%)
  local copies, waits for them, and re-layouts  78.8 us (10%)
  other arithmetic  58.9 us (8%)
  between operations  28.1 us (4%)
  matrix products  12.6 us (2%)
    ppermute x26, waiting for transfers between devices, to_right(): return lax.ppermute(block, 'sp', self.right)  171 us
    pallas_call x10, Pallas kernels, half(): pl.pallas_call(kernel, grid_spec=pltpu.PrefetchScalarGridSpec(num_scalar_...  75.9 us
    pallas_call x4, Pallas kernels, full_product(): pl.pallas_call(kernel, grid=(wide // step,), in_specs=specs + [UNREAD] *...  49.5 us
    ppermute x8, waiting for transfers between devices, butterfly(): lax.ppermute(vector, axis, [(i, i ^ step) for i in range(size)])  43.3 us
    ppermute x26, waiting for transfers between devices, to_left(): return lax.ppermute(block, 'sp', self.left)  40 us
    ppermute x26, starting transfers between devices, to_left(): return lax.ppermute(block, 'sp', self.left)  28.3 us
    ppermute x26, starting transfers between devices, to_right(): return lax.ppermute(block, 'sp', self.right)  27.4 us
    unnamed x133, local copies, waits for them, and re-layouts  25 us
  transfers between devices with their start and end apart: 78, of which 43 were waited for; matrix products, arithmetic and copies ran while one was open for 18% of the time, Pallas kernels for 27%

profile of v3, /device:TPU:0, one launch (start us, length us, event | category | flops | bytes accessed | tf_op | source)
XLA Modules:
  0.0 761.8 jit_solution(8249980524036327910)
XLA Ops:
  40.4 29.6 %collective-permute-done.6 = bf16[8,3328]{1,0:T(8,128)(2,1)S(1)} collective-permute-done((bf16[8,3328]{1,0:T(8,128)(2,1)S(1)}, bf16[8,3328]{1,0:T(8,128)(2,1)S(1)}, u32[]{:S(2)}, u32[]{:S(2)}) %collective-permute-start.6) | collective-permute-done | bytes 53280 | tf_op jit(solution)/shard_map/ppermute | solution.py:612
  122.1 13.9 %collective-permute-done.8 = bf16[256,2048]{1,0:T(8,128)(2,1)S(1)} collective-permute-done((bf16[256,2048]{1,0:T(8,128)(2,1)S(1)}, bf16[256,2048]{1,0:T(8,128)(2,1)S(1)}, u32[]{:S(2)}, u32[]{:S(2)}) %collective-permute-start.8) | collective-permute-done | bytes 1048608 | tf_op jit(solution)/shard_map/ppermute | solution.py:393
  149.3 19.6 %project.1 = (bf16[1024,2048]{1,0:T(8,128)(2,1)}, f32[1024,1024]{1,0:T(8,128)}) custom-call(bf16[1024,2048]{1,0:T(8,128)(2,1)} %add_convert_fusion.x_ref, bf16[2048,3072]{1,0:T(8,128)(2,1)} %all-gather.5.cloned.1.call-done.w_ref.refs_4_.refs_5_.refs_6_.refs_7_), custom_call_target="tpu_custom_call" | custom-call | flops 1024 | bytes 1024 | tf_op jit(solution)/shard_map/project/pallas_call | solution.py:95
  168.9 9.0 %retain_mix.1 = (bf16[1024,1024]{1,0:T(8,128)(2,1)}, bf16[1024,1024]{1,0:T(8,128)(2,1)}) custom-call(f32[2]{0:T(128)} %subtract_log_fusion.rate_ref, s32[8]{0:T(128)} %fusion.22.place_ref, bf16[1024,2048]{1,0:T(8,128)(2,1)} %get-tuple-element.65.q_ref.k_ref.v_ref, bf16[1024,2048]{1,0:T(8,128)(2,1)} %get-tuple-element.65.q_ref.k_ref.v_ref, ...), custom_call_target="tpu_custom_call" | custom-call | flops 1024 | bytes 1024 | tf_op jit(solution)/shard_map/retain_mix/pallas_call | solution.py:155
  177.9 13.8 %all-gather.7.cloned.1.call-done.refs_1_.w_ref = bf16[1024,2048]{1,0:T(8,128)(2,1)} async-done(((bf16[128,2048]{1,0:T(8,128)(2,1)}), bf16[1024,2048]{1,0:T(8,128)(2,1)}) %all-gather.7.cloned.1.call-update) | async-done | bytes 4194320 | tf_op jit(solution)/shard_map/all_gather | solution.py:705
  191.7 8.3 %full_product.4 = bf16[1024,2048]{1,0:T(8,128)(2,1)} custom-call(bf16[1024,1024]{1,0:T(8,128)(2,1)} %get-tuple-element.69.refs_0_.x_ref, bf16[1024,2048]{1,0:T(8,128)(2,1)} %all-gather.7.cloned.1.call-done.refs_1_.w_ref), custom_call_target="tpu_custom_call" | custom-call | flops 1024 | bytes 1024 | tf_op jit(solution)/shard_map/full_product/pallas_call | solution.py:358
  204.8 10.8 %collective-permute-done.13 = bf16[128,2048]{1,0:T(8,128)(2,1)S(1)} collective-permute-done((bf16[128,2048]{1,0:T(8,128)(2,1)S(1)}, bf16[128,2048]{1,0:T(8,128)(2,1)S(1)}, u32[]{:S(2)}, u32[]{:S(2)}) %collective-permute-start.13) | collective-permute-done | bytes 524320 | tf_op jit(solution)/shard_map/ppermute | solution.py:390
  225.7 19.0 %collective-permute-done.14 = bf16[256,2048]{1,0:T(8,128)(2,1)S(1)} collective-permute-done((bf16[256,2048]{1,0:T(8,128)(2,1)}, bf16[256,2048]{1,0:T(8,128)(2,1)S(1)}, u32[]{:S(2)}, u32[]{:S(2)}) %collective-permute-start.14) | collective-permute-done | bytes 1048608 | tf_op jit(solution)/shard_map/ppermute | solution.py:390
  252.4 20.5 %collective-permute-done.17 = bf16[256,2048]{1,0:T(8,128)(2,1)S(1)} collective-permute-done((bf16[256,2048]{1,0:T(8,128)(2,1)S(1)}, bf16[256,2048]{1,0:T(8,128)(2,1)S(1)}, u32[]{:S(2)}, u32[]{:S(2)}) %collective-permute-start.17) | collective-permute-done | bytes 1048608 | tf_op jit(solution)/shard_map/ppermute | solution.py:390
  288.6 12.6 %fusion.29.gate_ref.up_ref = f32[1024,2048]{1,0:T(8,128)S(1)} fusion(bf16[1024,2048]{1,0:T(8,128)(2,1)} %bitcast.31.x_ref, bf16[2048,2048]{1,0:T(8,128)(2,1)} %all-gather.9.cloned.1.call-done.refs_2_.refs_3_), kind=kOutput, calls=%fused_computation.157 | convolution fusion | flops 8589934592 | bytes 20971520 | tf_op jit(solution)/shard_map/dot_general | solution.py:22
  316.2 6.9 rows_sum.11.rest_0_
  323.2 13.3 %gate_back.1 = (bf16[1024,1024]{1,0:T(8,128)(2,1)}, bf16[1024,1024]{1,0:T(8,128)(2,1)}, f32[1,1024]{1,0:T(1,128)}, f32[1,1024]{1,0:T(1,128)}) custom-call(bf16[1024,2048]{1,0:T(8,128)(2,1)} %bitcast.21.refs_0_.g_ref, bf16[1024,2048]{1,0:T(8,128)(2,1)} %all-gather.11.cloned.1.call-done.w_ref.refs_1_, f32[1024,2048]{1,0:T(8,128)} %copy-done.2, ...), custom_call_target="tpu_custom_call" | custom-call | flops 1024 | bytes 1024 | tf_op jit(solution)/shard_map/gate_back/pallas_call | solution.py:259
  336.6 13.4 %full_product.5 = bf16[1024,2048]{1,0:T(8,128)(2,1)} custom-call(bf16[1024,1024]{1,0:T(8,128)(2,1)} %get-tuple-element.72.refs_0_, bf16[1024,1024]{1,0:T(8,128)(2,1)} %get-tuple-element.73.refs_1_, bf16[2048,2048]{1,0:T(8,128)(2,1)} %all-gather.9.cloned.1.call-done.refs_2_.refs_3_, bf16[2048,2048]{1,0:T(8,128)(2,1)} %all-gather.9.cloned.1.call-done.refs_2_.refs_3_), custom_call_target="tpu_custom_call" | custom-call | flops 1024 | bytes 1024 | tf_op jit(solution)/shard_map/full_product/pallas_call | solution.py:358
  352.3 8.8 %rows_sum.12 = bf16[1024,2048]{1,0:T(8,128)(2,1)} custom-call(s32[1]{0:T(128)} %bitcast.35.core_ref, bf16[1024,2048]{1,0:T(8,128)(2,1)} %bitcast.31.x_ref, bf16[1024,1024]{1,0:T(8,128)(2,1)} %get-tuple-element.72.refs_0_, bf16[1024,1024]{1,0:T(8,128)(2,1)} %get-tuple-element.73.refs_1_, bf16[128,2048]{1,0:T(8,128)(2,1)} %get-tuple-element.136.refs_2_, ...), custom_call_target="tpu_custom_call" | custom-call | flops 1024 | bytes 1024 | tf_op jit(solution)/shard_map/rows_sum/pallas_call | solution.py:579
  363.3 12.4 %collective-permute-done.23 = bf16[128,2048]{1,0:T(8,128)(2,1)} collective-permute-done((bf16[128,2048]{1,0:T(8,128)(2,1)}, bf16[128,2048]{1,0:T(8,128)(2,1)}, u32[]{:S(2)}, u32[]{:S(2)}) %collective-permute-start.23) | collective-permute-done | bytes 524320 | tf_op jit(solution)/shard_map/ppermute | solution.py:390
  379.9 9.5 %rows_sum.13.refs_2_ = bf16[1024,2048]{1,0:T(8,128)(2,1)} custom-call(s32[1]{0:T(128)} %bitcast.32.core_ref, bf16[1024,2048]{1,0:T(8,128)(2,1)} %bitcast.31.x_ref, bf16[1024,1024]{1,0:T(8,128)(2,1)} %get-tuple-element.72.refs_0_, bf16[1024,1024]{1,0:T(8,128)(2,1)} %get-tuple-element.73.refs_1_, bf16[1024,2048]{1,0:T(8,128)(2,1)} %collective-permute-done.22.refs_2_, ...), custom_call_target="tpu_custom_call" | custom-call | flops 1024 | bytes 1024 | tf_op jit(solution)/shard_map/rows_sum/pallas_call | solution.py:579
  391.7 8.5 %full_product.6 = bf16[1024,2048]{1,0:T(8,128)(2,1)} custom-call(bf16[1024,1024]{1,0:T(8,128)(2,1)} %fusion.3.x_ref.refs_0_, bf16[1024,2048]{1,0:T(8,128)(2,1)} %all-gather.11.cloned.1.call-done.w_ref.refs_1_, bf16[1024,2048]{1,0:T(8,128)(2,1)} %rows_sum.13.refs_2_), custom_call_target="tpu_custom_call" | custom-call | flops 1024 | bytes 1024 | tf_op jit(solution)/shard_map/full_product/pallas_call | solution.py:358
  400.2 14.0 %collective-permute-done.25 = bf16[256,2048]{1,0:T(8,128)(2,1)} collective-permute-done((bf16[256,2048]{1,0:T(8,128)(2,1)}, bf16[256,2048]{1,0:T(8,128)(2,1)}, u32[]{:S(2)}, u32[]{:S(2)}) %collective-permute-start.25) | collective-permute-done | bytes 1048608 | tf_op jit(solution)/shard_map/ppermute | solution.py:390
  422.2 21.1 %collective-permute-done.27 = bf16[256,2048]{1,0:T(8,128)(2,1)S(1)} collective-permute-done((bf16[256,2048]{1,0:T(8,128)(2,1)S(1)}, bf16[256,2048]{1,0:T(8,128)(2,1)S(1)}, u32[]{:S(2)}, u32[]{:S(2)}) %collective-permute-start.27) | collective-permute-done | bytes 1048608 | tf_op jit(solution)/shard_map/ppermute | solution.py:390
  468.0 6.9 rows_sum.15.rest_0_
  479.0 17.5 %mixed_back.1 = (bf16[1024,1024]{1,0:T(8,128)(2,1)}, bf16[1024,1024]{1,0:T(8,128)(2,1)}, f32[1,1024]{1,0:T(1,128)}, f32[1,1024]{1,0:T(1,128)}) custom-call(s32[8]{0:T(128)} %fusion.22.place_ref, bf16[1024,2048]{1,0:T(8,128)(2,1)} %bitcast.41.refs_0_.d_ref, bf16[1024,2048]{1,0:T(8,128)(2,1)} %all-gather.7.cloned.1.call-done.refs_1_.w_ref, ...), custom_call_target="tpu_custom_call" | custom-call | flops 1024 | bytes 1024 | tf_op jit(solution)/shard_map/mixed_back/pallas_call | solution.py:317
  496.6 12.7 %retain_back.1 = (bf16[1024,512]{1,0:T(8,128)(2,1)}, bf16[1024,512]{1,0:T(8,128)(2,1)}, bf16[1024,1024]{1,0:T(8,128)(2,1)}) custom-call(f32[2]{0:T(128)} %subtract_log_fusion.rate_ref, bf16[1024,2048]{1,0:T(8,128)(2,1)} %get-tuple-element.65.q_ref.k_ref.v_ref, bf16[1024,2048]{1,0:T(8,128)(2,1)} %get-tuple-element.65.q_ref.k_ref.v_ref, ...), custom_call_target="tpu_custom_call" | custom-call | flops 1024 | bytes 1024 | tf_op jit(solution)/shard_map/retain_back/pallas_call | solution.py:209
  512.8 8.8 %rows_sum.16 = bf16[1024,2048]{1,0:T(8,128)(2,1)} custom-call(s32[1]{0:T(128)} %bitcast.35.core_ref, bf16[1024,2048]{1,0:T(8,128)(2,1)} %add_convert_fusion.x_ref, bf16[1024,1024]{1,0:T(8,128)(2,1)} %get-tuple-element.84.refs_0_.refs_2_, bf16[1024,1024]{1,0:T(8,128)(2,1)} %get-tuple-element.85.refs_1_.refs_3_, ...), custom_call_target="tpu_custom_call" | custom-call | flops 1024 | bytes 1024 | tf_op jit(solution)/shard_map/rows_sum/pallas_call | solution.py:579
  531.2 6.9 collective-permute-done.37.refs_6_.refs_3_
  540.3 9.5 %rows_sum.17.refs_8_ = bf16[1024,2048]{1,0:T(8,128)(2,1)} custom-call(s32[1]{0:T(128)} %bitcast.32.core_ref, bf16[1024,2048]{1,0:T(8,128)(2,1)} %add_convert_fusion.x_ref, bf16[1024,1024]{1,0:T(8,128)(2,1)} %get-tuple-element.84.refs_0_.refs_2_, bf16[1024,1024]{1,0:T(8,128)(2,1)} %get-tuple-element.85.refs_1_.refs_3_, ...), custom_call_target="tpu_custom_call" | custom-call | flops 1024 | bytes 1024 | tf_op jit(solution)/shard_map/rows_sum/pallas_call | solution.py:579
  554.0 19.2 %full_product.7 = bf16[1024,2048]{1,0:T(8,128)(2,1)} custom-call(bf16[1024,512]{1,0:T(8,128)(2,1)} %get-tuple-element.82.refs_0_, bf16[1024,512]{1,0:T(8,128)(2,1)} %get-tuple-element.83.refs_1_, bf16[1024,1024]{1,0:T(8,128)(2,1)} %get-tuple-element.84.refs_0_.refs_2_, bf16[1024,1024]{1,0:T(8,128)(2,1)} %get-tuple-element.85.refs_1_.refs_3_, ...), custom_call_target="tpu_custom_call" | custom-call | flops 1024 | bytes 1024 | tf_op jit(solution)/shard_map/full_product/pallas_call | solution.py:358
  577.3 8.6 %collective-permute-done.41.refs_1_ = bf16[128,2048]{1,0:T(8,128)(2,1)} collective-permute-done((bf16[128,2048]{1,0:T(8,128)(2,1)}, bf16[128,2048]{1,0:T(8,128)(2,1)}, u32[]{:S(2)}, u32[]{:S(2)}) %collective-permute-start.41) | collective-permute-done | bytes 524320 | tf_op jit(solution)/shard_map/ppermute | solution.py:390
  601.3 13.8 %collective-permute-done.46.refs_3_ = bf16[64,2048]{1,0:T(8,128)(2,1)S(1)} collective-permute-done((bf16[64,2048]{1,0:T(8,128)(2,1)S(1)}, bf16[64,2048]{1,0:T(8,128)(2,1)S(1)}, u32[]{:S(2)}, u32[]{:S(2)}) %collective-permute-start.46) | collective-permute-done | bytes 262176 | tf_op jit(solution)/shard_map/ppermute | solution.py:390
  641.6 6.8 gather_columns.3
  665.3 15.8 %collective-permute-done.50.refs_1_ = bf16[256,2048]{1,0:T(8,128)(2,1)} collective-permute-done((bf16[256,2048]{1,0:T(8,128)(2,1)}, bf16[256,2048]{1,0:T(8,128)(2,1)}, u32[]{:S(2)}, u32[]{:S(2)}) %collective-permute-start.50) | collective-permute-done | bytes 1048608 | tf_op jit(solution)/shard_map/ppermute | solution.py:390
  710.2 7.2 collective-permute-done.55
  722.3 9.3 %collective-permute-done.61.refs_3_ = bf16[128,2048]{1,0:T(8,128)(2,1)} collective-permute-done((bf16[128,2048]{1,0:T(8,128)(2,1)S(1)}, bf16[128,2048]{1,0:T(8,128)(2,1)}, u32[]{:S(2)}, u32[]{:S(2)}) %collective-permute-start.61) | collective-permute-done | bytes 524320 | tf_op jit(solution)/shard_map/ppermute | solution.py:390
  (409 shorter events, 325.7 us)
Async XLA Ops:
  7.2 142.0 %all-gather.5.cloned.1.call-start = ((), (), s32[]{:S(2)}) async-start(), calls=%async_computation.5 | async-start | bytes 14155776 | tf_op jit(solution)/shard_map/all_gather | solution.py:705
  11.2 180.5 %all-gather.7.cloned.1.call-start = ((), (), s32[]{:S(2)}) async-start(), calls=%async_computation.6 | async-start | bytes 4718592 | tf_op jit(solution)/shard_map/all_gather | solution.py:705
  13.8 58.6 %collective-permute-start = (bf16[256,2048]{1,0:T(8,128)(2,1)S(1)}, bf16[256,2048]{1,0:T(8,128)(2,1)}, u32[]{:S(2)}, u32[]{:S(2)}) collective-permute-start(bf16[256,2048]{1,0:T(8,128)(2,1)S(1)} %bitcast.132), channel_id=1, source_target_pairs={{0,1},{1,3},{3,2},{2,0},{4,5},{5,7},{7,6},{6,4},{8,9},{9,11},{11,1... | collective-permute-start | bytes 3145736 | tf_op jit(solution)/shard_map/ppermute | solution.py:390
  16.4 57.2 %collective-permute-start.1 = (bf16[256,2048]{1,0:T(8,128)(2,1)S(1)}, bf16[256,2048]{1,0:T(8,128)(2,1)}, u32[]{:S(2)}, u32[]{:S(2)}) collective-permute-start(bf16[256,2048]{1,0:T(8,128)(2,1)S(1)} %bitcast.133), channel_id=1, source_target_pairs={{0,2},{1,0},{3,1},{2,3},{4,6},{5,4},{7,5},{6,7},{8,10},{9,8},{11,9... | collective-permute-start | bytes 3145736 | tf_op jit(solution)/shard_map/ppermute | solution.py:393
  19.6 51.1 %collective-permute-start.11 = (bf16[128,2048]{1,0:T(8,128)(2,1)}, bf16[128,2048]{1,0:T(8,128)(2,1)}, u32[]{:S(2)}, u32[]{:S(2)}) collective-permute-start(bf16[128,2048]{1,0:T(8,128)(2,1)} %constant_dynamic-slice_fusion.10), channel_id=1, source_target_pairs={{0,0},{4,4},{8,16},{12,20},{16,8},{20,12},{24,24},{28,28},{1,9},{5... | collective-permute-start | bytes 1572872 | tf_op jit(solution)/shard_map/ppermute | solution.py:639
  30.9 39.2 %collective-permute-start.6 = (bf16[8,3328]{1,0:T(8,128)(2,1)S(1)}, bf16[8,3328]{1,0:T(8,128)(2,1)S(1)}, u32[]{:S(2)}, u32[]{:S(2)}) collective-permute-start(bf16[8,3328]{1,0:T(8,128)(2,1)S(1)} %add.294), channel_id=1, source_target_pairs={{0,16},{4,20},{8,24},{12,28},{16,0},{20,4},{24,8},{28,12},{1,17},{... | collective-permute-start | bytes 159752 | tf_op jit(solution)/shard_map/ppermute | solution.py:612
  70.7 26.3 %collective-permute-start.12 = (bf16[128,2048]{1,0:T(8,128)(2,1)}, bf16[128,2048]{1,0:T(8,128)(2,1)S(1)}, u32[]{:S(2)}, u32[]{:S(2)}) collective-permute-start(bf16[128,2048]{1,0:T(8,128)(2,1)} %collective-permute-done.11), channel_id=1, source_target_pairs={{0,0},{4,4},{16,17},{20,21},{8,10},{12,14},{24,27},{28,31},{9,8},{... | collective-permute-start | bytes 1572872 | tf_op jit(solution)/shard_map/ppermute | solution.py:640
  97.8 190.8 %all-gather.9.cloned.1.call-start = ((), (), s32[]{:S(2)}) async-start(), calls=%async_computation.7 | async-start | bytes 9437184 | tf_op jit(solution)/shard_map/all_gather | solution.py:705
  112.8 210.5 %all-gather.11.cloned.1.call-start = ((), (), s32[]{:S(2)}) async-start(), calls=%async_computation.8 | async-start | bytes 4718592 | tf_op jit(solution)/shard_map/all_gather | solution.py:705
  224.3 151.9 %reduce-scatter.6.cloned.1.call-start = ((), (), s32[]{:S(2)}) async-start(), calls=%async_computation.9 | async-start | bytes 2621440 | tf_op jit(solution)/shard_map/reduce_scatter | solution.py:602
  323.2 151.7 %reduce-scatter.8.cloned.1.call-start = ((), (), s32[]{:S(2)}) async-start(), calls=%async_computation.10 | async-start | bytes 5242880 | tf_op jit(solution)/shard_map/reduce_scatter | solution.py:602
  389.4 141.8 %reduce-scatter.10.cloned.1.call-start = ((), (), s32[]{:S(2)}) async-start(), calls=%async_computation.11 | async-start | bytes 2621440 | tf_op jit(solution)/shard_map/reduce_scatter | solution.py:602
  474.9 37.9 %collective-permute-start.32 = (bf16[256,2048]{1,0:T(8,128)(2,1)}, bf16[256,2048]{1,0:T(8,128)(2,1)}, u32[]{:S(2)}, u32[]{:S(2)}) collective-permute-start(bf16[256,2048]{1,0:T(8,128)(2,1)} %reduce-scatter.8.cloned.1.call-done.rest_1_.refs_2_.refs_0_), channel_id=1, source_target_pairs={{0,1},{1,3},{3,2},{2,0},{4,5},{5,7},{7,6},{6,4},{8,9},{9,11},{11,1... | collective-permute-start | bytes 3145736 | tf_op jit(solution)/shard_map/ppermute | solution.py:390
  476.3 36.5 %collective-permute-start.33 = (bf16[256,2048]{1,0:T(8,128)(2,1)}, bf16[256,2048]{1,0:T(8,128)(2,1)}, u32[]{:S(2)}, u32[]{:S(2)}) collective-permute-start(bf16[256,2048]{1,0:T(8,128)(2,1)} %reduce-scatter.8.cloned.1.call-done.rest_1_.refs_2_.refs_0_), channel_id=1, source_target_pairs={{0,2},{1,0},{3,1},{2,3},{4,6},{5,4},{7,5},{6,7},{8,10},{9,8},{11,9... | collective-permute-start | bytes 3145736 | tf_op jit(solution)/shard_map/ppermute | solution.py:393
  476.9 35.9 %collective-permute-start.35 = (bf16[128,2048]{1,0:T(8,128)(2,1)}, bf16[128,2048]{1,0:T(8,128)(2,1)}, u32[]{:S(2)}, u32[]{:S(2)}) collective-permute-start(bf16[128,2048]{1,0:T(8,128)(2,1)} %get-tuple-element.80.refs_3_), channel_id=1, source_target_pairs={{0,2},{1,0},{3,1},{2,3},{4,6},{5,4},{7,5},{6,7},{8,10},{9,8},{11,9... | collective-permute-start | bytes 1572872 | tf_op jit(solution)/shard_map/ppermute | solution.py:393
  477.9 34.9 %collective-permute-start.34 = (bf16[128,2048]{1,0:T(8,128)(2,1)}, bf16[128,2048]{1,0:T(8,128)(2,1)}, u32[]{:S(2)}, u32[]{:S(2)}) collective-permute-start(bf16[128,2048]{1,0:T(8,128)(2,1)} %get-tuple-element.79.refs_2_), channel_id=1, source_target_pairs={{0,1},{1,3},{3,2},{2,0},{4,5},{5,7},{7,6},{6,4},{8,9},{9,11},{11,1... | collective-permute-start | bytes 1572872 | tf_op jit(solution)/shard_map/ppermute | solution.py:390
  479.0 178.8 %reduce-scatter.12.cloned.1.call-start = ((), (), s32[]{:S(2)}) async-start(), calls=%async_computation.12 | async-start | bytes 5242880 | tf_op jit(solution)/shard_map/reduce_scatter | solution.py:602
  549.8 138.1 %reduce-scatter.14.cloned.1.call-start = ((), (), s32[]{:S(2)}) async-start(), calls=%async_computation.13 | async-start | bytes 2621440 | tf_op jit(solution)/shard_map/reduce_scatter | solution.py:602
  549.9 26.5 %collective-permute-start.39 = (bf16[256,2048]{1,0:T(8,128)(2,1)}, bf16[256,2048]{1,0:T(8,128)(2,1)}, u32[]{:S(2)}, u32[]{:S(2)}) collective-permute-start(bf16[256,2048]{1,0:T(8,128)(2,1)} %get-tuple-element.129.refs_3_), channel_id=1, source_target_pairs={{0,1},{1,3},{3,2},{2,0},{4,5},{5,7},{7,6},{6,4},{8,9},{9,11},{11,1... | collective-permute-start | bytes 3145736 | tf_op jit(solution)/shard_map/ppermute | solution.py:390
  550.9 26.4 %collective-permute-start.40 = (bf16[256,2048]{1,0:T(8,128)(2,1)}, bf16[256,2048]{1,0:T(8,128)(2,1)}, u32[]{:S(2)}, u32[]{:S(2)}) collective-permute-start(bf16[256,2048]{1,0:T(8,128)(2,1)} %get-tuple-element.130.refs_4_), channel_id=1, source_target_pairs={{0,2},{1,0},{3,1},{2,3},{4,6},{5,4},{7,5},{6,7},{8,10},{9,8},{11,9... | collective-permute-start | bytes 3145736 | tf_op jit(solution)/shard_map/ppermute | solution.py:393
  551.9 34.0 %collective-permute-start.41 = (bf16[128,2048]{1,0:T(8,128)(2,1)}, bf16[128,2048]{1,0:T(8,128)(2,1)}, u32[]{:S(2)}, u32[]{:S(2)}) collective-permute-start(bf16[128,2048]{1,0:T(8,128)(2,1)} %reduce-scatter.6.cloned.1.call-done.refs_0_), channel_id=1, source_target_pairs={{0,1},{1,3},{3,2},{2,0},{4,5},{5,7},{7,6},{6,4},{8,9},{9,11},{11,1... | collective-permute-start | bytes 1572872 | tf_op jit(solution)/shard_map/ppermute | solution.py:390
  552.9 33.7 %collective-permute-start.42 = (bf16[128,2048]{1,0:T(8,128)(2,1)}, bf16[128,2048]{1,0:T(8,128)(2,1)}, u32[]{:S(2)}, u32[]{:S(2)}) collective-permute-start(bf16[128,2048]{1,0:T(8,128)(2,1)} %reduce-scatter.6.cloned.1.call-done.refs_0_), channel_id=1, source_target_pairs={{0,2},{1,0},{3,1},{2,3},{4,6},{5,4},{7,5},{6,7},{8,10},{9,8},{11,9... | collective-permute-start | bytes 1572872 | tf_op jit(solution)/shard_map/ppermute | solution.py:393
  595.0 25.2 %collective-permute-start.43 = (bf16[1024,1024]{1,0:T(8,128)(2,1)}, bf16[1024,1024]{1,0:T(8,128)(2,1)}, u32[]{:S(2)}, u32[]{:S(2)}) collective-permute-start(bf16[1024,1024]{1,0:T(8,128)(2,1)} %rows_sum.18), channel_id=1, source_target_pairs={{0,4},{4,0},{8,12},{12,8},{16,20},{20,16},{24,28},{28,24},{1,5},{5... | collective-permute-start | bytes 6291464 | tf_op jit(solution)/shard_map/ppermute | solution.py:551
  626.7 26.8 %collective-permute-start.48 = (bf16[256,2048]{1,0:T(8,128)(2,1)}, bf16[256,2048]{1,0:T(8,128)(2,1)}, u32[]{:S(2)}, u32[]{:S(2)}) collective-permute-start(bf16[256,2048]{1,0:T(8,128)(2,1)} %get-tuple-element.126.refs_3_), channel_id=1, source_target_pairs={{0,1},{1,3},{3,2},{2,0},{4,5},{5,7},{7,6},{6,4},{8,9},{9,11},{11,1... | collective-permute-start | bytes 3145736 | tf_op jit(solution)/shard_map/ppermute | solution.py:390
  628.1 26.4 %collective-permute-start.49 = (bf16[256,2048]{1,0:T(8,128)(2,1)}, bf16[256,2048]{1,0:T(8,128)(2,1)}, u32[]{:S(2)}, u32[]{:S(2)}) collective-permute-start(bf16[256,2048]{1,0:T(8,128)(2,1)} %get-tuple-element.125.refs_4_), channel_id=1, source_target_pairs={{0,2},{1,0},{3,1},{2,3},{4,6},{5,4},{7,5},{6,7},{8,10},{9,8},{11,9... | collective-permute-start | bytes 3145736 | tf_op jit(solution)/shard_map/ppermute | solution.py:393
  658.0 28.5 %collective-permute-start.51 = (bf16[256,2048]{1,0:T(8,128)(2,1)}, bf16[256,2048]{1,0:T(8,128)(2,1)}, u32[]{:S(2)}, u32[]{:S(2)}) collective-permute-start(bf16[256,2048]{1,0:T(8,128)(2,1)} %reduce-scatter.12.cloned.1.call-done.refs_0_), channel_id=1, source_target_pairs={{0,2},{1,0},{3,1},{2,3},{4,6},{5,4},{7,5},{6,7},{8,10},{9,8},{11,9... | collective-permute-start | bytes 3145736 | tf_op jit(solution)/shard_map/ppermute | solution.py:393
  659.9 30.2 %collective-permute-start.64 = (bf16[128,2048]{1,0:T(8,128)(2,1)}, bf16[128,2048]{1,0:T(8,128)(2,1)}, u32[]{:S(2)}, u32[]{:S(2)}) collective-permute-start(bf16[128,2048]{1,0:T(8,128)(2,1)} %collective-permute-done.63), channel_id=1, source_target_pairs={{0,0},{4,4},{16,8},{20,12},{8,16},{12,20},{24,24},{28,28},{9,1},{1... | collective-permute-start | bytes 1572872 | tf_op jit(solution)/shard_map/ppermute | solution.py:644
  690.0 27.4 %collective-permute-start.65 = (bf16[128,2048]{1,0:T(8,128)(2,1)}, bf16[128,2048]{1,0:T(8,128)(2,1)S(1)}, u32[]{:S(2)}, u32[]{:S(2)}) collective-permute-start(bf16[128,2048]{1,0:T(8,128)(2,1)} %collective-permute-done.64.refs_0_), channel_id=1, source_target_pairs={{0,1},{1,3},{3,2},{2,0},{4,5},{5,7},{7,6},{6,4},{8,9},{9,11},{11,1... | collective-permute-start | bytes 1572872 | tf_op jit(solution)/shard_map/ppermute | solution.py:390
  690.9 28.6 %collective-permute-start.66 = (bf16[128,2048]{1,0:T(8,128)(2,1)}, bf16[128,2048]{1,0:T(8,128)(2,1)S(1)}, u32[]{:S(2)}, u32[]{:S(2)}) collective-permute-start(bf16[128,2048]{1,0:T(8,128)(2,1)} %collective-permute-done.64.refs_0_), channel_id=1, source_target_pairs={{0,2},{1,0},{3,1},{2,3},{4,6},{5,4},{7,5},{6,7},{8,10},{9,8},{11,9... | collective-permute-start | bytes 1572872 | tf_op jit(solution)/shard_map/ppermute | solution.py:393
  704.5 36.4 %collective-permute-start.59 = (bf16[128,1024]{1,0:T(8,128)(2,1)}, bf16[128,1024]{1,0:T(8,128)(2,1)S(1)}, u32[]{:S(2)}, u32[]{:S(2)}) collective-permute-start(bf16[128,1024]{1,0:T(8,128)(2,1)} %slice.245), channel_id=1, source_target_pairs={{0,1},{1,3},{3,2},{2,0},{4,5},{5,7},{7,6},{6,4},{8,9},{9,11},{11,1... | collective-permute-start | bytes 786440 | tf_op jit(solution)/shard_map/ppermute | solution.py:390
  707.0 33.9 %collective-permute-start.60 = (bf16[128,1024]{1,0:T(8,128)(2,1)}, bf16[128,1024]{1,0:T(8,128)(2,1)}, u32[]{:S(2)}, u32[]{:S(2)}) collective-permute-start(bf16[128,1024]{1,0:T(8,128)(2,1)} %slice.246), channel_id=1, source_target_pairs={{0,2},{1,0},{3,1},{2,3},{4,6},{5,4},{7,5},{6,7},{8,10},{9,8},{11,9... | collective-permute-start | bytes 786440 | tf_op jit(solution)/shard_map/ppermute | solution.py:393
  719.6 27.0 %collective-permute-start.56 = (f32[8,3328]{1,0:T(8,128)S(1)}, f32[8,3328]{1,0:T(8,128)}, u32[]{:S(2)}, u32[]{:S(2)}) collective-permute-start(f32[8,3328]{1,0:T(8,128)S(1)} %add.682), channel_id=1, source_target_pairs={{0,2},{1,3},{2,0},{3,1},{4,6},{5,7},{6,4},{7,5},{8,10},{9,11},{10,... | collective-permute-start | bytes 319496 | tf_op jit(solution)/shard_map/ppermute | solution.py:612
  (85 other events, 1015.5 us)
Sparse Core Ops, SparseCore 0:
  11.3 129.9 all-gather.4
  143.4 48.1 all-gather.6
  193.8 80.7 all-gather.8
  276.1 45.6 all-gather.10
  323.9 43.6 reduce-scatter.5
  389.5 77.8 reduce-scatter.7
  479.1 45.2 reduce-scatter.9
  549.9 78.3 reduce-scatter.11
  631.2 44.4 reduce-scatter.13

commit v4 on v3

--- a/solution.py
+++ b/solution.py
@@ -340,7 +340,7 @@
 
 def full_product(lefts, rights, dims, wide, deps):
     length = lefts[0].shape[0]
-    step = min(wide, 512)
+    step = min(wide, 1024)
     specs = [pl.BlockSpec((length, left.shape[1]), lambda n: (0, 0)) for left in lefts]
     for left, (_, column) in zip(lefts, rights):
         depth = left.shape[1]

time: 773 us -> 773 us (level)
  no operation moved by 1% of the time
where the time goes in v4:
time: 773 us; the launch traced here: 762 us
  waiting for transfers between devices  274 us (35%)
  Pallas kernels  227 us (29%)
  starting transfers between devices  82 us (11%)
  local copies, waits for them, and re-layouts  78.8 us (10%)
  other arithmetic  58.9 us (8%)
  between operations  28.3 us (4%)
  matrix products  12.6 us (2%)
    ppermute x26, waiting for transfers between devices, to_right(): return lax.ppermute(block, 'sp', self.right)  170 us
    pallas_call x10, Pallas kernels, half(): pl.pallas_call(kernel, grid_spec=pltpu.PrefetchScalarGridSpec(num_scalar_...  75.9 us
    pallas_call x4, Pallas kernels, full_product(): pl.pallas_call(kernel, grid=(wide // step,), in_specs=specs + [UNREAD] *...  51 us
    ppermute x8, waiting for transfers between devices, butterfly(): lax.ppermute(vector, axis, [(i, i ^ step) for i in range(size)])  43.6 us
    ppermute x26, waiting for transfers between devices, to_left(): return lax.ppermute(block, 'sp', self.left)  39.7 us
    ppermute x26, starting transfers between devices, to_right(): return lax.ppermute(block, 'sp', self.right)  28.6 us
    ppermute x26, starting transfers between devices, to_left(): return lax.ppermute(block, 'sp', self.left)  27.3 us
    unnamed x133, local copies, waits for them, and re-layouts  25 us
  transfers between devices with their start and end apart: 78, of which 43 were waited for; matrix products, arithmetic and copies ran while one was open for 18% of the time, Pallas kernels for 27%

profile of v4, /device:TPU:0, one launch (start us, length us, event | category | flops | bytes accessed | tf_op | source)
XLA Modules:
  0.0 762.3 jit_solution(12647584796439654529)
XLA Ops:
  40.4 29.6 %collective-permute-done.6 = bf16[8,3328]{1,0:T(8,128)(2,1)S(1)} collective-permute-done((bf16[8,3328]{1,0:T(8,128)(2,1)S(1)}, bf16[8,3328]{1,0:T(8,128)(2,1)S(1)}, u32[]{:S(2)}, u32[]{:S(2)}) %collective-permute-start.6) | collective-permute-done | bytes 53280 | tf_op jit(solution)/shard_map/ppermute | solution.py:612
  122.1 13.9 %collective-permute-done.8 = bf16[256,2048]{1,0:T(8,128)(2,1)S(1)} collective-permute-done((bf16[256,2048]{1,0:T(8,128)(2,1)S(1)}, bf16[256,2048]{1,0:T(8,128)(2,1)S(1)}, u32[]{:S(2)}, u32[]{:S(2)}) %collective-permute-start.8) | collective-permute-done | bytes 1048608 | tf_op jit(solution)/shard_map/ppermute | solution.py:393
  149.3 19.6 %project.1 = (bf16[1024,2048]{1,0:T(8,128)(2,1)}, f32[1024,1024]{1,0:T(8,128)}) custom-call(bf16[1024,2048]{1,0:T(8,128)(2,1)} %add_convert_fusion.x_ref, bf16[2048,3072]{1,0:T(8,128)(2,1)} %all-gather.5.cloned.1.call-done.w_ref.refs_4_.refs_5_.refs_6_.refs_7_), custom_call_target="tpu_custom_call" | custom-call | flops 1024 | bytes 1024 | tf_op jit(solution)/shard_map/project/pallas_call | solution.py:95
  168.9 9.0 %retain_mix.1 = (bf16[1024,1024]{1,0:T(8,128)(2,1)}, bf16[1024,1024]{1,0:T(8,128)(2,1)}) custom-call(f32[2]{0:T(128)} %subtract_log_fusion.rate_ref, s32[8]{0:T(128)} %fusion.22.place_ref, bf16[1024,2048]{1,0:T(8,128)(2,1)} %get-tuple-element.65.q_ref.k_ref.v_ref, bf16[1024,2048]{1,0:T(8,128)(2,1)} %get-tuple-element.65.q_ref.k_ref.v_ref, ...), custom_call_target="tpu_custom_call" | custom-call | flops 1024 | bytes 1024 | tf_op jit(solution)/shard_map/retain_mix/pallas_call | solution.py:155
  177.9 13.7 %all-gather.7.cloned.1.call-done.refs_1_.w_ref = bf16[1024,2048]{1,0:T(8,128)(2,1)} async-done(((bf16[128,2048]{1,0:T(8,128)(2,1)}), bf16[1024,2048]{1,0:T(8,128)(2,1)}) %all-gather.7.cloned.1.call-update) | async-done | bytes 4194320 | tf_op jit(solution)/shard_map/all_gather | solution.py:705
  191.7 8.2 %full_product.4 = bf16[1024,2048]{1,0:T(8,128)(2,1)} custom-call(bf16[1024,1024]{1,0:T(8,128)(2,1)} %get-tuple-element.69.refs_0_.x_ref, bf16[1024,2048]{1,0:T(8,128)(2,1)} %all-gather.7.cloned.1.call-done.refs_1_.w_ref), custom_call_target="tpu_custom_call" | custom-call | flops 1024 | bytes 1024 | tf_op jit(solution)/shard_map/full_product/pallas_call | solution.py:358
  204.7 10.7 %collective-permute-done.13 = bf16[128,2048]{1,0:T(8,128)(2,1)S(1)} collective-permute-done((bf16[128,2048]{1,0:T(8,128)(2,1)S(1)}, bf16[128,2048]{1,0:T(8,128)(2,1)S(1)}, u32[]{:S(2)}, u32[]{:S(2)}) %collective-permute-start.13) | collective-permute-done | bytes 524320 | tf_op jit(solution)/shard_map/ppermute | solution.py:390
  225.5 19.0 %collective-permute-done.14 = bf16[256,2048]{1,0:T(8,128)(2,1)S(1)} collective-permute-done((bf16[256,2048]{1,0:T(8,128)(2,1)}, bf16[256,2048]{1,0:T(8,128)(2,1)S(1)}, u32[]{:S(2)}, u32[]{:S(2)}) %collective-permute-start.14) | collective-permute-done | bytes 1048608 | tf_op jit(solution)/shard_map/ppermute | solution.py:390
  252.3 20.4 %collective-permute-done.17 = bf16[256,2048]{1,0:T(8,128)(2,1)S(1)} collective-permute-done((bf16[256,2048]{1,0:T(8,128)(2,1)S(1)}, bf16[256,2048]{1,0:T(8,128)(2,1)S(1)}, u32[]{:S(2)}, u32[]{:S(2)}) %collective-permute-start.17) | collective-permute-done | bytes 1048608 | tf_op jit(solution)/shard_map/ppermute | solution.py:390
  288.4 12.6 %fusion.29.gate_ref.up_ref = f32[1024,2048]{1,0:T(8,128)S(1)} fusion(bf16[1024,2048]{1,0:T(8,128)(2,1)} %bitcast.31.x_ref, bf16[2048,2048]{1,0:T(8,128)(2,1)} %all-gather.9.cloned.1.call-done.refs_2_.refs_3_), kind=kOutput, calls=%fused_computation.157 | convolution fusion | flops 8589934592 | bytes 20971520 | tf_op jit(solution)/shard_map/dot_general | solution.py:22
  316.2 6.9 rows_sum.11.rest_0_
  323.2 13.3 %gate_back.1 = (bf16[1024,1024]{1,0:T(8,128)(2,1)}, bf16[1024,1024]{1,0:T(8,128)(2,1)}, f32[1,1024]{1,0:T(1,128)}, f32[1,1024]{1,0:T(1,128)}) custom-call(bf16[1024,2048]{1,0:T(8,128)(2,1)} %bitcast.21.refs_0_.g_ref, bf16[1024,2048]{1,0:T(8,128)(2,1)} %all-gather.11.cloned.1.call-done.w_ref.refs_1_, f32[1024,2048]{1,0:T(8,128)} %copy-done.2, ...), custom_call_target="tpu_custom_call" | custom-call | flops 1024 | bytes 1024 | tf_op jit(solution)/shard_map/gate_back/pallas_call | solution.py:259
  336.5 14.0 %full_product.5 = bf16[1024,2048]{1,0:T(8,128)(2,1)} custom-call(bf16[1024,1024]{1,0:T(8,128)(2,1)} %get-tuple-element.72.refs_0_, bf16[1024,1024]{1,0:T(8,128)(2,1)} %get-tuple-element.73.refs_1_, bf16[2048,2048]{1,0:T(8,128)(2,1)} %all-gather.9.cloned.1.call-done.refs_2_.refs_3_, bf16[2048,2048]{1,0:T(8,128)(2,1)} %all-gather.9.cloned.1.call-done.refs_2_.refs_3_), custom_call_target="tpu_custom_call" | custom-call | flops 1024 | bytes 1024 | tf_op jit(solution)/shard_map/full_product/pallas_call | solution.py:358
  352.7 8.8 %rows_sum.12 = bf16[1024,2048]{1,0:T(8,128)(2,1)} custom-call(s32[1]{0:T(128)} %bitcast.35.core_ref, bf16[1024,2048]{1,0:T(8,128)(2,1)} %bitcast.31.x_ref, bf16[1024,1024]{1,0:T(8,128)(2,1)} %get-tuple-element.72.refs_0_, bf16[1024,1024]{1,0:T(8,128)(2,1)} %get-tuple-element.73.refs_1_, bf16[128,2048]{1,0:T(8,128)(2,1)} %get-tuple-element.136.refs_2_, ...), custom_call_target="tpu_custom_call" | custom-call | flops 1024 | bytes 1024 | tf_op jit(solution)/shard_map/rows_sum/pallas_call | solution.py:579
  363.9 12.3 %collective-permute-done.23 = bf16[128,2048]{1,0:T(8,128)(2,1)} collective-permute-done((bf16[128,2048]{1,0:T(8,128)(2,1)}, bf16[128,2048]{1,0:T(8,128)(2,1)}, u32[]{:S(2)}, u32[]{:S(2)}) %collective-permute-start.23) | collective-permute-done | bytes 524320 | tf_op jit(solution)/shard_map/ppermute | solution.py:390
  380.4 9.5 %rows_sum.13.refs_2_ = bf16[1024,2048]{1,0:T(8,128)(2,1)} custom-call(s32[1]{0:T(128)} %bitcast.32.core_ref, bf16[1024,2048]{1,0:T(8,128)(2,1)} %bitcast.31.x_ref, bf16[1024,1024]{1,0:T(8,128)(2,1)} %get-tuple-element.72.refs_0_, bf16[1024,1024]{1,0:T(8,128)(2,1)} %get-tuple-element.73.refs_1_, bf16[1024,2048]{1,0:T(8,128)(2,1)} %collective-permute-done.22.refs_2_, ...), custom_call_target="tpu_custom_call" | custom-call | flops 1024 | bytes 1024 | tf_op jit(solution)/shard_map/rows_sum/pallas_call | solution.py:579
  392.1 8.2 %full_product.6 = bf16[1024,2048]{1,0:T(8,128)(2,1)} custom-call(bf16[1024,1024]{1,0:T(8,128)(2,1)} %fusion.3.x_ref.refs_0_, bf16[1024,2048]{1,0:T(8,128)(2,1)} %all-gather.11.cloned.1.call-done.w_ref.refs_1_, bf16[1024,2048]{1,0:T(8,128)(2,1)} %rows_sum.13.refs_2_), custom_call_target="tpu_custom_call" | custom-call | flops 1024 | bytes 1024 | tf_op jit(solution)/shard_map/full_product/pallas_call | solution.py:358
  400.3 14.5 %collective-permute-done.25 = bf16[256,2048]{1,0:T(8,128)(2,1)} collective-permute-done((bf16[256,2048]{1,0:T(8,128)(2,1)}, bf16[256,2048]{1,0:T(8,128)(2,1)}, u32[]{:S(2)}, u32[]{:S(2)}) %collective-permute-start.25) | collective-permute-done | bytes 1048608 | tf_op jit(solution)/shard_map/ppermute | solution.py:390
  422.6 21.2 %collective-permute-done.27 = bf16[256,2048]{1,0:T(8,128)(2,1)S(1)} collective-permute-done((bf16[256,2048]{1,0:T(8,128)(2,1)S(1)}, bf16[256,2048]{1,0:T(8,128)(2,1)S(1)}, u32[]{:S(2)}, u32[]{:S(2)}) %collective-permute-start.27) | collective-permute-done | bytes 1048608 | tf_op jit(solution)/shard_map/ppermute | solution.py:390
  468.6 6.9 rows_sum.15.rest_0_
  479.9 17.5 %mixed_back.1 = (bf16[1024,1024]{1,0:T(8,128)(2,1)}, bf16[1024,1024]{1,0:T(8,128)(2,1)}, f32[1,1024]{1,0:T(1,128)}, f32[1,1024]{1,0:T(1,128)}) custom-call(s32[8]{0:T(128)} %fusion.22.place_ref, bf16[1024,2048]{1,0:T(8,128)(2,1)} %bitcast.41.refs_0_.d_ref, bf16[1024,2048]{1,0:T(8,128)(2,1)} %all-gather.7.cloned.1.call-done.refs_1_.w_ref, ...), custom_call_target="tpu_custom_call" | custom-call | flops 1024 | bytes 1024 | tf_op jit(solution)/shard_map/mixed_back/pallas_call | solution.py:317
  497.4 12.7 %retain_back.1 = (bf16[1024,512]{1,0:T(8,128)(2,1)}, bf16[1024,512]{1,0:T(8,128)(2,1)}, bf16[1024,1024]{1,0:T(8,128)(2,1)}) custom-call(f32[2]{0:T(128)} %subtract_log_fusion.rate_ref, bf16[1024,2048]{1,0:T(8,128)(2,1)} %get-tuple-element.65.q_ref.k_ref.v_ref, bf16[1024,2048]{1,0:T(8,128)(2,1)} %get-tuple-element.65.q_ref.k_ref.v_ref, ...), custom_call_target="tpu_custom_call" | custom-call | flops 1024 | bytes 1024 | tf_op jit(solution)/shard_map/retain_back/pallas_call | solution.py:209
  513.2 8.8 %rows_sum.16 = bf16[1024,2048]{1,0:T(8,128)(2,1)} custom-call(s32[1]{0:T(128)} %bitcast.35.core_ref, bf16[1024,2048]{1,0:T(8,128)(2,1)} %add_convert_fusion.x_ref, bf16[1024,1024]{1,0:T(8,128)(2,1)} %get-tuple-element.84.refs_0_.refs_2_, bf16[1024,1024]{1,0:T(8,128)(2,1)} %get-tuple-element.85.refs_1_.refs_3_, ...), custom_call_target="tpu_custom_call" | custom-call | flops 1024 | bytes 1024 | tf_op jit(solution)/shard_map/rows_sum/pallas_call | solution.py:579
  531.6 6.9 collective-permute-done.37.refs_6_.refs_3_
  540.7 9.5 %rows_sum.17.refs_8_ = bf16[1024,2048]{1,0:T(8,128)(2,1)} custom-call(s32[1]{0:T(128)} %bitcast.32.core_ref, bf16[1024,2048]{1,0:T(8,128)(2,1)} %add_convert_fusion.x_ref, bf16[1024,1024]{1,0:T(8,128)(2,1)} %get-tuple-element.84.refs_0_.refs_2_, bf16[1024,1024]{1,0:T(8,128)(2,1)} %get-tuple-element.85.refs_1_.refs_3_, ...), custom_call_target="tpu_custom_call" | custom-call | flops 1024 | bytes 1024 | tf_op jit(solution)/shard_map/rows_sum/pallas_call | solution.py:579
  554.7 20.6 %full_product.7 = bf16[1024,2048]{1,0:T(8,128)(2,1)} custom-call(bf16[1024,512]{1,0:T(8,128)(2,1)} %get-tuple-element.82.refs_0_, bf16[1024,512]{1,0:T(8,128)(2,1)} %get-tuple-element.83.refs_1_, bf16[1024,1024]{1,0:T(8,128)(2,1)} %get-tuple-element.84.refs_0_.refs_2_, bf16[1024,1024]{1,0:T(8,128)(2,1)} %get-tuple-element.85.refs_1_.refs_3_, ...), custom_call_target="tpu_custom_call" | custom-call | flops 1024 | bytes 1024 | tf_op jit(solution)/shard_map/full_product/pallas_call | solution.py:358
  578.0 8.4 %collective-permute-done.41.refs_1_ = bf16[128,2048]{1,0:T(8,128)(2,1)} collective-permute-done((bf16[128,2048]{1,0:T(8,128)(2,1)}, bf16[128,2048]{1,0:T(8,128)(2,1)}, u32[]{:S(2)}, u32[]{:S(2)}) %collective-permute-start.41) | collective-permute-done | bytes 524320 | tf_op jit(solution)/shard_map/ppermute | solution.py:390
  601.7 14.1 %collective-permute-done.46.refs_3_ = bf16[64,2048]{1,0:T(8,128)(2,1)S(1)} collective-permute-done((bf16[64,2048]{1,0:T(8,128)(2,1)S(1)}, bf16[64,2048]{1,0:T(8,128)(2,1)S(1)}, u32[]{:S(2)}, u32[]{:S(2)}) %collective-permute-start.46) | collective-permute-done | bytes 262176 | tf_op jit(solution)/shard_map/ppermute | solution.py:390
  642.1 6.8 gather_columns.3
  665.6 15.9 %collective-permute-done.50.refs_1_ = bf16[256,2048]{1,0:T(8,128)(2,1)} collective-permute-done((bf16[256,2048]{1,0:T(8,128)(2,1)}, bf16[256,2048]{1,0:T(8,128)(2,1)}, u32[]{:S(2)}, u32[]{:S(2)}) %collective-permute-start.50) | collective-permute-done | bytes 1048608 | tf_op jit(solution)/shard_map/ppermute | solution.py:390
  710.6 7.5 collective-permute-done.55
  722.6 9.3 %collective-permute-done.61.refs_3_ = bf16[128,2048]{1,0:T(8,128)(2,1)} collective-permute-done((bf16[128,2048]{1,0:T(8,128)(2,1)S(1)}, bf16[128,2048]{1,0:T(8,128)(2,1)}, u32[]{:S(2)}, u32[]{:S(2)}) %collective-permute-start.61) | collective-permute-done | bytes 524320 | tf_op jit(solution)/shard_map/ppermute | solution.py:390
  (409 shorter events, 323.9 us)
Async XLA Ops:
  7.2 142.1 %all-gather.5.cloned.1.call-start = ((), (), s32[]{:S(2)}) async-start(), calls=%async_computation.5 | async-start | bytes 14155776 | tf_op jit(solution)/shard_map/all_gather | solution.py:705
  11.2 180.5 %all-gather.7.cloned.1.call-start = ((), (), s32[]{:S(2)}) async-start(), calls=%async_computation.6 | async-start | bytes 4718592 | tf_op jit(solution)/shard_map/all_gather | solution.py:705
  13.8 58.6 %collective-permute-start = (bf16[256,2048]{1,0:T(8,128)(2,1)S(1)}, bf16[256,2048]{1,0:T(8,128)(2,1)}, u32[]{:S(2)}, u32[]{:S(2)}) collective-permute-start(bf16[256,2048]{1,0:T(8,128)(2,1)S(1)} %bitcast.132), channel_id=1, source_target_pairs={{0,1},{1,3},{3,2},{2,0},{4,5},{5,7},{7,6},{6,4},{8,9},{9,11},{11,1... | collective-permute-start | bytes 3145736 | tf_op jit(solution)/shard_map/ppermute | solution.py:390
  16.4 57.2 %collective-permute-start.1 = (bf16[256,2048]{1,0:T(8,128)(2,1)S(1)}, bf16[256,2048]{1,0:T(8,128)(2,1)}, u32[]{:S(2)}, u32[]{:S(2)}) collective-permute-start(bf16[256,2048]{1,0:T(8,128)(2,1)S(1)} %bitcast.133), channel_id=1, source_target_pairs={{0,2},{1,0},{3,1},{2,3},{4,6},{5,4},{7,5},{6,7},{8,10},{9,8},{11,9... | collective-permute-start | bytes 3145736 | tf_op jit(solution)/shard_map/ppermute | solution.py:393
  19.6 51.1 %collective-permute-start.11 = (bf16[128,2048]{1,0:T(8,128)(2,1)}, bf16[128,2048]{1,0:T(8,128)(2,1)}, u32[]{:S(2)}, u32[]{:S(2)}) collective-permute-start(bf16[128,2048]{1,0:T(8,128)(2,1)} %constant_dynamic-slice_fusion.10), channel_id=1, source_target_pairs={{0,0},{4,4},{8,16},{12,20},{16,8},{20,12},{24,24},{28,28},{1,9},{5... | collective-permute-start | bytes 1572872 | tf_op jit(solution)/shard_map/ppermute | solution.py:639
  30.9 39.2 %collective-permute-start.6 = (bf16[8,3328]{1,0:T(8,128)(2,1)S(1)}, bf16[8,3328]{1,0:T(8,128)(2,1)S(1)}, u32[]{:S(2)}, u32[]{:S(2)}) collective-permute-start(bf16[8,3328]{1,0:T(8,128)(2,1)S(1)} %add.294), channel_id=1, source_target_pairs={{0,16},{4,20},{8,24},{12,28},{16,0},{20,4},{24,8},{28,12},{1,17},{... | collective-permute-start | bytes 159752 | tf_op jit(solution)/shard_map/ppermute | solution.py:612
  70.7 26.3 %collective-permute-start.12 = (bf16[128,2048]{1,0:T(8,128)(2,1)}, bf16[128,2048]{1,0:T(8,128)(2,1)S(1)}, u32[]{:S(2)}, u32[]{:S(2)}) collective-permute-start(bf16[128,2048]{1,0:T(8,128)(2,1)} %collective-permute-done.11), channel_id=1, source_target_pairs={{0,0},{4,4},{16,17},{20,21},{8,10},{12,14},{24,27},{28,31},{9,8},{... | collective-permute-start | bytes 1572872 | tf_op jit(solution)/shard_map/ppermute | solution.py:640
  97.8 190.6 %all-gather.9.cloned.1.call-start = ((), (), s32[]{:S(2)}) async-start(), calls=%async_computation.7 | async-start | bytes 9437184 | tf_op jit(solution)/shard_map/all_gather | solution.py:705
  112.8 210.4 %all-gather.11.cloned.1.call-start = ((), (), s32[]{:S(2)}) async-start(), calls=%async_computation.8 | async-start | bytes 4718592 | tf_op jit(solution)/shard_map/all_gather | solution.py:705
  224.1 152.5 %reduce-scatter.6.cloned.1.call-start = ((), (), s32[]{:S(2)}) async-start(), calls=%async_computation.9 | async-start | bytes 2621440 | tf_op jit(solution)/shard_map/reduce_scatter | solution.py:602
  323.1 152.4 %reduce-scatter.8.cloned.1.call-start = ((), (), s32[]{:S(2)}) async-start(), calls=%async_computation.10 | async-start | bytes 5242880 | tf_op jit(solution)/shard_map/reduce_scatter | solution.py:602
  389.9 141.7 %reduce-scatter.10.cloned.1.call-start = ((), (), s32[]{:S(2)}) async-start(), calls=%async_computation.11 | async-start | bytes 2621440 | tf_op jit(solution)/shard_map/reduce_scatter | solution.py:602
  475.5 37.7 %collective-permute-start.32 = (bf16[256,2048]{1,0:T(8,128)(2,1)}, bf16[256,2048]{1,0:T(8,128)(2,1)}, u32[]{:S(2)}, u32[]{:S(2)}) collective-permute-start(bf16[256,2048]{1,0:T(8,128)(2,1)} %reduce-scatter.8.cloned.1.call-done.rest_1_.refs_2_.refs_0_), channel_id=1, source_target_pairs={{0,1},{1,3},{3,2},{2,0},{4,5},{5,7},{7,6},{6,4},{8,9},{9,11},{11,1... | collective-permute-start | bytes 3145736 | tf_op jit(solution)/shard_map/ppermute | solution.py:390
  476.7 36.5 %collective-permute-start.33 = (bf16[256,2048]{1,0:T(8,128)(2,1)}, bf16[256,2048]{1,0:T(8,128)(2,1)}, u32[]{:S(2)}, u32[]{:S(2)}) collective-permute-start(bf16[256,2048]{1,0:T(8,128)(2,1)} %reduce-scatter.8.cloned.1.call-done.rest_1_.refs_2_.refs_0_), channel_id=1, source_target_pairs={{0,2},{1,0},{3,1},{2,3},{4,6},{5,4},{7,5},{6,7},{8,10},{9,8},{11,9... | collective-permute-start | bytes 3145736 | tf_op jit(solution)/shard_map/ppermute | solution.py:393
  477.5 35.7 %collective-permute-start.35 = (bf16[128,2048]{1,0:T(8,128)(2,1)}, bf16[128,2048]{1,0:T(8,128)(2,1)}, u32[]{:S(2)}, u32[]{:S(2)}) collective-permute-start(bf16[128,2048]{1,0:T(8,128)(2,1)} %get-tuple-element.80.refs_3_), channel_id=1, source_target_pairs={{0,2},{1,0},{3,1},{2,3},{4,6},{5,4},{7,5},{6,7},{8,10},{9,8},{11,9... | collective-permute-start | bytes 1572872 | tf_op jit(solution)/shard_map/ppermute | solution.py:393
  478.6 34.6 %collective-permute-start.34 = (bf16[128,2048]{1,0:T(8,128)(2,1)}, bf16[128,2048]{1,0:T(8,128)(2,1)}, u32[]{:S(2)}, u32[]{:S(2)}) collective-permute-start(bf16[128,2048]{1,0:T(8,128)(2,1)} %get-tuple-element.79.refs_2_), channel_id=1, source_target_pairs={{0,1},{1,3},{3,2},{2,0},{4,5},{5,7},{7,6},{6,4},{8,9},{9,11},{11,1... | collective-permute-start | bytes 1572872 | tf_op jit(solution)/shard_map/ppermute | solution.py:390
  479.6 178.5 %reduce-scatter.12.cloned.1.call-start = ((), (), s32[]{:S(2)}) async-start(), calls=%async_computation.12 | async-start | bytes 5242880 | tf_op jit(solution)/shard_map/reduce_scatter | solution.py:602
  550.3 138.0 %reduce-scatter.14.cloned.1.call-start = ((), (), s32[]{:S(2)}) async-start(), calls=%async_computation.13 | async-start | bytes 2621440 | tf_op jit(solution)/shard_map/reduce_scatter | solution.py:602
  550.3 26.5 %collective-permute-start.39 = (bf16[256,2048]{1,0:T(8,128)(2,1)}, bf16[256,2048]{1,0:T(8,128)(2,1)}, u32[]{:S(2)}, u32[]{:S(2)}) collective-permute-start(bf16[256,2048]{1,0:T(8,128)(2,1)} %get-tuple-element.129.refs_3_), channel_id=1, source_target_pairs={{0,1},{1,3},{3,2},{2,0},{4,5},{5,7},{7,6},{6,4},{8,9},{9,11},{11,1... | collective-permute-start | bytes 3145736 | tf_op jit(solution)/shard_map/ppermute | solution.py:390
  551.6 26.4 %collective-permute-start.40 = (bf16[256,2048]{1,0:T(8,128)(2,1)}, bf16[256,2048]{1,0:T(8,128)(2,1)}, u32[]{:S(2)}, u32[]{:S(2)}) collective-permute-start(bf16[256,2048]{1,0:T(8,128)(2,1)} %get-tuple-element.130.refs_4_), channel_id=1, source_target_pairs={{0,2},{1,0},{3,1},{2,3},{4,6},{5,4},{7,5},{6,7},{8,10},{9,8},{11,9... | collective-permute-start | bytes 3145736 | tf_op jit(solution)/shard_map/ppermute | solution.py:393
  552.4 33.9 %collective-permute-start.41 = (bf16[128,2048]{1,0:T(8,128)(2,1)}, bf16[128,2048]{1,0:T(8,128)(2,1)}, u32[]{:S(2)}, u32[]{:S(2)}) collective-permute-start(bf16[128,2048]{1,0:T(8,128)(2,1)} %reduce-scatter.6.cloned.1.call-done.refs_0_), channel_id=1, source_target_pairs={{0,1},{1,3},{3,2},{2,0},{4,5},{5,7},{7,6},{6,4},{8,9},{9,11},{11,1... | collective-permute-start | bytes 1572872 | tf_op jit(solution)/shard_map/ppermute | solution.py:390
  553.6 33.7 %collective-permute-start.42 = (bf16[128,2048]{1,0:T(8,128)(2,1)}, bf16[128,2048]{1,0:T(8,128)(2,1)}, u32[]{:S(2)}, u32[]{:S(2)}) collective-permute-start(bf16[128,2048]{1,0:T(8,128)(2,1)} %reduce-scatter.6.cloned.1.call-done.refs_0_), channel_id=1, source_target_pairs={{0,2},{1,0},{3,1},{2,3},{4,6},{5,4},{7,5},{6,7},{8,10},{9,8},{11,9... | collective-permute-start | bytes 1572872 | tf_op jit(solution)/shard_map/ppermute | solution.py:393
  595.6 25.1 %collective-permute-start.43 = (bf16[1024,1024]{1,0:T(8,128)(2,1)}, bf16[1024,1024]{1,0:T(8,128)(2,1)}, u32[]{:S(2)}, u32[]{:S(2)}) collective-permute-start(bf16[1024,1024]{1,0:T(8,128)(2,1)} %rows_sum.18), channel_id=1, source_target_pairs={{0,4},{4,0},{8,12},{12,8},{16,20},{20,16},{24,28},{28,24},{1,5},{5... | collective-permute-start | bytes 6291464 | tf_op jit(solution)/shard_map/ppermute | solution.py:551
  627.2 26.8 %collective-permute-start.48 = (bf16[256,2048]{1,0:T(8,128)(2,1)}, bf16[256,2048]{1,0:T(8,128)(2,1)}, u32[]{:S(2)}, u32[]{:S(2)}) collective-permute-start(bf16[256,2048]{1,0:T(8,128)(2,1)} %get-tuple-element.126.refs_3_), channel_id=1, source_target_pairs={{0,1},{1,3},{3,2},{2,0},{4,5},{5,7},{7,6},{6,4},{8,9},{9,11},{11,1... | collective-permute-start | bytes 3145736 | tf_op jit(solution)/shard_map/ppermute | solution.py:390
  628.5 26.4 %collective-permute-start.49 = (bf16[256,2048]{1,0:T(8,128)(2,1)}, bf16[256,2048]{1,0:T(8,128)(2,1)}, u32[]{:S(2)}, u32[]{:S(2)}) collective-permute-start(bf16[256,2048]{1,0:T(8,128)(2,1)} %get-tuple-element.125.refs_4_), channel_id=1, source_target_pairs={{0,2},{1,0},{3,1},{2,3},{4,6},{5,4},{7,5},{6,7},{8,10},{9,8},{11,9... | collective-permute-start | bytes 3145736 | tf_op jit(solution)/shard_map/ppermute | solution.py:393
  658.3 28.5 %collective-permute-start.51 = (bf16[256,2048]{1,0:T(8,128)(2,1)}, bf16[256,2048]{1,0:T(8,128)(2,1)}, u32[]{:S(2)}, u32[]{:S(2)}) collective-permute-start(bf16[256,2048]{1,0:T(8,128)(2,1)} %reduce-scatter.12.cloned.1.call-done.refs_0_), channel_id=1, source_target_pairs={{0,2},{1,0},{3,1},{2,3},{4,6},{5,4},{7,5},{6,7},{8,10},{9,8},{11,9... | collective-permute-start | bytes 3145736 | tf_op jit(solution)/shard_map/ppermute | solution.py:393
  660.3 30.1 %collective-permute-start.64 = (bf16[128,2048]{1,0:T(8,128)(2,1)}, bf16[128,2048]{1,0:T(8,128)(2,1)}, u32[]{:S(2)}, u32[]{:S(2)}) collective-permute-start(bf16[128,2048]{1,0:T(8,128)(2,1)} %collective-permute-done.63), channel_id=1, source_target_pairs={{0,0},{4,4},{16,8},{20,12},{8,16},{12,20},{24,24},{28,28},{9,1},{1... | collective-permute-start | bytes 1572872 | tf_op jit(solution)/shard_map/ppermute | solution.py:644
  690.4 27.7 %collective-permute-start.65 = (bf16[128,2048]{1,0:T(8,128)(2,1)}, bf16[128,2048]{1,0:T(8,128)(2,1)S(1)}, u32[]{:S(2)}, u32[]{:S(2)}) collective-permute-start(bf16[128,2048]{1,0:T(8,128)(2,1)} %collective-permute-done.64.refs_0_), channel_id=1, source_target_pairs={{0,1},{1,3},{3,2},{2,0},{4,5},{5,7},{7,6},{6,4},{8,9},{9,11},{11,1... | collective-permute-start | bytes 1572872 | tf_op jit(solution)/shard_map/ppermute | solution.py:390
  691.6 28.6 %collective-permute-start.66 = (bf16[128,2048]{1,0:T(8,128)(2,1)}, bf16[128,2048]{1,0:T(8,128)(2,1)S(1)}, u32[]{:S(2)}, u32[]{:S(2)}) collective-permute-start(bf16[128,2048]{1,0:T(8,128)(2,1)} %collective-permute-done.64.refs_0_), channel_id=1, source_target_pairs={{0,2},{1,0},{3,1},{2,3},{4,6},{5,4},{7,5},{6,7},{8,10},{9,8},{11,9... | collective-permute-start | bytes 1572872 | tf_op jit(solution)/shard_map/ppermute | solution.py:393
  704.9 36.4 %collective-permute-start.59 = (bf16[128,1024]{1,0:T(8,128)(2,1)}, bf16[128,1024]{1,0:T(8,128)(2,1)S(1)}, u32[]{:S(2)}, u32[]{:S(2)}) collective-permute-start(bf16[128,1024]{1,0:T(8,128)(2,1)} %slice.245), channel_id=1, source_target_pairs={{0,1},{1,3},{3,2},{2,0},{4,5},{5,7},{7,6},{6,4},{8,9},{9,11},{11,1... | collective-permute-start | bytes 786440 | tf_op jit(solution)/shard_map/ppermute | solution.py:390
  707.6 33.7 %collective-permute-start.60 = (bf16[128,1024]{1,0:T(8,128)(2,1)}, bf16[128,1024]{1,0:T(8,128)(2,1)}, u32[]{:S(2)}, u32[]{:S(2)}) collective-permute-start(bf16[128,1024]{1,0:T(8,128)(2,1)} %slice.246), channel_id=1, source_target_pairs={{0,2},{1,0},{3,1},{2,3},{4,6},{5,4},{7,5},{6,7},{8,10},{9,8},{11,9... | collective-permute-start | bytes 786440 | tf_op jit(solution)/shard_map/ppermute | solution.py:393
  720.2 26.8 %collective-permute-start.56 = (f32[8,3328]{1,0:T(8,128)S(1)}, f32[8,3328]{1,0:T(8,128)}, u32[]{:S(2)}, u32[]{:S(2)}) collective-permute-start(f32[8,3328]{1,0:T(8,128)S(1)} %add.682), channel_id=1, source_target_pairs={{0,2},{1,3},{2,0},{3,1},{4,6},{5,7},{6,4},{7,5},{8,10},{9,11},{10,... | collective-permute-start | bytes 319496 | tf_op jit(solution)/shard_map/ppermute | solution.py:612
  (85 other events, 1014.8 us)
Sparse Core Ops, SparseCore 0:
  11.3 129.9 all-gather.4
  143.4 48.1 all-gather.6
  193.8 80.7 all-gather.8
  276.1 45.6 all-gather.10
  324.0 43.4 reduce-scatter.5
  390.1 77.9 reduce-scatter.7
  479.7 44.6 reduce-scatter.9
  550.4 77.7 reduce-scatter.11
  631.0 44.4 reduce-scatter.13
